TPU v7x, 32 devices: a whole 2x2x4 slice. The times are simulated.
32 devices in a mesh: seq: 4 (over z), fsdp: 8 (over y, x, core).
Axes of the slice: x: 2, y: 2, z: 4, core: 2. Of those that a mesh axis runs over, the one named last changes fastest.
Arguments:
- hidden_in: bfloat16 [16, 1024, 1024], P('fsdp', 'seq'), may hold values from -6 to 6
- document_labels: int32 [16, 1024], P('fsdp', 'seq'), may hold values from 0 to 2, never falling along the last dimension, each value on 1 to 512 neighbouring positions
- cotangent: bfloat16 [16, 1024, 1024], P('fsdp', 'seq'), may hold values from -6 to 6
- ln_gain: bfloat16 [1024], P(('seq', 'fsdp')), may hold values from 0.5 to 1.5
- ln_bias: bfloat16 [1024], P(('seq', 'fsdp')), may hold values from -1 to 1
- qkv_weight: bfloat16 [1024, 3072], P(('seq', 'fsdp')), may hold values from -0.1875 to 0.1875
- qkv_bias: bfloat16 [3072], P(('seq', 'fsdp')), may hold values from -1 to 1
- out_weight: bfloat16 [1024, 1024], P(('seq', 'fsdp')), may hold values from -1.5 to 1.5
- out_bias: bfloat16 [1024], P(('seq', 'fsdp')), may hold values from -1 to 1
- fc_in_weight: bfloat16 [1024, 4096], P(('seq', 'fsdp')), may hold values from -0.1875 to 0.1875
- fc_in_bias: bfloat16 [4096], P(('seq', 'fsdp')), may hold values from -1 to 1
- fc_out_weight: bfloat16 [4096, 1024], P(('seq', 'fsdp')), may hold values from -0.09375 to 0.09375
- fc_out_bias: bfloat16 [1024], P(('seq', 'fsdp')), may hold values from -1 to 1
Outputs:
- output: bfloat16 [16, 1024, 1024], P('fsdp', 'seq')
- input_grad: bfloat16 [16, 1024, 1024], P('fsdp', 'seq')
- ln_gain_grad: float32 [1024], P(('seq', 'fsdp'))
- ln_bias_grad: float32 [1024], P(('seq', 'fsdp'))
- qkv_weight_grad: float32 [1024, 3072], P(('seq', 'fsdp'))
- qkv_bias_grad: float32 [3072], P(('seq', 'fsdp'))
- out_weight_grad: float32 [1024, 1024], P(('seq', 'fsdp'))
- out_bias_grad: float32 [1024], P(('seq', 'fsdp'))
- fc_in_weight_grad: float32 [1024, 4096], P(('seq', 'fsdp'))
- fc_in_bias_grad: float32 [4096], P(('seq', 'fsdp'))
- fc_out_weight_grad: float32 [4096, 1024], P(('seq', 'fsdp'))
- fc_out_bias_grad: float32 [1024], P(('seq', 'fsdp'))
Inputs may be any that keep to these rules, and one draw needn't show every extreme that they name: `document_labels`: along each sequence the numbers never fall; every document (a run of equal numbers) has 1 to 512 tokens, and one has exactly 512.
All inputs are finite; a program needn't handle non-finite values.
Results may differ from a plain program's by a relative error of at most 0.009.
Values may be sent and summed in bfloat16 or wider, within the bound.
No kernel may reach another device: no remote copies, remote signals or barrier semaphores. Data moves between devices by JAX's collectives and lax.ppermute only.
A program may use at most 256 MiB of HBM per device.

v0:
```python
from functools import partial
import math

import jax
import jax.numpy as jnp
import numpy as np
from jax import lax
from jax.experimental import pallas as pl
from jax.experimental.pallas import tpu as pltpu
from jax.sharding import PartitionSpec as P

D = 1024
H = 16
HD = 64
ROT = 16
GROUPS = 4
BF = jnp.bfloat16
F32 = jnp.float32


def rotate(values, cosine, sine_part):
    half_rot = ROT // 2
    first_part = values[..., :half_rot]
    second_part = values[..., half_rot:ROT]
    return jnp.concatenate(
        [
            first_part * cosine - second_part * sine_part,
            second_part * cosine + first_part * sine_part,
            values[..., ROT:],
        ],
        axis=-1,
    )


def position_angles(segments):
    length = segments.shape[0]
    places = jnp.arange(length, dtype=jnp.int32)
    boundary = jnp.concatenate([jnp.ones((1,), dtype=jnp.bool_), segments[1:] != segments[:-1]])
    starts = lax.cummax(jnp.where(boundary, places, 0), axis=0)
    positions = (places - starts).astype(jnp.float32)
    inverse = 1.0 / 10000.0 ** (jnp.arange(0, ROT, 2, dtype=jnp.float32) / ROT)
    return positions[:, None] * inverse[None, :]


def make_mask(segments, first_row, block_rows):
    length = segments.shape[0]
    query_index = first_row + jnp.arange(block_rows, dtype=jnp.int32)
    key_index = jnp.arange(length, dtype=jnp.int32)
    query_segments = lax.dynamic_slice_in_dim(segments, first_row, block_rows, 0)
    return (key_index[None, :] <= query_index[:, None]) & (
        query_segments[:, None] == segments[None, :]
    )


def outer_product(left, right):
    return lax.dot_general(
        left, right, (((0,), (0,)), ((), ())), preferred_element_type=jnp.float32
    )


def times_transposed(left, right):
    return lax.dot_general(
        left, right, (((1,), (1,)), ((), ())), preferred_element_type=jnp.float32
    )


def local_plain(
    hidden_in,
    document_labels,
    cotangent,
    ln_gain,
    ln_bias,
    qkv_weight,
    qkv_bias,
    out_weight,
    out_bias,
    fc_in_weight,
    fc_in_bias,
    fc_out_weight,
    fc_out_bias,
):
    gathered = (
        lax.all_gather(ln_gain, ("seq", "fsdp"), axis=0, tiled=True),
        lax.all_gather(ln_bias, ("seq", "fsdp"), axis=0, tiled=True),
        lax.all_gather(qkv_weight, ("seq", "fsdp"), axis=0, tiled=True),
        lax.all_gather(qkv_bias, ("seq", "fsdp"), axis=0, tiled=True),
        lax.all_gather(out_weight, ("seq", "fsdp"), axis=0, tiled=True),
        lax.all_gather(out_bias, ("seq", "fsdp"), axis=0, tiled=True),
        lax.all_gather(fc_in_weight, ("seq", "fsdp"), axis=0, tiled=True),
        lax.all_gather(fc_in_bias, ("seq", "fsdp"), axis=0, tiled=True),
        lax.all_gather(fc_out_weight, ("seq", "fsdp"), axis=0, tiled=True),
        lax.all_gather(fc_out_bias, ("seq", "fsdp"), axis=0, tiled=True),
    )
    norm_multiplier, norm_shift, w_qkv, b_qkv, w_out, b_out, w_in, b_in, w_fc, b_fc = gathered
    norm_multiplier = norm_multiplier.astype(jnp.float32)
    norm_shift = norm_shift.astype(jnp.float32)
    groups = lax.axis_size("seq")
    per_group = H // groups
    local_seqs = hidden_in.shape[0]
    tok_count = hidden_in.shape[1]
    row_count = local_seqs * tok_count
    tokens = hidden_in.reshape(row_count, D).astype(jnp.float32)
    average = jnp.mean(tokens, axis=-1, keepdims=True)
    centered = tokens - average
    spread = jnp.mean(centered * centered, axis=-1, keepdims=True)
    inv_std = lax.rsqrt(spread + 1e-05)
    rescaled_rows = centered * inv_std
    normed = (rescaled_rows * norm_multiplier + norm_shift).astype(jnp.bfloat16)
    projected = jnp.dot(normed, w_qkv, preferred_element_type=jnp.float32) + b_qkv.astype(
        jnp.float32
    )
    segments_all = lax.all_gather(document_labels, "seq", axis=1, tiled=True)
    angles_all = jax.vmap(position_angles)(segments_all)
    angles = lax.dynamic_slice_in_dim(
        angles_all, lax.axis_index("seq") * tok_count, tok_count, 1
    ).reshape(row_count, ROT // 2)
    cosine = jnp.cos(angles)[:, None, None, :]
    sine_part = jnp.sin(angles)[:, None, None, :]
    head_parts = projected.reshape(row_count, H, 3, HD)
    turned = jnp.concatenate(
        [rotate(head_parts[:, :, :2], cosine, sine_part), head_parts[:, :, 2:]], axis=2
    ).astype(jnp.bfloat16)
    outgoing = turned.reshape(local_seqs, tok_count, groups, per_group * 3 * HD)
    arrived = lax.all_to_all(outgoing, "seq", split_axis=2, concat_axis=1, tiled=True)
    length = arrived.shape[1]
    local_heads = arrived.reshape(local_seqs, length, per_group, 3, HD)
    queries_seq = local_heads[:, :, :, 0]
    keys_seq = local_heads[:, :, :, 1]
    values_seq = local_heads[:, :, :, 2]
    block_rows = min(512, length)
    block_count = length // block_rows
    scale_factor = 1.0 / math.sqrt(HD)

    def attend_forward(inputs):
        query_all, key_everywhere, value_all, segments = inputs

        def forward_step(running, block_index):
            first_row = block_index * block_rows
            query_rows = lax.dynamic_slice_in_dim(query_all, first_row, block_rows, 0)
            allowed = make_mask(segments, first_row, block_rows)
            raw_scores = (
                jnp.einsum(
                    "qhd,khd->hqk", query_rows, key_everywhere, preferred_element_type=jnp.float32
                )
                * scale_factor
            )
            raw_scores = jnp.where(allowed[None], raw_scores, -1e30)
            row_max = jnp.max(raw_scores, axis=-1, keepdims=True)
            unscaled = jnp.exp(raw_scores - row_max)
            row_total = jnp.sum(unscaled, axis=-1, keepdims=True)
            probabilities = (unscaled / row_total).astype(jnp.bfloat16)
            context_rows = jnp.einsum(
                "hqk,khd->qhd", probabilities, value_all, preferred_element_type=jnp.float32
            )
            log_total = (row_max + jnp.log(row_total))[..., 0]
            return (running, (context_rows, log_total))

        _, (context_blocks, log_blocks) = lax.scan(
            forward_step, None, jnp.arange(block_count, dtype=jnp.int32)
        )
        return (context_blocks.reshape(length, per_group * HD).astype(jnp.bfloat16), log_blocks)

    context_seq, log_totals = lax.map(
        attend_forward, (queries_seq, keys_seq, values_seq, segments_all)
    )
    context_heads = context_seq.reshape(local_seqs, length, 1, per_group * HD)
    returned = lax.all_to_all(context_heads, "seq", split_axis=1, concat_axis=2, tiled=True)
    context = returned.reshape(row_count, D)
    attn_out = jnp.dot(context, w_out, preferred_element_type=jnp.float32) + b_out.astype(
        jnp.float32
    )
    hidden_pre = jnp.dot(normed, w_in, preferred_element_type=jnp.float32) + b_in.astype(
        jnp.float32
    )
    activated = jax.nn.gelu(hidden_pre, approximate=False).astype(jnp.bfloat16)
    mlp_out = jnp.dot(activated, w_fc, preferred_element_type=jnp.float32) + b_fc.astype(
        jnp.float32
    )
    output = (tokens + attn_out + mlp_out).astype(jnp.bfloat16).reshape(local_seqs, tok_count, D)
    grad_out = cotangent.reshape(row_count, D)
    grad_wide = grad_out.astype(jnp.float32)
    out_bias_grad = jnp.sum(grad_wide, axis=0)
    fc_out_bias_grad = jnp.sum(grad_wide, axis=0)
    out_weight_grad = outer_product(context, grad_out)
    fc_out_weight_grad = outer_product(activated, grad_out)
    act_grad = times_transposed(grad_out, w_fc)
    _, gelu_back = jax.vjp(partial(jax.nn.gelu, approximate=False), hidden_pre)
    hidden_grad = gelu_back(act_grad)[0].astype(jnp.bfloat16)
    fc_in_weight_grad = outer_product(normed, hidden_grad)
    fc_in_bias_grad = jnp.sum(hidden_grad.astype(jnp.float32), axis=0)
    context_grad = times_transposed(grad_out, w_out).astype(jnp.bfloat16)
    grad_outgoing = context_grad.reshape(local_seqs, tok_count, groups, per_group * HD)
    head_grad_seq = lax.all_to_all(
        grad_outgoing, "seq", split_axis=2, concat_axis=1, tiled=True
    ).reshape(local_seqs, length, per_group, HD)

    def attend_backward(inputs):
        query_all, key_everywhere, value_all, segments, head_grad, log_blocks = inputs

        def backward_step(running, block_index):
            key_acc, value_accumulator = running
            first_row = block_index * block_rows
            query_rows = lax.dynamic_slice_in_dim(query_all, first_row, block_rows, 0)
            grad_rows = lax.dynamic_slice_in_dim(head_grad, first_row, block_rows, 0)
            log_rows = log_blocks[block_index]
            allowed = make_mask(segments, first_row, block_rows)
            raw_scores = (
                jnp.einsum(
                    "qhd,khd->hqk", query_rows, key_everywhere, preferred_element_type=jnp.float32
                )
                * scale_factor
            )
            raw_scores = jnp.where(allowed[None], raw_scores, -1e30)
            probabilities = jnp.where(allowed[None], jnp.exp(raw_scores - log_rows[..., None]), 0.0)
            value_accumulator = value_accumulator + jnp.einsum(
                "hqk,qhd->khd",
                probabilities.astype(jnp.bfloat16),
                grad_rows,
                preferred_element_type=jnp.float32,
            )
            prob_grad = jnp.einsum(
                "qhd,khd->hqk", grad_rows, value_all, preferred_element_type=jnp.float32
            )
            inner_total = jnp.sum(probabilities * prob_grad, axis=-1, keepdims=True)
            score_grad = (probabilities * (prob_grad - inner_total)).astype(jnp.bfloat16)
            query_grad = (
                jnp.einsum(
                    "hqk,khd->qhd", score_grad, key_everywhere, preferred_element_type=jnp.float32
                )
                * scale_factor
            )
            key_acc = (
                key_acc
                + jnp.einsum(
                    "hqk,qhd->khd", score_grad, query_rows, preferred_element_type=jnp.float32
                )
                * scale_factor
            )
            return ((key_acc, value_accumulator), query_grad)

        empty_grad = jnp.zeros((length, per_group, HD), jnp.float32)
        (key_grad, value_grad), query_blocks = lax.scan(
            backward_step, (empty_grad, empty_grad), jnp.arange(block_count, dtype=jnp.int32)
        )
        query_grad = query_blocks.reshape(length, per_group, HD)
        return jnp.stack([query_grad, key_grad, value_grad], axis=2).astype(jnp.bfloat16)

    stacked = lax.map(
        attend_backward,
        (queries_seq, keys_seq, values_seq, segments_all, head_grad_seq, log_totals),
    )
    returned_grad = lax.all_to_all(
        stacked.reshape(local_seqs, length, 1, per_group * 3 * HD),
        "seq",
        split_axis=1,
        concat_axis=2,
        tiled=True,
    )
    back_heads = returned_grad.reshape(row_count, H, 3, HD).astype(jnp.float32)
    unturned = jnp.concatenate(
        [rotate(back_heads[:, :, :2], cosine, -sine_part), back_heads[:, :, 2:]], axis=2
    )
    projected_grad = unturned.reshape(row_count, 3 * D).astype(jnp.bfloat16)
    qkv_weight_grad = outer_product(normed, projected_grad)
    qkv_bias_grad = jnp.sum(projected_grad.astype(jnp.float32), axis=0)
    normalized_gradient = times_transposed(projected_grad, w_qkv) + times_transposed(
        hidden_grad, w_in
    )
    ln_gain_grad = jnp.sum(normalized_gradient * rescaled_rows, axis=0)
    ln_bias_grad = jnp.sum(normalized_gradient, axis=0)
    standardized_gradient = normalized_gradient * norm_multiplier
    norm_back = (
        standardized_gradient
        - jnp.mean(standardized_gradient, axis=-1, keepdims=True)
        - rescaled_rows * jnp.mean(standardized_gradient * rescaled_rows, axis=-1, keepdims=True)
    ) * inv_std
    input_grad = (grad_wide + norm_back).astype(jnp.bfloat16).reshape(local_seqs, tok_count, D)
    summed = (
        lax.psum_scatter(ln_gain_grad, ("seq", "fsdp"), scatter_dimension=0, tiled=True),
        lax.psum_scatter(ln_bias_grad, ("seq", "fsdp"), scatter_dimension=0, tiled=True),
        lax.psum_scatter(qkv_weight_grad, ("seq", "fsdp"), scatter_dimension=0, tiled=True),
        lax.psum_scatter(qkv_bias_grad, ("seq", "fsdp"), scatter_dimension=0, tiled=True),
        lax.psum_scatter(out_weight_grad, ("seq", "fsdp"), scatter_dimension=0, tiled=True),
        lax.psum_scatter(out_bias_grad, ("seq", "fsdp"), scatter_dimension=0, tiled=True),
        lax.psum_scatter(fc_in_weight_grad, ("seq", "fsdp"), scatter_dimension=0, tiled=True),
        lax.psum_scatter(fc_in_bias_grad, ("seq", "fsdp"), scatter_dimension=0, tiled=True),
        lax.psum_scatter(fc_out_weight_grad, ("seq", "fsdp"), scatter_dimension=0, tiled=True),
        lax.psum_scatter(fc_out_bias_grad, ("seq", "fsdp"), scatter_dimension=0, tiled=True),
    )
    return (
        output,
        input_grad,
        summed[0],
        summed[1],
        summed[2],
        summed[3],
        summed[4],
        summed[5],
        summed[6],
        summed[7],
        summed[8],
        summed[9],
    )


def dot(left, right):
    return jnp.dot(left, right, preferred_element_type=F32)


def swap(value, axis, bit):
    return lax.ppermute(value, axis, [(i, i ^ bit) for i in range(lax.axis_size(axis))])


def shift(value, by):
    count = lax.axis_size("seq")
    return lax.ppermute(
        value, "seq", [(i, i + by) for i in range(count) if 0 <= i + by < count]
    )


class Clock:
    def __init__(self, token):
        self.token = token

    def join(self, *values):
        values, self.token = lax.optimization_barrier((values, self.token))
        return values


X, Y, NEAR, FAR = 1, 2, 4, 8
CHIPS = 16
ORDER = [0, 8, 4, 12, 1, 9, 5, 13, 2, 10, 6, 14, 3, 11, 7, 15]
SUMS = {"ax": [0, 8, 1, 9], "by": [4, 12, 6, 14], "yax": [2, 10, 3, 11], "xby": [5, 13, 7, 15]}


def place_of(chip):
    return (chip // FAR) % 2 + (chip // NEAR) % 2 * 2 + chip % 2 * 4 + (chip // Y) % 2 * 8


def cross(value, bit):
    return swap(value, "seq", bit // 4) if bit >= 4 else swap(value, "fsdp", bit * 2)


def other_core(value):
    return swap(value, "fsdp", 1)


class Gather:
    def __init__(self, shard):
        self.parts = {"s": shard}

    def jobs(self, stage):
        parts = self.parts
        if stage == "near":
            parts["a"] = jnp.concatenate([parts["s"], parts["f"]], axis=0)
        if stage == "second":
            parts["ax"] = jnp.concatenate([parts["a"], parts["xa"]], axis=0)
            parts["by"] = jnp.concatenate([parts["b"], parts["yb"]], axis=0)
        return {
            "far": [("f", "s", FAR)],
            "near": [("b", "a", NEAR)],
            "first": [("xa", "a", X), ("yb", "b", Y)],
            "second": [("yax", "ax", Y), ("xby", "by", X)],
        }[stage]

    def pieces(self):
        return [self.parts[name] for name in SUMS]


LAY = [(0, 0), (1, 0), (0, 1), (3, 0), (2, 0), (1, 1), (2, 1), (3, 1)]


def gathered(refs, columns=slice(None), which=slice(None)):
    half = refs[0].shape[0] // 2
    return jnp.concatenate(
        [refs[array][part * half : part * half + half, columns] for array, part in LAY[which]],
        axis=0,
    )


BLOCKS = {
    "a": [0, 8],
    "xa": [1, 9],
    "b": [4, 12],
    "yb": [6, 14],
    "yax": [2, 10, 3, 11],
    "xby": [5, 13, 7, 15],
}


class Scatter:
    def __init__(self, blocks):
        self.parts = dict(zip(BLOCKS, blocks))

    def total(self, first, last, *names):
        return sum(self.parts[name][first:last].astype(F32) for name in names)

    def jobs(self, stage):
        parts = self.parts
        rows = parts["a"].shape[0]
        if stage == "second":
            for name, other in (("xa", "r_yax"), ("yb", "r_xby")):
                value = parts[name].astype(F32) + parts[other][rows:].astype(F32)
                parts[name] = value.astype(BF)
        if stage == "near":
            parts["b"] = self.total(0, rows, "b", "r_xby", "r_yb").astype(BF)
        if stage == "far":
            value = self.total(rows // 2, rows, "a", "r_yax", "r_xa", "r_b")
            parts["send"] = value.astype(BF)
        return {
            "first": [("r_yax", "yax", Y), ("r_xby", "xby", X)],
            "second": [("r_xa", "xa", X), ("r_yb", "yb", Y)],
            "near": [("r_b", "b", NEAR)],
            "far": [("r_far", "send", FAR)],
        }[stage]

    def result(self):
        rows = self.parts["a"].shape[0] // 2
        return self.total(0, rows, "a", "r_yax", "r_xa", "r_b", "r_far")


def cost(flops, bytes_accessed, transcendentals=0):
    return pl.CostEstimate(
        flops=flops, bytes_accessed=bytes_accessed, transcendentals=transcendentals
    )


SMEM = pl.BlockSpec(memory_space=pltpu.SMEM)
VMEM = pl.BlockSpec(memory_space=pltpu.VMEM)
ANY = pl.BlockSpec(memory_space=pl.ANY)


def whole(array):
    return pl.BlockSpec(array.shape, lambda *_: (0,) * len(array.shape))


def shaped(rows, columns, dtype):
    return jax.ShapeDtypeStruct((rows, columns), dtype)


def stack(refs):
    return jnp.concatenate([ref[...] for ref in refs], axis=0)


def lanes_low(rows):
    return lax.broadcasted_iota(jnp.int32, (rows, 128), 1) < HD


def cut_kernel(where_ref, qkv_ref, in_ref, out_w_ref, gain_ref, shift_ref, qb_ref, ob_ref, ib_ref, fb_ref, label_ref, *refs):
    keep1, give1, keep2, give2, in_keep, in_give, folded, columns_ref, line_ref = refs
    core = where_ref[1]
    rows = qkv_ref.shape[0]
    columns_ref[...] = jnp.zeros_like(columns_ref)
    for row, ref in enumerate((gain_ref, shift_ref, ob_ref, fb_ref)):
        columns_ref[row : row + 1, :rows] = ref[...].astype(F32)
    line_ref[...] = jnp.zeros_like(line_ref)
    line_ref[0:1, :96] = qb_ref[...].astype(F32)
    line_ref[1:2, :] = ib_ref[...].astype(F32)
    bias, units = line_ref[0:1, :], line_ref[1:2, :]
    lane = lax.broadcasted_iota(jnp.int32, (1, 128), 1)
    first = core == 0
    parts = []
    for seq in range(2):
        for part in range(2):
            labels = (label_ref[seq : seq + 1, 128 * part : 128 * part + 128] + 1).astype(F32)
            parts += [pltpu.roll(labels, HD, 1), labels]
    zero = jnp.zeros_like(bias)
    parts.append(jnp.where(first, pltpu.roll(bias, 64, 1), zero))
    parts.append(
        jnp.where(
            first,
            jnp.where(lane < 96, bias, zero),
            jnp.where(lane >= 96, pltpu.roll(bias, 96, 1), zero),
        )
    )
    parts.append(jnp.where(first, zero, pltpu.roll(bias, 32, 1)))
    parts += [pltpu.roll(units, HD, 1), units]
    for row, value in enumerate(parts):
        line_ref[row : row + 1, :] = value
    low = lanes_low(rows)
    side = jnp.where(low, columns_ref[...].T[:rows], line_ref[...]).astype(BF)
    for owner, out1, out2 in ((core, keep1, keep2), (1 - core, give1, give2)):
        for group in range(GROUPS):
            at = pl.multiple_of((owner * GROUPS + group) * 384, 128)
            b0, b1, b2 = (
                qkv_ref[:, pl.ds(at + 128 * part, 128)].astype(F32) for part in range(3)
            )
            out = out1 if group < 2 else out2
            place = (group % 2) * 384
            turned = pltpu.roll(b0, HD, 1), pltpu.roll(b2, HD, 1)
            out[:, place : place + 128] = jnp.where(low, b0, b1).astype(BF)
            out[:, place + 128 : place + 256] = jnp.where(low, *turned).astype(BF)
            out[:, place + 256 : place + 384] = jnp.where(low, b1, b2).astype(BF)
        out1[:, 768:] = side
    for owner, out in ((core, in_keep), (1 - core, in_give)):
        for block in range(CHIPS):
            at = pl.multiple_of((2 * block + owner) * 128, 128)
            out[:, block * 128 : block * 128 + 128] = in_ref[:, pl.ds(at, 128)]
    folded[:rows, :] = out_w_ref[:, : D // 2]
    folded[rows:, :] = out_w_ref[:, D // 2 :]


def cut(where, qkv_rows, in_rows, out_rows, vectors, labels):
    rows = qkv_rows.shape[0]
    widths = (896, 896, 768, 768, 2048, 2048)
    return pl.pallas_call(
        cut_kernel,
        out_shape=tuple(shaped(rows, width, BF) for width in widths)
        + (shaped(2 * rows, D // 2, BF),),
        in_specs=[SMEM] + [VMEM] * 10,
        out_specs=(VMEM,) * 7,
        scratch_shapes=[pltpu.VMEM((128, 128), F32), pltpu.VMEM((rows, 128), F32)],
        cost_estimate=cost(0, 8 * rows * 4 * D),
        name="cut",
    )(where, qkv_rows, in_rows, out_rows, *[vector.reshape(1, -1) for vector in vectors], labels)


def turn(value, cosine, forth, back):
    return (
        value * cosine
        + pltpu.roll(value, 128 - ROT // 2, 1) * forth
        + pltpu.roll(value, ROT // 2, 1) * back
    )


def marks_kernel(where_ref, a_ref, b_ref, speed_ref, forth_ref, back_ref, bias_ref, cos_ref, to_ref, from_ref, side_ref):
    seq = pl.program_id(0)
    line, core = where_ref[0] // 4, where_ref[1]

    @pl.when(seq == 0)
    def _():
        side_ref[:128, :] = a_ref[...].astype(F32)
        side_ref[128:, :] = b_ref[...].astype(F32)

    owner = jnp.where(seq < 2, core, 1 - core)
    low = lanes_low(1)
    chunks = []
    for back in range(3):
        other = line - back
        relative = jnp.where(other >= 0, other, 0) ^ line
        block = relative // 2 + 2 * (relative % 2)
        rows = side_ref[pl.ds(pl.multiple_of(block * 64 + owner * 32, 8), 8), :]
        rows = jnp.where(seq % 2 == 0, rows[:4], rows[4:])
        rows = jnp.where(other >= 0, rows, jnp.zeros_like(rows))
        chunks.append(
            [
                jnp.where(low, pltpu.roll(rows[i : i + 1], HD, 1), rows[i + 1 : i + 2])
                for i in (0, 2)
            ]
        )
    total = None
    query = lax.broadcasted_iota(jnp.int32, (128, 256), 1)
    key = lax.broadcasted_iota(jnp.int32, (128, 256), 0)
    mine = jnp.concatenate(chunks[0], axis=1)
    for back, halves in enumerate(chunks):
        for half, labels in enumerate(halves):
            column = jnp.broadcast_to(labels, (128, 128)).T
            column = jnp.concatenate([column, column], axis=1)
            same = column == mine
            if back == 0:
                same = same & (key + 128 * half <= query)
            at = back * 256 + half * 128
            bias_ref[0, at : at + 128, :] = jnp.where(same, 0.0, -1e30)
            count = jnp.sum(jnp.where(same, 1.0, 0.0), axis=0, keepdims=True)
            total = count if total is None else total + count
    for half in range(2):
        position = total[:, 128 * half : 128 * half + 128] - 1.0
        angle = jnp.broadcast_to(position, (128, 128)).T * speed_ref[...]
        here = slice(128 * half, 128 * half + 128)
        cos_ref[here, :] = jnp.cos(angle)
        sine = jnp.sin(angle)
        to_ref[here, :] = sine * forth_ref[...]
        from_ref[here, :] = sine * back_ref[...]


def marks(where, a, b):
    half = ROT // 2
    inverse = 1.0 / 10000.0 ** (jnp.arange(0, ROT, 2, dtype=F32) / ROT)
    speed = jnp.concatenate([inverse, inverse, jnp.zeros((HD - ROT,), F32)])
    speed = jnp.concatenate([speed, speed]).reshape(1, 128)
    lanes = np.arange(128) % HD
    forth = jnp.asarray(-(lanes < half).astype(np.float32)[None, :])
    back = jnp.asarray(((lanes >= half) & (lanes < ROT)).astype(np.float32)[None, :])
    side = pl.BlockSpec((128, 128), lambda i: (0, 6))
    table = pl.BlockSpec((256, 128), lambda i: (i, 0))
    return pl.pallas_call(
        marks_kernel,
        grid=(4,),
        out_shape=(jax.ShapeDtypeStruct((4, 768, 256), F32),) + (shaped(1024, 128, F32),) * 3,
        in_specs=[SMEM, side, side, whole(speed), whole(forth), whole(back)],
        out_specs=(pl.BlockSpec((1, 768, 256), lambda i: (i, 0, 0)), table, table, table),
        scratch_shapes=[pltpu.VMEM((256, 128), F32)],
        cost_estimate=cost(1024 * 128 * 100, 4 * 1024 * 1024),
        name="marks",
    )(where, a, b, speed, forth, back)


def choice_into(me, chosen_ref):
    step = 128
    column = lax.broadcasted_iota(jnp.int32, (1, D), 1)
    place = column // 64
    chip = place % 2 * FAR + (place // 2) % 2 * NEAR + (place // 4) % 2 * X + place // 8 * Y
    wanted = (chip ^ me) * 64 + column % 64

    def some(i, carry):
        here = pl.ds(pl.multiple_of(i * step, step), step)
        row = lax.broadcasted_iota(jnp.int32, (step, D), 0) + i * step
        chosen_ref[here, :] = jnp.where(row == wanted, 1.0, 0.0).astype(BF)
        return carry

    lax.fori_loop(0, D // step, some, 0)


def prepare_kernel(
    steps, where_ref, own_ref, other_ref, xhat_ref, inv_ref, chosen_ref, rows_ref
):
    step = pl.program_id(0)

    @pl.when(step == 0)
    def _():
        choice_into(where_ref[0], chosen_ref)

    @pl.when(step < steps)
    def _():
        rows_ref[...] = own_ref[...]

    @pl.when(step >= steps)
    def _():
        rows_ref[...] = other_ref[...]

    x = dot(rows_ref[...], chosen_ref[...])
    average = jnp.mean(x, axis=-1, keepdims=True)
    centered = x - average
    spread = jnp.mean(centered * centered, axis=-1, keepdims=True)
    inv_std = lax.rsqrt(spread + 1e-05)
    xhat_ref[...] = centered * inv_std
    inv_ref[...] = inv_std


def prepare(where, own, other):
    rows = own.shape[0]
    step = 128
    steps = rows // step
    return pl.pallas_call(
        partial(prepare_kernel, steps),
        grid=(2 * steps,),
        out_shape=(shaped(2 * rows, D, F32), shaped(2 * rows, 1, F32)),
        in_specs=[
            SMEM,
            pl.BlockSpec((step, D), lambda i: (jnp.minimum(i, steps - 1), 0)),
            pl.BlockSpec((step, D), lambda i: (jnp.maximum(i - steps, 0), 0)),
        ],
        out_specs=(
            pl.BlockSpec((step, D), lambda i: (i, 0)),
            pl.BlockSpec((step, 1), lambda i: (i, 0)),
        ),
        scratch_shapes=[pltpu.VMEM((D, D), BF), pltpu.VMEM((step, D), BF)],
        cost_estimate=cost(4 * rows * D * D, 16 * rows * D),
        name="prepare",
    )(where, own, other)


def emit_heads(value, tables, outs):
    pairs = [
        (q_ref, kv_ref, pair)
        for q_ref, kv_ref in zip(outs[::2], outs[1::2])
        for pair in range(q_ref.shape[1] // 128)
    ]
    for index, (q_ref, kv_ref, pair) in enumerate(pairs):
        first, q, k = index * 384, pair * 128, pair * 256
        q_ref[:, q : q + 128] = turn(value[:, first : first + 128], *tables).astype(BF)
        kv_ref[:, k : k + 128] = turn(value[:, first + 128 : first + 256], *tables).astype(BF)
        kv_ref[:, k + 128 : k + 256] = value[:, first + 256 : first + 384].astype(BF)


def project_first_kernel(where_ref, xhat_ref, cos_ref, forth_ref, back_ref, *refs):
    pieces, outs = refs[:4], refs[4:8]
    normed_ref, normed_t_ref, more_ref, units_ref, rows_ref, gain_ref, side_ref, bias_ref, two_ref = refs[8:]
    me, core = where_ref[0], where_ref[1]

    @pl.when(pl.program_id(0) == 0)
    def _():
        side_ref[...] = gathered(pieces, slice(768, 896)).astype(F32)
        across = side_ref[...].T
        two_ref[...] = across[:8]
        gain_ref[...] = across[0:1]
        rows_ref[...] = across[2:3] + across[3:4]
        low = lanes_low(1)

        def block(chip, owner):
            start = place_of(chip ^ me) * 64 + owner * 32 + 8
            return side_ref[pl.ds(pl.multiple_of(start, 8), 8), :]

        def pair(one, two):
            return jnp.where(low, pltpu.roll(one, HD, 1), two)

        for group in range(GROUPS):
            heads = []
            for head in range(2):
                chip = core * 8 + 2 * group + head
                zero, one = block(chip, 0), block(chip, 1)
                heads.append((zero[0:1], zero[1:2] + one[1:2], one[2:3]))
            out = bias_ref if group < 2 else more_ref
            for part in range(3):
                at = (group % 2) * 384 + part * 128
                out[:, at : at + 128] = pair(heads[0][part], heads[1][part])
        for chip in range(CHIPS):
            found = block(chip, core)
            units_ref[:, chip * 128 : chip * 128 + 128] = pair(found[3:4], found[4:5])

    normed = (xhat_ref[...] * two_ref[0:1, :] + two_ref[1:2, :]).astype(BF)
    normed_ref[...] = normed
    normed_t_ref[...] = normed.T
    value = dot(normed, gathered(pieces, slice(0, 768))) + bias_ref[...]
    emit_heads(value, (cos_ref[...], forth_ref[...], back_ref[...]), outs)


TWO_PAIRS = (shaped(1024, 128, BF), shaped(1024, 256, BF)) * 2
ONE_GROUP = (shaped(1024, 256, BF), shaped(1024, 512, BF))


def rows_spec(columns, step=256):
    return pl.BlockSpec((step, columns), lambda i: (i, 0))


def project_first(where, xhat, tables, pieces):
    small = (shaped(1, 768, F32), shaped(1, 2048, F32), shaped(1, D, F32), shaped(1, D, F32))
    return pl.pallas_call(
        project_first_kernel,
        grid=(4,),
        out_shape=TWO_PAIRS + (shaped(1024, D, BF), shaped(D, 1024, BF)) + small,
        in_specs=[SMEM, rows_spec(D)] + [rows_spec(128)] * 3 + [whole(piece) for piece in pieces],
        out_specs=tuple(rows_spec(shape.shape[1]) for shape in TWO_PAIRS)
        + (rows_spec(D), pl.BlockSpec((D, 256), lambda i: (0, i)))
        + tuple(whole(shape) for shape in small),
        scratch_shapes=[
            pltpu.VMEM((D, 128), F32),
            pltpu.VMEM((1, 768), F32),
            pltpu.VMEM((8, D), F32),
        ],
        cost_estimate=cost(2 * 1024 * D * 768, 12 * 1024 * D),
        name="project_first",
    )(where, xhat, *tables, *pieces)


def project_more_kernel(normed_ref, bias_ref, cos_ref, forth_ref, back_ref, *refs):
    value = dot(normed_ref[...], gathered(refs[:4], slice(512, 1280))) + bias_ref[...]
    emit_heads(value, (cos_ref[...], forth_ref[...], back_ref[...]), refs[4:])


def project_more(normed, bias, tables, pieces):
    return pl.pallas_call(
        project_more_kernel,
        grid=(4,),
        out_shape=ONE_GROUP,
        in_specs=[rows_spec(D), whole(bias)]
        + [rows_spec(128)] * 3
        + [whole(piece) for piece in pieces],
        out_specs=tuple(rows_spec(shape.shape[1]) for shape in ONE_GROUP),
        cost_estimate=cost(2 * 1024 * D * 768, 6 * 1024 * D),
        name="project_more",
    )(normed, bias, *tables, *pieces)


def head_rows_kernel(where_ref, *refs):
    keep_ref, give_ref, held_ref = refs[4:]
    me, core = where_ref[0], where_ref[1]
    for index, chip in enumerate(ORDER):
        array, part = LAY[index // 2]
        piece, at = refs[array], part * 128 + index % 2 * 64
        found = chip ^ me
        start = pl.multiple_of((((found // 8) ^ core) * 8 + found % 8) * 32, 32)
        held_ref[pl.ds(start, 32), : D // 2] = piece[at : at + 32, :]
        held_ref[pl.ds(start, 32), D // 2 :] = piece[at + 32 : at + 64, :]
    keep_ref[...] = held_ref[:256, :]
    give_ref[...] = held_ref[256:, :]


def head_rows(where, pieces):
    return pl.pallas_call(
        head_rows_kernel,
        out_shape=(shaped(256, D, BF),) * 2,
        grid=(1,),
        in_specs=[SMEM] + [pl.BlockSpec((256, D // 2), lambda i: (0, 0))] * 4,
        out_specs=(pl.BlockSpec((256, D), lambda i: (0, 0)),) * 2,
        scratch_shapes=[pltpu.VMEM((512, D), BF)],
        cost_estimate=cost(0, 4 * 512 * D),
        name="head_rows",
    )(where, *pieces)


def context_grad_kernel(
    where_ref, own_ref, other_ref, keep_ref, more_ref, grad_ref, heads_ref, rows_ref
):
    core = where_ref[1]
    step = pl.program_id(0)

    @pl.when(step == 0)
    def _():
        for chip in range(8):
            rows = slice(chip * 32, chip * 32 + 32)
            heads_ref[pl.ds(pl.multiple_of(chip * 64 + core * 32, 32), 32), :] = keep_ref[rows, :]
            at = pl.multiple_of(chip * 64 + (1 - core) * 32, 32)
            heads_ref[pl.ds(at, 32), :] = more_ref[rows, :]

    @pl.when(step < 2)
    def _():
        rows_ref[...] = own_ref[...]

    @pl.when(step >= 2)
    def _():
        rows_ref[...] = other_ref[...]

    grad_ref[...] = times_transposed(rows_ref[...], heads_ref[...]).astype(BF)


def context_gradient(where, own, other, keep, more):
    return pl.pallas_call(
        context_grad_kernel,
        grid=(4,),
        out_shape=(shaped(1024, D // 2, BF), shaped(D // 2, D, BF)),
        in_specs=[
            SMEM,
            pl.BlockSpec((256, D), lambda i: (jnp.minimum(i, 1), 0)),
            pl.BlockSpec((256, D), lambda i: (jnp.maximum(i - 2, 0), 0)),
            whole(keep),
            whole(more),
        ],
        out_specs=(rows_spec(D // 2), pl.BlockSpec((D // 2, D), lambda i: (0, 0))),
        scratch_shapes=[pltpu.VMEM((256, D), BF)],
        cost_estimate=cost(1024 * D * D, 6 * 1024 * D),
        name="context_grad",
    )(where, own, other, keep, more)


def attend_kernel(q_ref, do_ref, bias_ref, *refs):
    kv_refs, o_ref, dq_ref, dkv_refs = refs[:3], refs[3], refs[4], refs[5:8]
    weight_ref, probs_ref, grad_ref = refs[8:]
    rows = q_ref.shape[0]
    scaled = q_ref[...] * 0.125
    given = do_ref[...]
    given_t = given.T.astype(F32)
    low = lanes_low(rows)
    zero = jnp.zeros_like(given)

    def heads(value):
        return jnp.concatenate([jnp.where(low, value, zero), jnp.where(low, zero, value)], axis=0)

    queries, grads = heads(scaled), heads(given)
    spans = [slice(chunk * rows, chunk * rows + rows) for chunk in range(3)]
    top = None
    for here, ref in zip(spans, kv_refs):
        bias = bias_ref[0, here, :]
        scores = times_transposed(ref[:, :128], queries) + jnp.concatenate([bias, bias], axis=1)
        weight_ref[here, :] = scores
        most = jnp.max(scores, axis=0, keepdims=True)
        top = most if top is None else jnp.maximum(top, most)
    total = jnp.zeros_like(top)
    for here in spans:
        unscaled = jnp.exp(weight_ref[here, :] - top)
        weight_ref[here, :] = unscaled
        total = total + jnp.sum(unscaled, axis=0, keepdims=True)
    inverse = 1.0 / total
    for here in spans:
        probs = weight_ref[here, :] * inverse
        weight_ref[here, :] = probs
        probs_ref[here, :] = probs.astype(BF)

    def both_heads(across, right_ref):
        return jnp.concatenate(
            [dot(across[:HD], right_ref[:, :rows]), dot(across[HD:], right_ref[:, rows:])], axis=0
        )

    values_t = jnp.concatenate([ref[:, 128:] for ref in kv_refs], axis=0).T
    keys_t = jnp.concatenate([ref[:, :128] for ref in kv_refs], axis=0).T
    out_t = both_heads(values_t, probs_ref)
    product = out_t * given_t
    inner = jnp.concatenate(
        [
            jnp.sum(product[:HD], axis=0, keepdims=True),
            jnp.sum(product[HD:], axis=0, keepdims=True),
        ],
        axis=1,
    )
    for here, ref in zip(spans, kv_refs):
        prob_grad = times_transposed(ref[:, 128:], grads)
        grad_ref[here, :] = (weight_ref[here, :] * (prob_grad - inner)).astype(BF)
    dq_t = both_heads(keys_t, grad_ref)
    o_ref[...] = out_t.T.astype(BF)
    dq_ref[...] = (dq_t.T * 0.125).astype(BF)
    for here, ref in zip(spans, dkv_refs):
        ref[:, :128] = dot(grad_ref[here, :], queries).astype(ref.dtype)
        ref[:, 128:] = dot(probs_ref[here, :], grads).astype(ref.dtype)


def attend(first, query, grad, bias, kvs):
    pairs = query.shape[1] // 128
    narrow = pl.BlockSpec((256, 128), lambda b, p: (b, p))
    wide = pl.BlockSpec((256, 256), lambda b, p: (b, p))
    return pl.pallas_call(
        attend_kernel,
        grid=(4, pairs),
        out_shape=(shaped(1024, 128 * pairs, BF),) * 2
        + (shaped(1024, 256 * pairs, F32),)
        + (shaped(1024, 256 * pairs, BF),) * 2,
        in_specs=[
            narrow,
            pl.BlockSpec((256, 128), lambda b, p: (b, first + p)),
            pl.BlockSpec((1, 768, 256), lambda b, p: (b, 0, 0)),
        ]
        + [wide] * 3,
        out_specs=(narrow, narrow) + (wide,) * 3,
        scratch_shapes=[pltpu.VMEM((768, 512), dtype) for dtype in (F32, BF, BF)],
        cost_estimate=cost(
            pairs * 24 * 4 * 256 * 768 * 128, pairs * 9 * 1024 * 1024, pairs * 8 * 256 * 768
        ),
        name="attend",
    )(query, grad, bias, *kvs)


def unturn_kernel(groups, cos_ref, forth_ref, back_ref, *refs):
    cosine, forth, back = cos_ref[...], -forth_ref[...], -back_ref[...]
    out_ref, sum_ref = refs[-2:]
    first = 0
    for group in range(groups):
        dq_ref, own_ref, more_ref = refs[3 * group : 3 * group + 3]
        for pair in range(dq_ref.shape[1] // 128):
            here = slice(pair * 256, pair * 256 + 256)
            kv = (own_ref[:, here] + more_ref[:, here].astype(F32)).astype(BF)
            key = kv[:, :128].astype(F32)
            query = dq_ref[:, pair * 128 : pair * 128 + 128].astype(F32)
            out_ref[:, first : first + 128] = turn(query, cosine, forth, back).astype(BF)
            out_ref[:, first + 128 : first + 256] = turn(key, cosine, forth, back).astype(BF)
            out_ref[:, first + 256 : first + 384] = kv[:, 128:]
            first += 384

    @pl.when(pl.program_id(0) == 0)
    def _():
        sum_ref[...] = jnp.zeros_like(sum_ref)

    sum_ref[...] += jnp.sum(out_ref[...].astype(F32), axis=0, keepdims=True)


def unturn(tables, triples):
    rows = triples[0][0].shape[0]
    step = 256
    width = 3 * sum(dq.shape[1] for dq, _, _ in triples)

    def spec(columns):
        return pl.BlockSpec((step, columns), lambda i: (i, 0))

    specs, arrays = [], []
    for dq, own, more in triples:
        specs += [spec(dq.shape[1]), spec(own.shape[1]), spec(more.shape[1])]
        arrays += [dq, own, more]
    return pl.pallas_call(
        partial(unturn_kernel, len(triples)),
        grid=(rows // step,),
        out_shape=(
            jax.ShapeDtypeStruct((rows, width), BF),
            jax.ShapeDtypeStruct((1, width), F32),
        ),
        in_specs=[spec(128)] * 3 + specs,
        out_specs=(spec(width), pl.BlockSpec((1, width), lambda i: (0, 0))),
        cost_estimate=cost(rows * width * 10, rows * width * 8),
        name="unturn",
    )(*tables, *arrays)


ROOT_HALF = math.sqrt(0.5)
DENSITY = 1.0 / math.sqrt(2.0 * math.pi)


def gelu_and_slope(value):
    share = 0.5 + 0.5 * lax.erf(value * ROOT_HALF)
    return value * share, share + value * (DENSITY * jnp.exp(-0.5 * value * value))


def hidden_kernel(normed_ref, bias_ref, *refs):
    act_ref, act_t_ref, slope_ref, value_ref = refs[-4:]
    rows = 128
    value_ref[...] = dot(normed_ref[...], gathered(refs[:4])) + bias_ref[...]

    def some(i, carry):
        here = pl.ds(pl.multiple_of(i * rows, rows), rows)
        act, slope = gelu_and_slope(value_ref[here, :])
        act = act.astype(BF)
        act_ref[here, :] = act
        act_t_ref[:, here] = act.T
        slope_ref[here, :] = slope
        return carry

    lax.fori_loop(0, normed_ref.shape[0] // rows, some, 0)


def hidden(normed, pieces, bias):
    rows, width = normed.shape[0], bias.shape[1]
    step = 512
    column = pl.BlockSpec((rows, step), lambda j: (0, j))
    return pl.pallas_call(
        hidden_kernel,
        grid=(width // step,),
        out_shape=(shaped(rows, width, BF), shaped(width, rows, BF), shaped(rows, width, F32)),
        in_specs=[whole(normed), pl.BlockSpec((1, step), lambda j: (0, j))]
        + [pl.BlockSpec((piece.shape[0], step), lambda j: (0, j)) for piece in pieces],
        out_specs=(column, pl.BlockSpec((step, rows), lambda j: (j, 0)), column),
        scratch_shapes=[pltpu.VMEM((rows, step), F32)],
        cost_estimate=cost(2 * rows * D * width + 50 * rows * width, 9 * rows * width),
        name="hidden",
    )(normed, bias, *pieces)


def fetch_units(me, pieces, w_ref, sem):
    copies = []
    for index, chip in enumerate(ORDER):
        first = pl.multiple_of((me ^ chip) * 128, 128)
        array, part = LAY[index // 2]
        copies.append(
            pltpu.make_async_copy(
                pieces[array].at[pl.ds(part * 256 + index % 2 * 128, 128), :],
                w_ref.at[pl.ds(first, 128), :],
                sem,
            )
        )
    for copy in copies:
        copy.start()
    return copies


def unit_back_kernel(where_ref, own_ref, other_ref, slope_ref, *refs):
    hg_ref, sum_ref, w_ref, sem = refs[4:]
    j = pl.program_id(0)
    step = hg_ref.shape[1]

    @pl.when(j == 0)
    def _():
        for copy in fetch_units(where_ref[0], refs[:4], w_ref, sem):
            copy.wait()

    w = w_ref[pl.ds(pl.multiple_of(j * step, step), step), :]
    total = None
    rows = own_ref.shape[0]
    for half, g_ref in enumerate((own_ref, other_ref)):
        here = slice(half * rows, half * rows + rows)
        grad = (times_transposed(g_ref[...], w) * slope_ref[here, :]).astype(BF)
        hg_ref[here, :] = grad
        part = jnp.sum(grad.astype(F32), axis=0, keepdims=True)
        total = part if total is None else total + part
    sum_ref[...] = total


def unit_back(where, own, other, slope, pieces):
    rows, width = slope.shape
    step = 512
    column = pl.BlockSpec((rows, step), lambda j: (0, j))
    return pl.pallas_call(
        unit_back_kernel,
        grid=(width // step,),
        out_shape=(shaped(rows, width, BF), shaped(1, width, F32)),
        in_specs=[SMEM, whole(own), whole(other), column] + [ANY] * 4,
        out_specs=(column, pl.BlockSpec((1, step), lambda j: (0, j))),
        scratch_shapes=[pltpu.VMEM((width, D), BF), pltpu.SemaphoreType.DMA],
        cost_estimate=cost(2 * rows * D * width, 8 * rows * width),
        name="unit_back",
    )(where, own, other, slope, *pieces)


def unit_out_kernel(where_ref, act_ref, heads_ref, *refs):
    contexts, pieces = refs[:3], refs[3:7]
    mine_ref, theirs_ref, w_ref, total_ref, sem = refs[7:]
    step = pl.program_id(0)

    @pl.when(step == 0)
    def _():
        for copy in fetch_units(where_ref[0], pieces, w_ref, sem):
            copy.wait()

    context = jnp.concatenate([ref[...] for ref in contexts], axis=1)
    total_ref[...] = dot(act_ref[...], w_ref[...]) + dot(context, heads_ref[...])

    @pl.when(step < 2)
    def _():
        mine_ref[...] = total_ref[...]

    @pl.when(step >= 2)
    def _():
        theirs_ref[...] = total_ref[...]


def unit_out(where, act, heads, contexts, pieces):
    rows, width = act.shape
    return pl.pallas_call(
        unit_out_kernel,
        grid=(4,),
        out_shape=(shaped(rows // 2, D, F32),) * 2,
        in_specs=[SMEM, rows_spec(width), whole(heads)]
        + [rows_spec(context.shape[1]) for context in contexts]
        + [ANY] * 4,
        out_specs=(
            pl.BlockSpec((256, D), lambda i: (jnp.minimum(i, 1), 0)),
            pl.BlockSpec((256, D), lambda i: (jnp.maximum(i - 2, 0), 0)),
        ),
        scratch_shapes=[
            pltpu.VMEM((width, D), BF),
            pltpu.VMEM((256, D), F32),
            pltpu.SemaphoreType.DMA,
        ],
        cost_estimate=cost(3 * rows * D * width, 6 * rows * width),
        name="unit_out",
    )(where, act, heads, *contexts, *pieces)


def row_grads_kernel(steps, where_ref, left_ref, right_ref, *refs):
    out_refs = refs[-6:]
    spots = [[place_of(chip) for chip in chips] for chips in BLOCKS.values()]

    @pl.when(pl.program_id(0) < steps)
    def _():
        value = dot(left_ref[...], right_ref[...]).astype(BF)
        for places, ref in zip(spots, out_refs):
            for at, place in enumerate(places):
                ref[at * 64 : at * 64 + 64, :] = value[place * 64 : place * 64 + 64]

    if len(refs) == 7:
        held_ref = refs[0]
        me, core = where_ref[0], where_ref[1]

        @pl.when(pl.program_id(0) >= steps)
        def _():
            for chips, ref in zip(BLOCKS.values(), out_refs):
                for at, chip in enumerate(chips):
                    found = chip ^ me
                    start = (((found // 8) ^ core) * 8 + found % 8) * 32
                    rows = held_ref[pl.ds(pl.multiple_of(start, 32), 32), :]
                    ref[at * 64 : at * 64 + 32, :] = rows[:, : D // 2]
                    ref[at * 64 + 32 : at * 64 + 64, :] = rows[:, D // 2 :]


def row_grads(where, left, right, more=None):
    rows, tokens = left.shape
    step = 512
    steps = right.shape[1] // step
    columns = right.shape[1] + (0 if more is None else D // 2)
    heights = [64 * len(chips) for chips in BLOCKS.values()]
    return pl.pallas_call(
        partial(row_grads_kernel, steps),
        grid=(columns // step,),
        out_shape=tuple(shaped(height, columns, BF) for height in heights),
        in_specs=[
            SMEM,
            whole(left),
            pl.BlockSpec((tokens, step), lambda j: (0, jnp.minimum(j, steps - 1))),
        ]
        + ([] if more is None else [whole(more)]),
        out_specs=tuple(pl.BlockSpec((height, step), lambda j: (0, j)) for height in heights),
        cost_estimate=cost(2 * rows * tokens * columns, 2 * (rows * tokens + rows * columns)),
        name="row_grads",
    )(where, left, right, *([] if more is None else [more]))


def unit_grads_kernel(order_ref, *refs):
    lefts, own_ref, other_ref, out_refs = refs[:4], refs[4], refs[5], refs[6:]
    left = stack(lefts)
    tokens = own_ref.shape[0]
    a, xa, b, yb, yax, xby = out_refs
    columns = 512

    def some(i, carry):
        here = pl.ds(pl.multiple_of(i * columns, columns), columns)
        value = dot(left[:, :tokens], own_ref[:, here]) + dot(left[:, tokens:], other_ref[:, here])
        value = value.astype(BF)
        for piece, outs in enumerate(((a, xa), (b, yb), (yax,), (xby,))):

            @pl.when(pl.program_id(0) == piece)
            def _(outs=outs):
                rows = 512 // len(outs)
                for at, ref in enumerate(outs):
                    ref[:, here] = value[at * rows : at * rows + rows]

        return carry

    lax.fori_loop(0, D // columns, some, 0)


def unit_grads(me, left, own, other):
    tokens = left.shape[1]
    order = jnp.asarray(np.array(sum(SUMS.values(), []), np.int32)) ^ me

    def block(place):
        return pl.BlockSpec((128, tokens), lambda k, order: (order[4 * k + place], 0))

    return pl.pallas_call(
        unit_grads_kernel,
        out_shape=tuple(shaped(128 * len(chips), D, BF) for chips in BLOCKS.values()),
        grid_spec=pltpu.PrefetchScalarGridSpec(
            num_scalar_prefetch=1,
            grid=(4,),
            in_specs=[block(place) for place in range(4)] + [whole(own), whole(other)],
            out_specs=tuple(
                pl.BlockSpec((128 * len(chips), D), lambda k, order: (0, 0))
                for chips in BLOCKS.values()
            ),
        ),
        cost_estimate=cost(2 * tokens * D * 2048, 4 * 2048 * D),
        name="unit_grads",
    )(order, left, left, left, left, own, other)


def out_grad_kernel(where_ref, own_ref, other_ref, *refs):
    contexts, keep_ref, give_ref, across_ref = refs[:3], refs[3], refs[4], refs[5]
    first = where_ref[1] == 0
    tokens = own_ref.shape[0]
    group = pl.program_id(0)

    @pl.when(group == 0)
    def _():
        lane = 0
        for ref in contexts:
            across_ref[lane : lane + ref.shape[1], :] = ref[...].T
            lane += ref.shape[1]

    across = across_ref[pl.ds(pl.multiple_of(group * 128, 128), 128), :]
    value = dot(across[:, :tokens], own_ref[...]) + dot(across[:, tokens:], other_ref[...])
    value = value.astype(BF)
    for head in range(2):
        zero, one = value[head * 64 : head * 64 + 32], value[head * 64 + 32 : head * 64 + 64]
        rows = slice(head * 32, head * 32 + 32)
        keep_ref[rows, :] = jnp.where(first, zero, one)
        give_ref[rows, :] = jnp.where(first, one, zero)


def out_grad(where, own, other, contexts):
    block = pl.BlockSpec((64, D), lambda i: (i, 0))
    return pl.pallas_call(
        out_grad_kernel,
        grid=(4,),
        out_shape=(shaped(256, D, BF),) * 2,
        in_specs=[SMEM, whole(own), whole(other)] + [whole(context) for context in contexts],
        out_specs=(block, block),
        scratch_shapes=[pltpu.VMEM((D // 2, 1024), BF)],
        cost_estimate=cost(1024 * D * D, 6 * 1024 * D),
        name="out_grad",
    )(where, own, other, *contexts)


def norm_grad_kernel(spans, left_ref, *refs):
    count = 4 * len(spans)
    mine_ref, theirs_ref, total_ref = refs[-3:]
    earlier = refs[count:-3]
    step = pl.program_id(0)
    first = 0
    lefts = []
    for start, end in spans:
        lefts.append(left_ref[:, first : first + end - start])
        first += end - start
    for pair in range(4):
        total = None
        for line, (left, span) in enumerate(zip(lefts, spans)):
            right = gathered(
                refs[4 * line : 4 * line + 4], slice(*span), slice(2 * pair, 2 * pair + 2)
            )
            part = times_transposed(left, right)
            total = part if total is None else total + part
        total_ref[:, 256 * pair : 256 * pair + 256] = total

    for half, out_ref in enumerate((mine_ref, theirs_ref)):

        @pl.when(step // 2 == half)
        def _(half=half, out_ref=out_ref):
            if earlier:
                out_ref[...] = total_ref[...] + earlier[half][...]
            else:
                out_ref[...] = total_ref[...]


def norm_grad(left, lines, spans, earlier=()):
    rows = left.shape[0]
    flat = [piece for line in lines for piece in line]
    halves = (
        pl.BlockSpec((256, D), lambda i: (jnp.minimum(i, 1), 0)),
        pl.BlockSpec((256, D), lambda i: (jnp.maximum(i - 2, 0), 0)),
    )
    return pl.pallas_call(
        partial(norm_grad_kernel, spans),
        grid=(4,),
        out_shape=(shaped(rows // 2, D, F32),) * 2,
        in_specs=[rows_spec(left.shape[1])]
        + [whole(piece) for piece in flat]
        + list(halves[: len(earlier)]),
        out_specs=halves,
        scratch_shapes=[pltpu.VMEM((256, D), F32)],
        cost_estimate=cost(2 * rows * D * left.shape[1], 12 * rows * D),
        name="norm_grad",
    )(left, *flat, *earlier)


def norm_back_kernel(
    where_ref, part_ref, more_ref, xhat_ref, inv_ref, gain_ref, g_ref, out_ref, sum_ref, chosen_ref
):
    @pl.when(pl.program_id(0) == 0)
    def _():
        choice_into(where_ref[0], chosen_ref)
        sum_ref[...] = jnp.zeros_like(sum_ref)

    grad = part_ref[...] + more_ref[...]
    xhat = xhat_ref[...]
    scaled = grad * gain_ref[...]
    value = (
        scaled
        - jnp.mean(scaled, axis=-1, keepdims=True)
        - xhat * jnp.mean(scaled * xhat, axis=-1, keepdims=True)
    ) * inv_ref[...]
    high = value.astype(BF)
    low = (value - high.astype(F32)).astype(BF)
    value = times_transposed(high, chosen_ref[...]) + times_transposed(low, chosen_ref[...])
    out_ref[...] = (g_ref[...].astype(F32) + value).astype(BF)
    sum_ref[0:1, :] += jnp.sum(grad * xhat, axis=0, keepdims=True)
    sum_ref[1:2, :] += jnp.sum(grad, axis=0, keepdims=True)


def norm_back(where, part, more, xhat, inv_std, gain, grad):
    rows = grad.shape[0]
    one = pl.BlockSpec((1, D), lambda i: (0, 0))
    return pl.pallas_call(
        norm_back_kernel,
        grid=(rows // 256,),
        out_shape=(shaped(rows, D, BF), shaped(8, D, F32)),
        in_specs=[SMEM] + [rows_spec(D)] * 3 + [rows_spec(1), one, rows_spec(D)],
        out_specs=(rows_spec(D), pl.BlockSpec((8, D), lambda i: (0, 0))),
        scratch_shapes=[pltpu.VMEM((D, D), BF)],
        cost_estimate=cost(4 * rows * D * D, 16 * rows * D),
        name="norm_back",
    )(where, part, more, xhat, inv_std, gain, grad)


def paste_in_kernel(where_ref, mine_ref, other_ref, out_ref):
    core = where_ref[1]
    for owner, ref in ((core, mine_ref), (1 - core, other_ref)):
        for block in range(CHIPS):
            at = pl.multiple_of((2 * block + owner) * 128, 128)
            out_ref[:, pl.ds(at, 128)] = ref[:, block * 128 : block * 128 + 128]


def paste_qkv_kernel(where_ref, mine_ref, other_ref, out_ref):
    core = where_ref[1]
    low = lanes_low(mine_ref.shape[0])
    for owner, ref in ((core, mine_ref), (1 - core, other_ref)):
        for group in range(GROUPS):
            q, k, v = (
                ref[:, group * 384 + part * 128 : group * 384 + part * 128 + 128]
                for part in range(3)
            )
            turned = pltpu.roll(k, HD, 1)
            blocks = (jnp.where(low, q, turned), jnp.where(low, v, q), jnp.where(low, turned, v))
            for part, value in enumerate(blocks):
                at = (owner * GROUPS + group) * 384 + part * 128
                out_ref[:, pl.ds(pl.multiple_of(at, 128), 128)] = value


def paste(kernel, where, mine, other):
    return pl.pallas_call(
        kernel,
        out_shape=shaped(mine.shape[0], 2 * mine.shape[1], F32),
        in_specs=[SMEM, VMEM, VMEM],
        out_specs=VMEM,
        cost_estimate=cost(0, 16 * mine.shape[0] * mine.shape[1]),
        name="paste",
    )(where, mine, other)


def local_fast(
    hidden_in,
    document_labels,
    cotangent,
    ln_gain,
    ln_bias,
    qkv_weight,
    qkv_bias,
    out_weight,
    out_bias,
    fc_in_weight,
    fc_in_bias,
    fc_out_weight,
    fc_out_bias,
):
    local_seqs, tok_count = hidden_in.shape[:2]
    row_count = local_seqs * tok_count
    d_rows = qkv_weight.shape[0]
    f_rows = fc_out_weight.shape[0]
    units = fc_in_weight.shape[1] // 2
    pair = 2
    core = lax.axis_index("fsdp") % 2
    me = lax.axis_index("seq") * 4 + lax.axis_index("fsdp") // 2
    clock = Clock(jnp.stack([me, core]).astype(jnp.int32))
    box = {}

    waiting = []

    def slot(jobs, work=None, *inputs, chain=None, late=(), then=None):
        nonlocal waiting
        jobs, late = list(jobs), list(late)
        name, follow, more = chain if chain is not None else (None, None, ())
        gated, given, more = clock.join(tuple(job[2] for job in jobs + late), inputs, tuple(more))
        values = [job[3](value) for job, value in zip(jobs + late, gated)]
        made = work(*given) if work is not None else ()
        after = ()
        for job, value in list(zip(jobs, values)) + waiting:
            if chain is not None and job[1] == name:
                after = follow(value, *more)
        if then is not None:
            started = then(made)
            late = late + started
            values = values + [job[3](job[2]) for job in started]
        ended, values, older = waiting, values[: len(jobs)], values[len(jobs) :]
        found = values + [value for _, value in ended]
        found, made, after = clock.join(tuple(found), made, after)
        for job, value in zip(jobs + [job for job, _ in ended], found):
            job[0][job[1]] = value
        waiting = list(zip(late, older))
        return made if chain is None else (made, after)

    def moves(line, stage):
        return [
            (line.parts, name, line.parts[source], partial(cross, bit=bit))
            for name, source, bit in line.jobs(stage)
        ]

    def core_move(name, value):
        return (box, name, value, other_core)

    def pick(halves):
        first = core == 0
        return jnp.where(first, halves[0], halves[1]), jnp.where(first, halves[1], halves[0])

    def joined(mine, other):
        first = core == 0
        return jnp.concatenate(
            [jnp.where(first, mine, other), jnp.where(first, other, mine)], axis=0
        )

    x_own = hidden_in.reshape(row_count, D)
    g_own = cotangent.reshape(row_count, D)
    vectors = (ln_gain, ln_bias, qkv_bias, out_bias, fc_in_bias, fc_out_bias)
    keep1, give1, keep2, give2, in_keep, in_give, folded = cut(
        clock.token, qkv_weight, fc_in_weight, out_weight, vectors, document_labels
    )
    slot([core_move("give1", give1)])
    line_a = Gather(joined(keep1, box["give1"]))
    slot(moves(line_a, "far") + [core_move("x", x_own), core_move("give2", give2)])
    line_b = Gather(jnp.concatenate([folded, joined(keep2, box["give2"])], axis=1))
    line_d = Gather(fc_out_weight)
    slot(moves(line_a, "near") + moves(line_b, "far") + [core_move("in", in_give), core_move("g", g_own)])
    g_more = box["g"]
    bias, *tables = slot(
        moves(line_a, "first") + moves(line_b, "near"),
        lambda a, b: marks(clock.token, a, b),
        line_a.parts["a"],
        line_a.parts["b"],
    )
    line_c = Gather(joined(in_keep, box["in"]))
    (xhat, inv_std), grad_sum = slot(
        moves(line_a, "second") + moves(line_c, "far"),
        lambda own, other, g: (
            prepare(clock.token, own, other),
            jnp.sum(g.astype(F32), axis=0),
        ),
        x_own,
        box["x"],
        g_own,
    )
    a_pieces = line_a.pieces()
    made = slot(
        moves(line_b, "first") + moves(line_c, "near"),
        lambda xhat, tables, pieces: project_first(clock.token, xhat, tables, pieces),
        xhat,
        tables,
        a_pieces,
    )
    queries, kvs = [made[0], made[2]], [[made[1]], [made[3]]]
    normed, normed_t, b_more, b_in, b_rows, gain = made[4:]
    moved, results, backs = {}, {}, {}

    def up(group, hop):
        return (moved, (group, hop), kvs[group][hop], partial(shift, by=1))

    def landed(*found):
        for group, hop in found:
            kvs[group].append(moved[group, hop])

    def down(group, hop):
        value = results[group][4]
        if hop == 1:
            value = (results[group][3].astype(F32) + backs[group, 0].astype(F32)).astype(BF)
        return (backs, (group, hop), value, partial(shift, by=-1))

    def attention(*groups):
        def work(*given):
            return [attend(group, *args) for group, args in zip(groups, given)]

        return work, *[
            (queries[group], context_grad, bias, tuple(kvs[group])) for group in groups
        ]

    def attended(groups, found):
        for group, result in zip(groups, found):
            results[group] = result

    slot(moves(line_b, "second") + [up(0, 0)], late=moves(line_d, "far"))
    landed((0, 0))
    b_pieces = line_b.pieces()
    made, (out_keep, out_give) = slot(
        moves(line_c, "first") + [up(0, 1)],
        lambda normed, bias, tables, pieces: (
            project_more(normed, bias, tables, pieces),
            head_rows(clock.token, pieces),
        ),
        normed,
        b_more,
        tables,
        b_pieces,
    )
    landed((0, 1))
    queries.append(made[0])
    kvs.append([made[1]])

    def first_attention(out_more, g_own, g_more, out_keep, query, bias, kvs):
        grad, heads = context_gradient(clock.token, g_own, g_more, out_keep, out_more)
        return grad, heads, attend(0, query, grad, bias, kvs)

    _, (context_grad, out_heads, found) = slot(
        moves(line_c, "second") + moves(line_d, "near") + [up(1, 0), core_move("out", out_give)],
        chain=(
            "out",
            first_attention,
            (g_own, g_more, out_keep, queries[0], bias, tuple(kvs[0])),
        ),
    )
    results[0] = found
    landed((1, 0))
    c_pieces = line_c.pieces()
    act, act_t, slope = slot(
        moves(line_d, "first") + [up(1, 1), down(0, 0)],
        lambda normed, b_in, pieces: hidden(normed, pieces, b_in),
        normed,
        b_in,
        c_pieces,
        late=[up(2, 0)],
    )
    landed((1, 1))
    work, *given = attention(1)

    def with_units(given, act_t, own, other):
        found = work(given)
        return found, unit_grads(clock.token[0], act_t, own, other), shift(found[0][4], -1)

    (found, fc_parts, backs[1, 0]), moved[2, 1] = slot(
        moves(line_d, "second") + [down(0, 1)],
        with_units,
        *given,
        act_t,
        g_own,
        g_more,
        chain=((2, 0), lambda value: shift(value, 1), ()),
    )
    attended([1], found)
    landed((2, 0), (2, 1))
    d_pieces = line_d.pieces()
    sum_fc = Scatter(fc_parts)
    work2, *given = attention(2)

    def last_attention(given, earlier, own, other):
        found = work2(given)
        contexts = earlier + [found[0][0]]
        return found, contexts, out_grad(clock.token, own, other, contexts)

    found, contexts, (out_keep, out_give) = slot(
        moves(sum_fc, "first") + [down(1, 1)],
        last_attention,
        *given,
        [results[group][0] for group in range(2)],
        g_own,
        g_more,
        then=lambda made: [(backs, (2, 0), made[0][0][4], partial(shift, by=-1))],
    )
    attended([2], found)

    def units_back(out_more, out_keep, normed_t, own, other, slope, pieces):
        hidden_grad, hidden_sum = unit_back(clock.token, own, other, slope, pieces)
        more = jnp.concatenate([out_keep, out_more], axis=0)
        return hidden_grad, hidden_sum, row_grads(clock.token, normed_t, hidden_grad, more)

    _, (hidden_grad, hidden_sum, in_parts) = slot(
        moves(sum_fc, "second") + [core_move("out_grad", out_give)],
        chain=("out_grad", units_back, (out_keep, normed_t, g_own, g_more, slope, d_pieces)),
    )
    sum_in = Scatter(in_parts)
    (out_mine, out_theirs), earlier = slot(
        moves(sum_in, "first") + [down(2, 1)],
        lambda act, heads, contexts, pieces, grad, c_pieces: (
            unit_out(clock.token, act, heads, contexts, pieces),
            norm_grad(grad, [c_pieces], [(0, units)]),
        ),
        act,
        out_heads,
        contexts,
        d_pieces,
        hidden_grad,
        c_pieces,
    )

    def last_grads(normed_t, tables, triples):
        projected_grad, total = unturn(tables, triples)
        return projected_grad, total, row_grads(clock.token, normed_t, projected_grad)

    projected_grad, qkv_bias_sum, parts = slot(
        moves(sum_in, "second") + moves(sum_fc, "near") + [core_move("out_side", out_theirs)],
        last_grads,
        normed_t,
        tables,
        [(results[group][1], results[group][2], backs[group, 1]) for group in range(3)],
    )
    sum_qkv = Scatter(parts)
    norm_mine, norm_theirs = slot(
        moves(sum_qkv, "first") + moves(sum_in, "near") + moves(sum_fc, "far"),
        lambda projected_grad, earlier, *lines: norm_grad(
            projected_grad, lines, [(0, 768), (512, 1280)], earlier
        ),
        projected_grad,
        earlier,
        a_pieces,
        b_pieces,
    )

    def finish_output(x_own, out_mine, out_more, b_rows):
        order = jnp.asarray(np.array(ORDER, np.int32)) ^ me
        spots = place_of(jnp.arange(CHIPS, dtype=jnp.int32) ^ me)
        b_rows = b_rows.reshape(CHIPS, 2 * d_rows)[spots].reshape(1, D)
        return (x_own.astype(F32) + out_mine + out_more + b_rows).astype(BF)

    def small_rows(norm_sums, qkv_bias_sum, hidden_sum, grad_sum):
        spots = place_of(jnp.arange(CHIPS, dtype=jnp.int32) ^ me)
        norm_sums = norm_sums[:2].reshape(2, CHIPS, 2, d_rows)[:, spots].reshape(2, D)
        mine = (jnp.arange(2) == core)[:, None]
        qkv_full = (
            jnp.where(mine, qkv_bias_sum, 0.0)
            .reshape(2, GROUPS, 3, pair, HD)
            .transpose(0, 1, 3, 2, 4)
            .reshape(3 * D)
        )
        in_full = jnp.where(mine[None], hidden_sum.reshape(CHIPS, 1, f_rows), 0.0)
        packed = jnp.concatenate(
            [
                vector.reshape(2 * CHIPS, -1)
                for vector in (norm_sums[0], norm_sums[1], qkv_full, grad_sum, in_full)
            ],
            axis=1,
        ).reshape(CHIPS, -1)
        return packed[jnp.asarray(np.array(ORDER, np.int32)) ^ me]

    def back_work(norm_more, norm_mine, xhat, inv_std, gain, g_own, *sums):
        input_grad, norm_sums = norm_back(
            clock.token, norm_mine, norm_more, xhat, inv_std, gain, g_own
        )
        return input_grad, small_rows(norm_sums, *sums)

    _, (input_grad, packed) = slot(
        moves(sum_qkv, "second") + moves(sum_in, "far") + [core_move("norm", norm_theirs)],
        chain=(
            "norm",
            back_work,
            (norm_mine, xhat, inv_std, gain, g_own, qkv_bias_sum, hidden_sum, grad_sum),
        ),
    )

    def fold(bit):
        return (box, "fold", packed[packed.shape[0] // 2 :], partial(cross, bit=bit))

    def half_sum():
        return packed[: packed.shape[0] // 2] + box["fold"]

    def two_folds(value, rows):
        half = rows[: rows.shape[0] // 2] + value
        give = half[half.shape[0] // 2 :]
        return half[: half.shape[0] // 2] + cross(give, X)

    in_rows = sum_in.result()
    in_keep, in_give = pick(in_rows[:, :units].reshape(2, d_rows, units))
    out_weight_grad = in_rows[:, units:].reshape(2, d_rows, D // 2)
    output, packed = slot(
        moves(sum_qkv, "near") + [fold(Y), core_move("in_rows", in_give)],
        finish_output,
        x_own,
        out_mine,
        box["out_side"],
        b_rows,
        chain=("fold", two_folds, (packed,)),
    )
    fc_in_weight_grad = slot(
        moves(sum_qkv, "far") + [fold(NEAR)],
        lambda mine, other: paste(paste_in_kernel, clock.token, mine, other),
        in_keep,
        box["in_rows"],
    )
    packed = half_sum()
    qkv_keep, qkv_give = pick(sum_qkv.result().reshape(2, d_rows, -1))
    slot([core_move("qkv_rows", qkv_give), fold(FAR)])
    sums_keep, sums_give = pick(half_sum().reshape(2, -1))
    sums = sums_keep + other_core(sums_give)
    parts = []
    first = 0
    for width in (d_rows, d_rows, 3 * d_rows, d_rows, f_rows):
        parts.append(sums[first : first + width])
        first += width
    return (
        output.reshape(local_seqs, tok_count, D),
        input_grad.reshape(local_seqs, tok_count, D),
        parts[0],
        parts[1],
        paste(paste_qkv_kernel, clock.token, qkv_keep, box["qkv_rows"]),
        parts[2],
        jnp.concatenate([out_weight_grad[0], out_weight_grad[1]], axis=1),
        parts[3],
        fc_in_weight_grad,
        parts[4],
        sum_fc.result(),
        parts[3],
    )


def solution(mesh):
    rows = P(("seq", "fsdp"))
    wide = P(("seq", "fsdp"), None)
    act = P("fsdp", "seq", None)
    placed = (act, P("fsdp", "seq"), act) + (rows, rows) + (wide, rows) * 4
    small = dict(mesh.shape) == {"seq": 4, "fsdp": 8}
    return jax.shard_map(
        local_fast if small else local_plain,
        mesh=mesh,
        in_specs=placed,
        out_specs=(act, act, rows, rows) + (wide, rows) * 4,
        check_vma=False,
    )
```

profile of v0, /device:TPU:1, one launch (start us, length us, event | category | flops | bytes accessed | tf_op | source)
XLA Modules:
  0.0 434.2 jit_solution(1032713517828348480)
XLA Ops:
  5.9 3.7 collective-permute-start.1
  11.0 4.3 collective-permute-done.1
  19.1 3.1 collective-permute-start.5
  24.0 3.6 collective-permute-done.5
  35.7 5.0 %marks.1 = (f32[4,768,256]{2,1,0:T(8,128)}, f32[1024,128]{1,0:T(8,128)}, f32[1024,128]{1,0:T(8,128)}, f32[1024,128]{1,0:T(8,128)}) custom-call(s32[2]{0:T(128)} %pad_add_fusion.where_ref, bf16[128,896]{1,0:T(8,128)(2,1)} %copy-done.17, bf16[128,896]{1,0:T(8,128)(2,1)} %copy-done.18, f32[1,128]{1,0:T(1,128)} %bitcast.41, f32[1,128]{1,0:T(1,128)} %constant.130.clone.forth_ref, ...), custom_call_target="tpu_custom_call" | custom-call | flops 13107200 | bytes 4194304 | tf_op jit(solution)/shard_map/marks/pallas_call | solution.py:586
  46.2 9.4 %prepare.1 = (f32[1024,1024]{1,0:T(8,128)}, f32[1024,1]{1,0:T(8,128)}) custom-call(s32[2]{0:T(128)} %pad_add_fusion.where_ref, bf16[512,1024]{1,0:T(8,128)(2,1)} %bitcast.31, bf16[512,1024]{1,0:T(8,128)(2,1)} %collective-permute-done.2.other_ref), custom_call_target="tpu_custom_call" | custom-call | flops 2147483648 | bytes 8388608 | tf_op jit(solution)/shard_map/prepare/pallas_call | solution.py:644
  55.6 4.1 collective-permute-done.13
  64.4 7.9 %project_first.1 = (bf16[1024,128]{1,0:T(8,128)(2,1)}, bf16[1024,256]{1,0:T(8,128)(2,1)}, bf16[1024,128]{1,0:T(8,128)(2,1)}, bf16[1024,256]{1,0:T(8,128)(2,1)}, ...) custom-call(s32[2]{0:T(128)} %pad_add_fusion.where_ref, ...), custom_call_target="tpu_custom_call" | custom-call | flops 1610612736 | bytes 12582912 | tf_op jit(solution)/shard_map/project_first/pallas_call | solution.py:728
  77.2 3.0 collective-permute-start.19
  80.2 9.1 %collective-permute-done.19.refs_1_ = bf16[1024,256]{1,0:T(8,128)(2,1)} collective-permute-done((bf16[1024,256]{1,0:T(8,128)(2,1)}, bf16[1024,256]{1,0:T(8,128)(2,1)}, u32[]{:S(2)}, u32[]{:S(2)}) %collective-permute-start.19) | collective-permute-done | bytes 524320 | tf_op jit(solution)/shard_map/ppermute | solution.py:316
  92.2 3.5 collective-permute-start.22
  101.7 6.4 %project_more.1 = (bf16[1024,256]{1,0:T(8,128)(2,1)}, bf16[1024,512]{1,0:T(8,128)(2,1)}) custom-call(bf16[1024,1024]{1,0:T(8,128)(2,1)} %get-tuple-element.611.normed_ref, f32[1,768]{1,0:T(1,128)} %get-tuple-element.554.bias_ref, f32[1024,128]{1,0:T(8,128)} %get-tuple-element.772.cos_ref, f32[1024,128]{1,0:T(8,128)} %get-tuple-element.773.forth_ref, ...), custom_call_target="tpu_custom_call" | custom-call | flops 1610612736 | bytes 6291456 | tf_op jit(solution)/shard_map/project_more/pallas_call | solution.py:752
  108.1 2.8 collective-permute-done.23
  116.1 2.7 collective-permute-start.28
  118.7 5.9 %collective-permute-start.26 = (bf16[256,1024]{1,0:T(8,128)(2,1)}, bf16[256,1024]{1,0:T(8,128)(2,1)S(1)}, u32[]{:S(2)}, u32[]{:S(2)}) collective-permute-start(bf16[256,1024]{1,0:T(8,128)(2,1)} %get-tuple-element.607), channel_id=1, source_target_pairs={{0,8},{8,0},{16,24},{24,16},{1,9},{9,1},{17,25},{25,17},{2,10},{10... | collective-permute-start | bytes 1572872 | tf_op jit(solution)/shard_map/ppermute | solution.py:311
  124.6 2.7 collective-permute-start.27
  128.1 5.1 %context_grad.1 = (bf16[1024,512]{1,0:T(8,128)(2,1)}, bf16[512,1024]{1,0:T(8,128)(2,1)}) custom-call(s32[2]{0:T(128)} %pad_add_fusion.where_ref, bf16[512,1024]{1,0:T(8,128)(2,1)} %bitcast.24, bf16[512,1024]{1,0:T(8,128)(2,1)} %copy-done.15, bf16[256,1024]{1,0:T(8,128)(2,1)} %get-tuple-element.586.keep_ref, bf16[256,1024]{1,0:T(8,128)(2,1)} %copy-done.60), custom_call_target="tpu_custom_call" | custom-call | flops 1073741824 | bytes 6291456 | tf_op jit(solution)/shard_map/context_grad/pallas_call | solution.py:818
  133.2 9.0 %attend.3 = (bf16[1024,128]{1,0:T(8,128)(2,1)}, bf16[1024,128]{1,0:T(8,128)(2,1)}, f32[1024,256]{1,0:T(8,128)}, bf16[1024,256]{1,0:T(8,128)(2,1)}, bf16[1024,256]{1,0:T(8,128)(2,1)}) custom-call(bf16[1024,128]{1,0:T(8,128)(2,1)} %get-tuple-element.589.q_ref, bf16[1024,512]{1,0:T(8,128)(2,1)} %get-tuple-element.670.do_ref, ...), custom_call_target="tpu_custom_call" | custom-call | flops 2415919104 | bytes 9437184 | tf_op jit(solution)/shard_map/attend/pallas_call | solution.py:900
  142.2 5.2 %collective-permute-done.27.refs_1_ = bf16[1024,256]{1,0:T(8,128)(2,1)} collective-permute-done((bf16[1024,256]{1,0:T(8,128)(2,1)}, bf16[1024,256]{1,0:T(8,128)(2,1)}, u32[]{:S(2)}, u32[]{:S(2)}) %collective-permute-start.27) | collective-permute-done | bytes 524320 | tf_op jit(solution)/shard_map/ppermute | solution.py:316
  148.5 4.9 %collective-permute-start.31 = (bf16[1024,256]{1,0:T(8,128)(2,1)}, bf16[1024,256]{1,0:T(8,128)(2,1)}, u32[]{:S(2)}, u32[]{:S(2)}) collective-permute-start(bf16[1024,256]{1,0:T(8,128)(2,1)} %collective-permute-done.27.refs_1_), channel_id=1, source_target_pairs={{0,8},{8,16},{16,24},{1,9},{9,17},{17,25},{2,10},{10,18},{18,26},{... | collective-permute-start | bytes 1572872 | tf_op jit(solution)/shard_map/ppermute | solution.py:316
  154.6 5.0 %collective-permute-start.36 = (bf16[1024,512]{1,0:T(8,128)(2,1)}, bf16[1024,512]{1,0:T(8,128)(2,1)}, u32[]{:S(2)}, u32[]{:S(2)}) collective-permute-start(bf16[1024,512]{1,0:T(8,128)(2,1)} %get-tuple-element.672.refs_0_), channel_id=1, source_target_pairs={{0,8},{8,16},{16,24},{1,9},{9,17},{17,25},{2,10},{10,18},{18,26},{... | collective-permute-start | bytes 3145736 | tf_op jit(solution)/shard_map/ppermute | solution.py:316
  159.6 15.0 %hidden.1 = (bf16[1024,2048]{1,0:T(8,128)(2,1)}, bf16[2048,1024]{1,0:T(8,128)(2,1)}, f32[1024,2048]{1,0:T(8,128)}) custom-call(bf16[1024,1024]{1,0:T(8,128)(2,1)} %get-tuple-element.611.normed_ref, f32[1,2048]{1,0:T(1,128)} %get-tuple-element.612.bias_ref, bf16[256,2048]{1,0:T(8,128)(2,1)} %copy-done.12, bf16[256,2048]{1,0:T(8,128)(2,1)} %copy-done.48, ...), custom_call_target="tpu_custom_call" | custom-call | flops 4399824896 | bytes 18874368 | tf_op jit(solution)/shard_map/hidden/pallas_call | solution.py:1000
  178.0 7.2 %collective-permute-done.36.refs_1_ = bf16[1024,512]{1,0:T(8,128)(2,1)} collective-permute-done((bf16[1024,512]{1,0:T(8,128)(2,1)}, bf16[1024,512]{1,0:T(8,128)(2,1)}, u32[]{:S(2)}, u32[]{:S(2)}) %collective-permute-start.36) | collective-permute-done | bytes 1048608 | tf_op jit(solution)/shard_map/ppermute | solution.py:316
  185.2 5.1 %collective-permute-start.38 = (bf16[1024,512]{1,0:T(8,128)(2,1)}, bf16[1024,512]{1,0:T(8,128)(2,1)}, u32[]{:S(2)}, u32[]{:S(2)}) collective-permute-start(bf16[1024,512]{1,0:T(8,128)(2,1)} %collective-permute-done.36.refs_1_), channel_id=1, source_target_pairs={{0,8},{8,16},{16,24},{1,9},{9,17},{17,25},{2,10},{10,18},{18,26},{... | collective-permute-start | bytes 3145736 | tf_op jit(solution)/shard_map/ppermute | solution.py:316
  190.3 9.1 %attend.4 = (bf16[1024,128]{1,0:T(8,128)(2,1)}, bf16[1024,128]{1,0:T(8,128)(2,1)}, f32[1024,256]{1,0:T(8,128)}, bf16[1024,256]{1,0:T(8,128)(2,1)}, bf16[1024,256]{1,0:T(8,128)(2,1)}) custom-call(bf16[1024,128]{1,0:T(8,128)(2,1)} %get-tuple-element.634.q_ref, bf16[1024,512]{1,0:T(8,128)(2,1)} %get-tuple-element.670.do_ref, ...), custom_call_target="tpu_custom_call" | custom-call | flops 2415919104 | bytes 9437184 | tf_op jit(solution)/shard_map/attend/pallas_call | solution.py:900
  202.5 11.6 %unit_grads.1 = (bf16[256,1024]{1,0:T(8,128)(2,1)}, bf16[256,1024]{1,0:T(8,128)(2,1)}, bf16[256,1024]{1,0:T(8,128)(2,1)}, bf16[256,1024]{1,0:T(8,128)(2,1)}, bf1...) custom-call(s32[16]{0:T(128)} %broadcast_xor_fusion.order_ref, ...), custom_call_target="tpu_custom_call" | custom-call | flops 4294967296 | bytes 8388608 | tf_op jit(solution)/shard_map/unit_grads/pallas_call | solution.py:1192
  214.1 9.5 %collective-permute-done.35.refs_2_ = bf16[1024,256]{1,0:T(8,128)(2,1)S(1)} collective-permute-done((bf16[1024,256]{1,0:T(8,128)(2,1)S(1)}, bf16[1024,256]{1,0:T(8,128)(2,1)S(1)}, u32[]{:S(2)}, u32[]{:S(2)}) %collective-permute-start.35) | collective-permute-done | bytes 524320 | tf_op jit(solution)/shard_map/ppermute | solution.py:316
  227.8 16.3 %attend.5 = (bf16[1024,256]{1,0:T(8,128)(2,1)}, bf16[1024,256]{1,0:T(8,128)(2,1)}, f32[1024,512]{1,0:T(8,128)}, bf16[1024,512]{1,0:T(8,128)(2,1)}, bf16[1024,512]{1,0:T(8,128)(2,1)}) custom-call(bf16[1024,256]{1,0:T(8,128)(2,1)} %get-tuple-element.669.q_ref, bf16[1024,512]{1,0:T(8,128)(2,1)} %get-tuple-element.670.do_ref, ...), custom_call_target="tpu_custom_call" | custom-call | flops 4831838208 | bytes 18874368 | tf_op jit(solution)/shard_map/attend/pallas_call | solution.py:900
  244.1 5.0 %out_grad.1 = (bf16[256,1024]{1,0:T(8,128)(2,1)}, bf16[256,1024]{1,0:T(8,128)(2,1)}) custom-call(s32[2]{0:T(128)} %pad_add_fusion.where_ref, bf16[512,1024]{1,0:T(8,128)(2,1)} %bitcast.26, bf16[512,1024]{1,0:T(8,128)(2,1)} %copy-done.15, bf16[1024,128]{1,0:T(8,128)(2,1)} %get-tuple-element.736.refs_0_, bf16[1024,128]{1,0:T(8,128)(2,1)} %get-tuple-element.737.refs_1_, ...), custom_call_target="tpu_custom_call" | custom-call | flops 1073741824 | bytes 6291456 | tf_op jit(solution)/shard_map/out_grad/pallas_call | solution.py:1234
  249.2 3.4 add_convert_fusion.6
  252.6 4.0 collective-permute-start.44
  258.9 11.6 %unit_back.1 = (bf16[1024,2048]{1,0:T(8,128)(2,1)}, f32[1,2048]{1,0:T(1,128)}) custom-call(s32[2]{0:T(128)} %pad_add_fusion.where_ref, bf16[512,1024]{1,0:T(8,128)(2,1)} %bitcast.27, bf16[512,1024]{1,0:T(8,128)(2,1)} %copy-done.15, f32[1024,2048]{1,0:T(8,128)} %get-tuple-element.703.slope_ref, ...), custom_call_target="tpu_custom_call" | custom-call | flops 4294967296 | bytes 16777216 | tf_op jit(solution)/shard_map/unit_back/pallas_call | solution.py:1056
  272.9 9.2 %row_grads.2 = (bf16[128,2560]{1,0:T(8,128)(2,1)}, bf16[128,2560]{1,0:T(8,128)(2,1)}, bf16[128,2560]{1,0:T(8,128)(2,1)}, bf16[128,2560]{1,0:T(8,128)(2,1)}, bf16...) custom-call(s32[2]{0:T(128)} %pad_add_fusion.where_ref, bf16[1024,1024]{1,0:T(8,128)(2,1)} %get-tuple-element.787.left_ref, ...), custom_call_target="tpu_custom_call" | custom-call | flops 5368709120 | bytes 7340032 | tf_op jit(solution)/shard_map/row_grads/pallas_call | solution.py:1145
  290.2 9.6 %norm_grad.2 = (f32[512,1024]{1,0:T(8,128)}, f32[512,1024]{1,0:T(8,128)}) custom-call(bf16[1024,2048]{1,0:T(8,128)(2,1)} %get-tuple-element.745.right_ref.left_ref, bf16[256,2048]{1,0:T(8,128)(2,1)} %copy-done.12, bf16[256,2048]{1,0:T(8,128)(2,1)} %copy-done.48, bf16[256,2048]{1,0:T(8,128)(2,1)} %collective-permute-done.24.refs_2_, ...), custom_call_target="tpu_custom_call" | custom-call | flops 4294967296 | bytes 12582912 | tf_op jit(solution)/shard_map/norm_grad/pallas_call | solution.py:1283
  299.8 11.8 %unit_out.1 = (f32[512,1024]{1,0:T(8,128)}, f32[512,1024]{1,0:T(8,128)}) custom-call(s32[2]{0:T(128)} %pad_add_fusion.where_ref, bf16[1024,2048]{1,0:T(8,128)(2,1)} %get-tuple-element.734.act_ref, bf16[512,1024]{1,0:T(8,128)(2,1)} %get-tuple-element.735.heads_ref, bf16[1024,128]{1,0:T(8,128)(2,1)} %get-tuple-element.736.refs_0_, ...), custom_call_target="tpu_custom_call" | custom-call | flops 6442450944 | bytes 12582912 | tf_op jit(solution)/shard_map/unit_out/pallas_call | solution.py:1092
  313.5 3.1 collective-permute-done.46
  323.4 6.5 %unturn.1 = (bf16[1024,1536]{1,0:T(8,128)(2,1)}, f32[1,1536]{1,0:T(1,128)}) custom-call(f32[1024,128]{1,0:T(8,128)} %get-tuple-element.772.cos_ref, f32[1024,128]{1,0:T(8,128)} %get-tuple-element.773.forth_ref, f32[1024,128]{1,0:T(8,128)} %get-tuple-element.774.back_ref, bf16[1024,128]{1,0:T(8,128)(2,1)} %get-tuple-element.775.refs_0_, ...), custom_call_target="tpu_custom_call" | custom-call | flops 15728640 | bytes 12582912 | tf_op jit(solution)/shard_map/unturn/pallas_call | solution.py:956
  330.0 7.1 %row_grads.3 = (bf16[128,1536]{1,0:T(8,128)(2,1)}, bf16[128,1536]{1,0:T(8,128)(2,1)}, bf16[128,1536]{1,0:T(8,128)(2,1)}, bf16[128,1536]{1,0:T(8,128)(2,1)}, bf16...) custom-call(s32[2]{0:T(128)} %pad_add_fusion.where_ref, bf16[1024,1024]{1,0:T(8,128)(2,1)} %get-tuple-element.787.left_ref, ...), custom_call_target="tpu_custom_call" | custom-call | flops 3221225472 | bytes 5242880 | tf_op jit(solution)/shard_map/row_grads/pallas_call | solution.py:1145
  337.4 3.1 add_convert_fusion.2
  347.2 9.7 %norm_grad.3 = (f32[512,1024]{1,0:T(8,128)}, f32[512,1024]{1,0:T(8,128)}) custom-call(bf16[1024,1536]{1,0:T(8,128)(2,1)} %get-tuple-element.810.right_ref.left_ref, bf16[256,896]{1,0:T(8,128)(2,1)} %copy-done.8, bf16[256,896]{1,0:T(8,128)(2,1)} %copy-done.16, bf16[256,896]{1,0:T(8,128)(2,1)} %copy-done.44, bf16[256,896]{1,0:T(8,128)(2,1)} %collective-permute-done.12.refs_3_, ...), custom_call_target="tpu_custom_call" | custom-call | flops 3221225472 | bytes 12582912 | tf_op jit(solution)/shard_map/norm_grad/pallas_call | solution.py:1283
  356.9 7.0 %collective-permute-done.56 = bf16[128,1024]{1,0:T(8,128)(2,1)} collective-permute-done((bf16[128,1024]{1,0:T(8,128)(2,1)}, bf16[128,1024]{1,0:T(8,128)(2,1)}, u32[]{:S(2)}, u32[]{:S(2)}) %collective-permute-start.56) | collective-permute-done | bytes 262176 | tf_op jit(solution)/shard_map/ppermute | solution.py:311
  370.2 2.6 collective-permute-start.60
  378.1 7.2 %norm_back.1 = (bf16[512,1024]{1,0:T(8,128)(2,1)}, f32[8,1024]{1,0:T(8,128)}) custom-call(s32[2]{0:T(128)} %pad_add_fusion.where_ref, f32[512,1024]{1,0:T(8,128)} %get-tuple-element.844.part_ref, f32[512,1024]{1,0:T(8,128)} %copy-done.7, f32[1024,1024]{1,0:T(8,128)} %get-tuple-element.845.xhat_ref, f32[1024,1]{1,0:T(8,128)} %get-tuple-element.846.inv_ref, ...), custom_call_target="tpu_custom_call" | custom-call | flops 2147483648 | bytes 8388608 | tf_op jit(solution)/shard_map/norm_back/pallas_call | solution.py:1324
  388.2 3.1 collective-permute-done.59
  402.9 3.4 add_convert_fusion
  409.7 3.1 collective-permute-start.65
  417.9 3.5 collective-permute-done.65
  424.7 3.3 collective-permute-done.68
  (334 shorter events, 135.2 us)
Async XLA Ops:
  44.7 15.1 %collective-permute-start.11 = (bf16[256,896]{1,0:T(8,128)(2,1)S(1)}, bf16[256,896]{1,0:T(8,128)(2,1)S(1)}, u32[]{:S(2)}, u32[]{:S(2)}) collective-permute-start(bf16[256,896]{1,0:T(8,128)(2,1)S(1)} %pad_maximum_fusion.4.refs_0_), channel_id=1, source_target_pairs={{0,4},{1,5},{2,6},{3,7},{4,0},{5,1},{6,2},{7,3},{8,12},{9,13},{10,... | collective-permute-start | bytes 1376264 | tf_op jit(solution)/shard_map/ppermute | solution.py:311
  45.0 14.8 %collective-permute-start.12 = (bf16[256,896]{1,0:T(8,128)(2,1)S(1)}, bf16[256,896]{1,0:T(8,128)(2,1)}, u32[]{:S(2)}, u32[]{:S(2)}) collective-permute-start(bf16[256,896]{1,0:T(8,128)(2,1)S(1)} %constant_dynamic-update-slice_fusion.refs_1_), channel_id=1, source_target_pairs={{0,2},{1,3},{2,0},{3,1},{4,6},{5,7},{6,4},{7,5},{8,10},{9,11},{10,... | collective-permute-start | bytes 1376264 | tf_op jit(solution)/shard_map/ppermute | solution.py:311
  45.8 14.0 %collective-permute-start.13 = (bf16[64,2048]{1,0:T(8,128)(2,1)}, bf16[64,2048]{1,0:T(8,128)(2,1)S(1)}, u32[]{:S(2)}, u32[]{:S(2)}) collective-permute-start(bf16[64,2048]{1,0:T(8,128)(2,1)} %pad_maximum_fusion.6), channel_id=1, source_target_pairs={{0,16},{8,24},{16,0},{24,8},{1,17},{9,25},{17,1},{25,9},{2,18},{10... | collective-permute-start | bytes 786440 | tf_op jit(solution)/shard_map/ppermute | solution.py:311
  60.6 12.1 %collective-permute-start.16 = (bf16[128,2048]{1,0:T(8,128)(2,1)S(1)}, bf16[128,2048]{1,0:T(8,128)(2,1)S(1)}, u32[]{:S(2)}, u32[]{:S(2)}) collective-permute-start(bf16[128,2048]{1,0:T(8,128)(2,1)S(1)} %pad_maximum_fusion.3), channel_id=1, source_target_pairs={{0,8},{8,0},{16,24},{24,16},{1,9},{9,1},{17,25},{25,17},{2,10},{10... | collective-permute-start | bytes 1572872 | tf_op jit(solution)/shard_map/ppermute | solution.py:311
  60.7 11.6 %collective-permute-start.14 = (bf16[128,1280]{1,0:T(8,128)(2,1)}, bf16[128,1280]{1,0:T(8,128)(2,1)S(1)}, u32[]{:S(2)}, u32[]{:S(2)}) collective-permute-start(bf16[128,1280]{1,0:T(8,128)(2,1)} %pad_maximum_fusion.5), channel_id=1, source_target_pairs={{0,2},{1,3},{2,0},{3,1},{4,6},{5,7},{6,4},{7,5},{8,10},{9,11},{10,... | collective-permute-start | bytes 983048 | tf_op jit(solution)/shard_map/ppermute | solution.py:311
  73.5 15.8 %collective-permute-start.17 = (bf16[256,1280]{1,0:T(8,128)(2,1)S(1)}, bf16[256,1280]{1,0:T(8,128)(2,1)S(1)}, u32[]{:S(2)}, u32[]{:S(2)}) collective-permute-start(bf16[256,1280]{1,0:T(8,128)(2,1)S(1)} %pad_maximum_fusion.2.refs_0_.refs_4_), channel_id=1, source_target_pairs={{0,4},{1,5},{2,6},{3,7},{4,0},{5,1},{6,2},{7,3},{8,12},{9,13},{10,... | collective-permute-start | bytes 1966088 | tf_op jit(solution)/shard_map/ppermute | solution.py:311
  75.3 14.9 %collective-permute-start.18 = (bf16[256,1280]{1,0:T(8,128)(2,1)S(1)}, bf16[256,1280]{1,0:T(8,128)(2,1)S(1)}, u32[]{:S(2)}, u32[]{:S(2)}) collective-permute-start(bf16[256,1280]{1,0:T(8,128)(2,1)S(1)} %constant_dynamic-update-slice_fusion.2.refs_1_.refs_5_), channel_id=1, source_target_pairs={{0,2},{1,3},{2,0},{3,1},{4,6},{5,7},{6,4},{7,5},{8,10},{9,11},{10,... | collective-permute-start | bytes 1966088 | tf_op jit(solution)/shard_map/ppermute | solution.py:311
  77.2 12.2 %collective-permute-start.19 = (bf16[1024,256]{1,0:T(8,128)(2,1)}, bf16[1024,256]{1,0:T(8,128)(2,1)}, u32[]{:S(2)}, u32[]{:S(2)}) collective-permute-start(bf16[1024,256]{1,0:T(8,128)(2,1)} %get-tuple-element.591.refs_0_), channel_id=1, source_target_pairs={{0,8},{8,16},{16,24},{1,9},{9,17},{17,25},{2,10},{10,18},{18,26},{... | collective-permute-start | bytes 1572872 | tf_op jit(solution)/shard_map/ppermute | solution.py:316
  90.2 20.7 %collective-permute-start.20 = (bf16[128,2048]{1,0:T(8,128)(2,1)}, bf16[128,2048]{1,0:T(8,128)(2,1)}, u32[]{:S(2)}, u32[]{:S(2)}) collective-permute-start(bf16[128,2048]{1,0:T(8,128)(2,1)} %copy-done.40), channel_id=1, source_target_pairs={{0,2},{1,3},{2,0},{3,1},{4,6},{5,7},{6,4},{7,5},{8,10},{9,11},{10,... | collective-permute-start | bytes 1572872 | tf_op jit(solution)/shard_map/ppermute | solution.py:311
  91.8 19.2 %collective-permute-start.21 = (bf16[128,2048]{1,0:T(8,128)(2,1)}, bf16[128,2048]{1,0:T(8,128)(2,1)}, u32[]{:S(2)}, u32[]{:S(2)}) collective-permute-start(bf16[128,2048]{1,0:T(8,128)(2,1)} %copy-done.41), channel_id=1, source_target_pairs={{0,4},{1,5},{2,6},{3,7},{4,0},{5,1},{6,2},{7,3},{8,12},{9,13},{10,... | collective-permute-start | bytes 1572872 | tf_op jit(solution)/shard_map/ppermute | solution.py:311
  92.2 18.8 %collective-permute-start.22 = (bf16[1024,256]{1,0:T(8,128)(2,1)}, bf16[1024,256]{1,0:T(8,128)(2,1)}, u32[]{:S(2)}, u32[]{:S(2)}) collective-permute-start(bf16[1024,256]{1,0:T(8,128)(2,1)} %collective-permute-done.19.refs_1_), channel_id=1, source_target_pairs={{0,8},{8,16},{16,24},{1,9},{9,17},{17,25},{2,10},{10,18},{18,26},{... | collective-permute-start | bytes 1572872 | tf_op jit(solution)/shard_map/ppermute | solution.py:316
  97.4 13.5 %collective-permute-start.23 = (bf16[128,1024]{1,0:T(8,128)(2,1)}, bf16[128,1024]{1,0:T(8,128)(2,1)S(1)}, u32[]{:S(2)}, u32[]{:S(2)}) collective-permute-start(bf16[128,1024]{1,0:T(8,128)(2,1)} %param.28), channel_id=1, source_target_pairs={{0,16},{8,24},{16,0},{24,8},{1,17},{9,25},{17,1},{25,9},{2,18},{10... | collective-permute-start | bytes 786440 | tf_op jit(solution)/shard_map/ppermute | solution.py:311
  114.6 32.9 %collective-permute-start.24 = (bf16[256,2048]{1,0:T(8,128)(2,1)S(1)}, bf16[256,2048]{1,0:T(8,128)(2,1)}, u32[]{:S(2)}, u32[]{:S(2)}) collective-permute-start(bf16[256,2048]{1,0:T(8,128)(2,1)S(1)} %pad_maximum_fusion.refs_0_), channel_id=1, source_target_pairs={{0,4},{1,5},{2,6},{3,7},{4,0},{5,1},{6,2},{7,3},{8,12},{9,13},{10,... | collective-permute-start | bytes 3145736 | tf_op jit(solution)/shard_map/ppermute | solution.py:311
  115.8 31.7 %collective-permute-start.25 = (bf16[256,2048]{1,0:T(8,128)(2,1)S(1)}, bf16[256,2048]{1,0:T(8,128)(2,1)}, u32[]{:S(2)}, u32[]{:S(2)}) collective-permute-start(bf16[256,2048]{1,0:T(8,128)(2,1)S(1)} %constant_dynamic-update-slice_fusion.6.refs_1_), channel_id=1, source_target_pairs={{0,2},{1,3},{2,0},{3,1},{4,6},{5,7},{6,4},{7,5},{8,10},{9,11},{10,... | collective-permute-start | bytes 3145736 | tf_op jit(solution)/shard_map/ppermute | solution.py:311
  118.7 23.5 %collective-permute-start.26 = (bf16[256,1024]{1,0:T(8,128)(2,1)}, bf16[256,1024]{1,0:T(8,128)(2,1)S(1)}, u32[]{:S(2)}, u32[]{:S(2)}) collective-permute-start(bf16[256,1024]{1,0:T(8,128)(2,1)} %get-tuple-element.607), channel_id=1, source_target_pairs={{0,8},{8,0},{16,24},{24,16},{1,9},{9,1},{17,25},{25,17},{2,10},{10... | collective-permute-start | bytes 1572872 | tf_op jit(solution)/shard_map/ppermute | solution.py:311
  124.6 22.9 %collective-permute-start.27 = (bf16[1024,256]{1,0:T(8,128)(2,1)}, bf16[1024,256]{1,0:T(8,128)(2,1)}, u32[]{:S(2)}, u32[]{:S(2)}) collective-permute-start(bf16[1024,256]{1,0:T(8,128)(2,1)} %get-tuple-element.637.refs_0_), channel_id=1, source_target_pairs={{0,8},{8,16},{16,24},{1,9},{9,17},{17,25},{2,10},{10,18},{18,26},{... | collective-permute-start | bytes 1572872 | tf_op jit(solution)/shard_map/ppermute | solution.py:316
  147.5 27.2 %collective-permute-start.29 = (bf16[256,1024]{1,0:T(8,128)(2,1)}, bf16[256,1024]{1,0:T(8,128)(2,1)S(1)}, u32[]{:S(2)}, u32[]{:S(2)}) collective-permute-start(bf16[256,1024]{1,0:T(8,128)(2,1)} %get-tuple-element.607), channel_id=1, source_target_pairs={{0,2},{1,3},{2,0},{3,1},{4,6},{5,7},{6,4},{7,5},{8,10},{9,11},{10,... | collective-permute-start | bytes 1572872 | tf_op jit(solution)/shard_map/ppermute | solution.py:311
  148.1 26.5 %collective-permute-start.30 = (bf16[256,1024]{1,0:T(8,128)(2,1)S(1)}, bf16[256,1024]{1,0:T(8,128)(2,1)S(1)}, u32[]{:S(2)}, u32[]{:S(2)}) collective-permute-start(bf16[256,1024]{1,0:T(8,128)(2,1)S(1)} %collective-permute-done.26), channel_id=1, source_target_pairs={{0,4},{1,5},{2,6},{3,7},{4,0},{5,1},{6,2},{7,3},{8,12},{9,13},{10,... | collective-permute-start | bytes 1572872 | tf_op jit(solution)/shard_map/ppermute | solution.py:311
  148.5 26.2 %collective-permute-start.31 = (bf16[1024,256]{1,0:T(8,128)(2,1)}, bf16[1024,256]{1,0:T(8,128)(2,1)}, u32[]{:S(2)}, u32[]{:S(2)}) collective-permute-start(bf16[1024,256]{1,0:T(8,128)(2,1)} %collective-permute-done.27.refs_1_), channel_id=1, source_target_pairs={{0,8},{8,16},{16,24},{1,9},{9,17},{17,25},{2,10},{10,18},{18,26},{... | collective-permute-start | bytes 1572872 | tf_op jit(solution)/shard_map/ppermute | solution.py:316
  153.3 21.3 %collective-permute-start.32 = (bf16[1024,256]{1,0:T(8,128)(2,1)}, bf16[1024,256]{1,0:T(8,128)(2,1)S(1)}, u32[]{:S(2)}, u32[]{:S(2)}) collective-permute-start(bf16[1024,256]{1,0:T(8,128)(2,1)} %get-tuple-element.610), channel_id=1, source_target_pairs={{8,0},{16,8},{24,16},{9,1},{17,9},{25,17},{10,2},{18,10},{26,18},{... | collective-permute-start | bytes 1572872 | tf_op jit(solution)/shard_map/ppermute | solution.py:316
  154.6 30.6 %collective-permute-start.36 = (bf16[1024,512]{1,0:T(8,128)(2,1)}, bf16[1024,512]{1,0:T(8,128)(2,1)}, u32[]{:S(2)}, u32[]{:S(2)}) collective-permute-start(bf16[1024,512]{1,0:T(8,128)(2,1)} %get-tuple-element.672.refs_0_), channel_id=1, source_target_pairs={{0,8},{8,16},{16,24},{1,9},{9,17},{17,25},{2,10},{10,18},{18,26},{... | collective-permute-start | bytes 3145736 | tf_op jit(solution)/shard_map/ppermute | solution.py:316
  176.0 47.6 %collective-permute-start.33 = (bf16[512,1024]{1,0:T(8,128)(2,1)}, bf16[512,1024]{1,0:T(8,128)(2,1)}, u32[]{:S(2)}, u32[]{:S(2)}) collective-permute-start(bf16[512,1024]{1,0:T(8,128)(2,1)} %constant_dynamic-update-slice_fusion.8.refs_0_.refs_3_), channel_id=1, source_target_pairs={{0,4},{1,5},{2,6},{3,7},{4,0},{5,1},{6,2},{7,3},{8,12},{9,13},{10,... | collective-permute-start | bytes 3145736 | tf_op jit(solution)/shard_map/ppermute | solution.py:311
  177.2 46.4 %collective-permute-start.34 = (bf16[512,1024]{1,0:T(8,128)(2,1)S(1)}, bf16[512,1024]{1,0:T(8,128)(2,1)}, u32[]{:S(2)}, u32[]{:S(2)}) collective-permute-start(bf16[512,1024]{1,0:T(8,128)(2,1)S(1)} %constant_dynamic-update-slice_fusion.11.refs_1_.refs_4_), channel_id=1, source_target_pairs={{0,2},{1,3},{2,0},{3,1},{4,6},{5,7},{6,4},{7,5},{8,10},{9,11},{10,... | collective-permute-start | bytes 3145736 | tf_op jit(solution)/shard_map/ppermute | solution.py:311
  185.2 38.4 %collective-permute-start.38 = (bf16[1024,512]{1,0:T(8,128)(2,1)}, bf16[1024,512]{1,0:T(8,128)(2,1)}, u32[]{:S(2)}, u32[]{:S(2)}) collective-permute-start(bf16[1024,512]{1,0:T(8,128)(2,1)} %collective-permute-done.36.refs_1_), channel_id=1, source_target_pairs={{0,8},{8,16},{16,24},{1,9},{9,17},{17,25},{2,10},{10,18},{18,26},{... | collective-permute-start | bytes 3145736 | tf_op jit(solution)/shard_map/ppermute | solution.py:316
  199.4 14.7 %collective-permute-start.37 = (bf16[1024,256]{1,0:T(8,128)(2,1)}, bf16[1024,256]{1,0:T(8,128)(2,1)S(1)}, u32[]{:S(2)}, u32[]{:S(2)}) collective-permute-start(bf16[1024,256]{1,0:T(8,128)(2,1)} %get-tuple-element.644), channel_id=1, source_target_pairs={{8,0},{16,8},{24,16},{9,1},{17,9},{25,17},{10,2},{18,10},{26,18},{... | collective-permute-start | bytes 1572872 | tf_op jit(solution)/shard_map/ppermute | solution.py:316
  200.7 22.9 %collective-permute-start.35 = (bf16[1024,256]{1,0:T(8,128)(2,1)S(1)}, bf16[1024,256]{1,0:T(8,128)(2,1)S(1)}, u32[]{:S(2)}, u32[]{:S(2)}) collective-permute-start(bf16[1024,256]{1,0:T(8,128)(2,1)S(1)} %add_convert_fusion.9), channel_id=1, source_target_pairs={{8,0},{16,8},{24,16},{9,1},{17,9},{25,17},{10,2},{18,10},{26,18},{... | collective-permute-start | bytes 1572872 | tf_op jit(solution)/shard_map/ppermute | solution.py:316
  224.5 24.6 %collective-permute-start.39 = (bf16[512,1024]{1,0:T(8,128)(2,1)}, bf16[512,1024]{1,0:T(8,128)(2,1)S(1)}, u32[]{:S(2)}, u32[]{:S(2)}) collective-permute-start(bf16[512,1024]{1,0:T(8,128)(2,1)} %get-tuple-element.666), channel_id=1, source_target_pairs={{0,4},{1,5},{2,6},{3,7},{4,0},{5,1},{6,2},{7,3},{8,12},{9,13},{10,... | collective-permute-start | bytes 3145736 | tf_op jit(solution)/shard_map/ppermute | solution.py:311
  225.7 23.4 %collective-permute-start.40 = (bf16[512,1024]{1,0:T(8,128)(2,1)}, bf16[512,1024]{1,0:T(8,128)(2,1)S(1)}, u32[]{:S(2)}, u32[]{:S(2)}) collective-permute-start(bf16[512,1024]{1,0:T(8,128)(2,1)} %get-tuple-element.667), channel_id=1, source_target_pairs={{0,2},{1,3},{2,0},{3,1},{4,6},{5,7},{6,4},{7,5},{8,10},{9,11},{10,... | collective-permute-start | bytes 3145736 | tf_op jit(solution)/shard_map/ppermute | solution.py:311
  226.5 22.6 %collective-permute-start.41 = (bf16[1024,256]{1,0:T(8,128)(2,1)S(1)}, bf16[1024,256]{1,0:T(8,128)(2,1)S(1)}, u32[]{:S(2)}, u32[]{:S(2)}) collective-permute-start(bf16[1024,256]{1,0:T(8,128)(2,1)S(1)} %add_convert_fusion.8), channel_id=1, source_target_pairs={{8,0},{16,8},{24,16},{9,1},{17,9},{25,17},{10,2},{18,10},{26,18},{... | collective-permute-start | bytes 1572872 | tf_op jit(solution)/shard_map/ppermute | solution.py:316
  252.6 18.0 %collective-permute-start.44 = (bf16[256,1024]{1,0:T(8,128)(2,1)}, bf16[256,1024]{1,0:T(8,128)(2,1)}, u32[]{:S(2)}, u32[]{:S(2)}) collective-permute-start(bf16[256,1024]{1,0:T(8,128)(2,1)} %get-tuple-element.699), channel_id=1, source_target_pairs={{0,1},{1,0},{2,3},{3,2},{4,5},{5,4},{6,7},{7,6},{8,9},{9,8},{10,11... | collective-permute-start | bytes 1572872 | tf_op jit(solution)/shard_map/ppermute | solution.py:311
  256.6 28.0 %collective-permute-start.45 = (bf16[1024,512]{1,0:T(8,128)(2,1)}, bf16[1024,512]{1,0:T(8,128)(2,1)S(1)}, u32[]{:S(2)}, u32[]{:S(2)}) collective-permute-start(bf16[1024,512]{1,0:T(8,128)(2,1)} %get-tuple-element.679), channel_id=1, source_target_pairs={{8,0},{16,8},{24,16},{9,1},{17,9},{25,17},{10,2},{18,10},{26,18},{... | collective-permute-start | bytes 3145736 | tf_op jit(solution)/shard_map/ppermute | solution.py:316
  257.9 26.7 %collective-permute-start.42 = (bf16[256,1024]{1,0:T(8,128)(2,1)}, bf16[256,1024]{1,0:T(8,128)(2,1)S(1)}, u32[]{:S(2)}, u32[]{:S(2)}) collective-permute-start(bf16[256,1024]{1,0:T(8,128)(2,1)} %get-tuple-element.697), channel_id=1, source_target_pairs={{0,2},{1,3},{2,0},{3,1},{4,6},{5,7},{6,4},{7,5},{8,10},{9,11},{10,... | collective-permute-start | bytes 1572872 | tf_op jit(solution)/shard_map/ppermute | solution.py:311
  258.6 26.0 %collective-permute-start.43 = (bf16[256,1024]{1,0:T(8,128)(2,1)}, bf16[256,1024]{1,0:T(8,128)(2,1)S(1)}, u32[]{:S(2)}, u32[]{:S(2)}) collective-permute-start(bf16[256,1024]{1,0:T(8,128)(2,1)} %get-tuple-element.698), channel_id=1, source_target_pairs={{0,4},{1,5},{2,6},{3,7},{4,0},{5,1},{6,2},{7,3},{8,12},{9,13},{10,... | collective-permute-start | bytes 1572872 | tf_op jit(solution)/shard_map/ppermute | solution.py:311
  286.7 29.9 %collective-permute-start.46 = (bf16[256,2560]{1,0:T(8,128)(2,1)}, bf16[256,2560]{1,0:T(8,128)(2,1)S(1)}, u32[]{:S(2)}, u32[]{:S(2)}) collective-permute-start(bf16[256,2560]{1,0:T(8,128)(2,1)} %get-tuple-element.730), channel_id=1, source_target_pairs={{0,4},{1,5},{2,6},{3,7},{4,0},{5,1},{6,2},{7,3},{8,12},{9,13},{10,... | collective-permute-start | bytes 3932168 | tf_op jit(solution)/shard_map/ppermute | solution.py:311
  286.8 29.8 %collective-permute-start.47 = (bf16[256,2560]{1,0:T(8,128)(2,1)}, bf16[256,2560]{1,0:T(8,128)(2,1)S(1)}, u32[]{:S(2)}, u32[]{:S(2)}) collective-permute-start(bf16[256,2560]{1,0:T(8,128)(2,1)} %get-tuple-element.731), channel_id=1, source_target_pairs={{0,2},{1,3},{2,0},{3,1},{4,6},{5,7},{6,4},{7,5},{8,10},{9,11},{10,... | collective-permute-start | bytes 3932168 | tf_op jit(solution)/shard_map/ppermute | solution.py:311
  287.6 25.8 %collective-permute-start.48 = (bf16[1024,512]{1,0:T(8,128)(2,1)}, bf16[1024,512]{1,0:T(8,128)(2,1)}, u32[]{:S(2)}, u32[]{:S(2)}) collective-permute-start(bf16[1024,512]{1,0:T(8,128)(2,1)} %add_convert_fusion.1), channel_id=1, source_target_pairs={{8,0},{16,8},{24,16},{9,1},{17,9},{25,17},{10,2},{18,10},{26,18},{... | collective-permute-start | bytes 3145736 | tf_op jit(solution)/shard_map/ppermute | solution.py:316
  318.9 18.5 %collective-permute-start.52 = (f32[512,1024]{1,0:T(8,128)}, f32[512,1024]{1,0:T(8,128)S(1)}, u32[]{:S(2)}, u32[]{:S(2)}) collective-permute-start(f32[512,1024]{1,0:T(8,128)} %get-tuple-element.771), channel_id=1, source_target_pairs={{0,1},{1,0},{2,3},{3,2},{4,5},{5,4},{6,7},{7,6},{8,9},{9,8},{10,11... | collective-permute-start | bytes 6291464 | tf_op jit(solution)/shard_map/ppermute | solution.py:311
  320.4 16.7 %collective-permute-start.49 = (bf16[128,2560]{1,0:T(8,128)(2,1)}, bf16[128,2560]{1,0:T(8,128)(2,1)}, u32[]{:S(2)}, u32[]{:S(2)}) collective-permute-start(bf16[128,2560]{1,0:T(8,128)(2,1)} %add_convert_fusion.4), channel_id=1, source_target_pairs={{0,2},{1,3},{2,0},{3,1},{4,6},{5,7},{6,4},{7,5},{8,10},{9,11},{10,... | collective-permute-start | bytes 1966088 | tf_op jit(solution)/shard_map/ppermute | solution.py:311
  321.1 16.4 %collective-permute-start.50 = (bf16[128,2560]{1,0:T(8,128)(2,1)}, bf16[128,2560]{1,0:T(8,128)(2,1)}, u32[]{:S(2)}, u32[]{:S(2)}) collective-permute-start(bf16[128,2560]{1,0:T(8,128)(2,1)} %add_convert_fusion.3), channel_id=1, source_target_pairs={{0,4},{1,5},{2,6},{3,7},{4,0},{5,1},{6,2},{7,3},{8,12},{9,13},{10,... | collective-permute-start | bytes 1966088 | tf_op jit(solution)/shard_map/ppermute | solution.py:311
  322.2 14.9 %collective-permute-start.51 = (bf16[256,1024]{1,0:T(8,128)(2,1)}, bf16[256,1024]{1,0:T(8,128)(2,1)}, u32[]{:S(2)}, u32[]{:S(2)}) collective-permute-start(bf16[256,1024]{1,0:T(8,128)(2,1)} %add_convert_fusion.5), channel_id=1, source_target_pairs={{0,8},{8,0},{16,24},{24,16},{1,9},{9,1},{17,25},{25,17},{2,10},{10... | collective-permute-start | bytes 1572872 | tf_op jit(solution)/shard_map/ppermute | solution.py:311
  342.4 22.5 %collective-permute-start.53 = (bf16[256,1536]{1,0:T(8,128)(2,1)}, bf16[256,1536]{1,0:T(8,128)(2,1)}, u32[]{:S(2)}, u32[]{:S(2)}) collective-permute-start(bf16[256,1536]{1,0:T(8,128)(2,1)} %get-tuple-element.806), channel_id=1, source_target_pairs={{0,4},{1,5},{2,6},{3,7},{4,0},{5,1},{6,2},{7,3},{8,12},{9,13},{10,... | collective-permute-start | bytes 2359304 | tf_op jit(solution)/shard_map/ppermute | solution.py:311
  343.6 21.3 %collective-permute-start.54 = (bf16[256,1536]{1,0:T(8,128)(2,1)}, bf16[256,1536]{1,0:T(8,128)(2,1)S(1)}, u32[]{:S(2)}, u32[]{:S(2)}) collective-permute-start(bf16[256,1536]{1,0:T(8,128)(2,1)} %get-tuple-element.807), channel_id=1, source_target_pairs={{0,2},{1,3},{2,0},{3,1},{4,6},{5,7},{6,4},{7,5},{8,10},{9,11},{10,... | collective-permute-start | bytes 2359304 | tf_op jit(solution)/shard_map/ppermute | solution.py:311
  344.4 20.5 %collective-permute-start.55 = (bf16[128,2560]{1,0:T(8,128)(2,1)}, bf16[128,2560]{1,0:T(8,128)(2,1)}, u32[]{:S(2)}, u32[]{:S(2)}) collective-permute-start(bf16[128,2560]{1,0:T(8,128)(2,1)} %add_convert_fusion.2), channel_id=1, source_target_pairs={{0,8},{8,0},{16,24},{24,16},{1,9},{9,1},{17,25},{25,17},{2,10},{10... | collective-permute-start | bytes 1966088 | tf_op jit(solution)/shard_map/ppermute | solution.py:311
  345.6 18.3 %collective-permute-start.56 = (bf16[128,1024]{1,0:T(8,128)(2,1)}, bf16[128,1024]{1,0:T(8,128)(2,1)}, u32[]{:S(2)}, u32[]{:S(2)}) collective-permute-start(bf16[128,1024]{1,0:T(8,128)(2,1)} %add_convert_fusion.14), channel_id=1, source_target_pairs={{0,16},{8,24},{16,0},{24,8},{1,17},{9,25},{17,1},{25,9},{2,18},{10... | collective-permute-start | bytes 786440 | tf_op jit(solution)/shard_map/ppermute | solution.py:311
  373.3 18.0 %collective-permute-start.57 = (bf16[128,1536]{1,0:T(8,128)(2,1)}, bf16[128,1536]{1,0:T(8,128)(2,1)}, u32[]{:S(2)}, u32[]{:S(2)}) collective-permute-start(bf16[128,1536]{1,0:T(8,128)(2,1)} %add_convert_fusion.12), channel_id=1, source_target_pairs={{0,2},{1,3},{2,0},{3,1},{4,6},{5,7},{6,4},{7,5},{8,10},{9,11},{10,... | collective-permute-start | bytes 1179656 | tf_op jit(solution)/shard_map/ppermute | solution.py:311
  374.0 17.4 %collective-permute-start.58 = (bf16[128,1536]{1,0:T(8,128)(2,1)S(1)}, bf16[128,1536]{1,0:T(8,128)(2,1)}, u32[]{:S(2)}, u32[]{:S(2)}) collective-permute-start(bf16[128,1536]{1,0:T(8,128)(2,1)S(1)} %add_convert_fusion.11), channel_id=1, source_target_pairs={{0,4},{1,5},{2,6},{3,7},{4,0},{5,1},{6,2},{7,3},{8,12},{9,13},{10,... | collective-permute-start | bytes 1179656 | tf_op jit(solution)/shard_map/ppermute | solution.py:311
  374.4 17.0 %collective-permute-start.59 = (bf16[64,2560]{1,0:T(8,128)(2,1)}, bf16[64,2560]{1,0:T(8,128)(2,1)}, u32[]{:S(2)}, u32[]{:S(2)}) collective-permute-start(bf16[64,2560]{1,0:T(8,128)(2,1)} %add_convert_fusion.13), channel_id=1, source_target_pairs={{0,16},{8,24},{16,0},{24,8},{1,17},{9,25},{17,1},{25,9},{2,18},{10... | collective-permute-start | bytes 983048 | tf_op jit(solution)/shard_map/ppermute | solution.py:311
  409.7 11.7 %collective-permute-start.65 = (bf16[64,1536]{1,0:T(8,128)(2,1)S(1)}, bf16[64,1536]{1,0:T(8,128)(2,1)S(1)}, u32[]{:S(2)}, u32[]{:S(2)}) collective-permute-start(bf16[64,1536]{1,0:T(8,128)(2,1)S(1)} %add_convert_fusion.15), channel_id=1, source_target_pairs={{0,16},{8,24},{16,0},{24,8},{1,17},{9,25},{17,1},{25,9},{2,18},{10... | collective-permute-start | bytes 589832 | tf_op jit(solution)/shard_map/ppermute | solution.py:311
  (85 other events, 876.4 us)
where the time goes:
time: 437 us; the launch traced here: 434 us
  Pallas kernels  181 us (41%)
  starting transfers between devices  103 us (24%)
  waiting for transfers between devices  79.9 us (18%)
  other arithmetic  44.8 us (10%)
  local copies, waits for them, and re-layouts  24.6 us (6%)
    ppermute x58, starting transfers between devices, swap(): lax.ppermute(value, axis, [(i, i ^ bit) for i in range(lax.axis_size(axis...  70.8 us
    ppermute x58, waiting for transfers between devices, swap(): lax.ppermute(value, axis, [(i, i ^ bit) for i in range(lax.axis_size(axis...  44.5 us
    ppermute x12, waiting for transfers between devices, shift(): lax.ppermute(value, 'seq', [(i, i + by) for i in range(count) if 0 <= i +...  35.3 us
    pallas_call x3, Pallas kernels, attend(): pl.pallas_call(attend_kernel, grid=(4, pairs), out_shape=(shaped(1024, 12...  34.4 us
    ppermute x12, starting transfers between devices, shift(): lax.ppermute(value, 'seq', [(i, i + by) for i in range(count) if 0 <= i +...  32 us
    pallas_call x2, Pallas kernels, norm_grad(): pl.pallas_call(partial(norm_grad_kernel, spans), grid=(4,), out_shape=(sh...  19.3 us
    pallas_call x2, Pallas kernels, row_grads(): pl.pallas_call(partial(row_grads_kernel, steps), grid=(columns // step,),...  16.2 us
    pallas_call x1, Pallas kernels, hidden(): pl.pallas_call(hidden_kernel, grid=(width // step,), out_shape=(shaped(ro...  15 us
  transfers between devices with their start and end apart: 70, of which 24 were waited for; matrix products, arithmetic and copies ran while one was open for 6% of the time, Pallas kernels for 41%

commit v1 on v0

--- a/solution.py
+++ b/solution.py
@@ -639,7 +639,7 @@
 
 def prepare(where, own, other):
     rows = own.shape[0]
-    step = 128
+    step = 256
     steps = rows // step
     return pl.pallas_call(
         partial(prepare_kernel, steps),
@@ -1399,14 +1399,17 @@
     def slot(jobs, work=None, *inputs, chain=None, late=(), then=None):
         nonlocal waiting
         jobs, late = list(jobs), list(late)
-        name, follow, more = chain if chain is not None else (None, None, ())
-        gated, given, more = clock.join(tuple(job[2] for job in jobs + late), inputs, tuple(more))
+        chains = chain if isinstance(chain, list) else [chain] if chain is not None else []
+        gated, given, more = clock.join(
+            tuple(job[2] for job in jobs + late), inputs, tuple(tuple(link[2]) for link in chains)
+        )
         values = [job[3](value) for job, value in zip(jobs + late, gated)]
         made = work(*given) if work is not None else ()
-        after = ()
-        for job, value in list(zip(jobs, values)) + waiting:
-            if chain is not None and job[1] == name:
-                after = follow(value, *more)
+        after = []
+        for (name, follow, _), inputs in zip(chains, more):
+            for job, value in list(zip(jobs, values)) + waiting:
+                if job[1] == name:
+                    after.append(follow(value, *inputs))
         if then is not None:
             started = then(made)
             late = late + started
@@ -1417,7 +1420,9 @@
         for job, value in zip(jobs + [job for job, _ in ended], found):
             job[0][job[1]] = value
         waiting = list(zip(late, older))
-        return made if chain is None else (made, after)
+        if chain is None:
+            return made
+        return made, after if isinstance(chain, list) else after[0]
 
     def moves(line, stage):
         return [
@@ -1470,7 +1475,7 @@
     )
     a_pieces = line_a.pieces()
     made = slot(
-        moves(line_b, "first") + moves(line_c, "near"),
+        moves(line_b, "first") + moves(line_c, "near") + moves(line_d, "far"),
         lambda xhat, tables, pieces: project_first(clock.token, xhat, tables, pieces),
         xhat,
         tables,
@@ -1505,11 +1510,11 @@
         for group, result in zip(groups, found):
             results[group] = result
 
-    slot(moves(line_b, "second") + [up(0, 0)], late=moves(line_d, "far"))
+    slot(moves(line_b, "second") + [up(0, 0)])
     landed((0, 0))
     b_pieces = line_b.pieces()
     made, (out_keep, out_give) = slot(
-        moves(line_c, "first") + [up(0, 1)],
+        moves(line_c, "first") + [up(0, 1), up(1, 0)],
         lambda normed, bias, tables, pieces: (
             project_more(normed, bias, tables, pieces),
             head_rows(clock.token, pieces),
@@ -1519,7 +1524,7 @@
         tables,
         b_pieces,
     )
-    landed((0, 1))
+    landed((0, 1), (1, 0))
     queries.append(made[0])
     kvs.append([made[1]])
 
@@ -1528,7 +1533,7 @@
         return grad, heads, attend(0, query, grad, bias, kvs)
 
     _, (context_grad, out_heads, found) = slot(
-        moves(line_c, "second") + moves(line_d, "near") + [up(1, 0), core_move("out", out_give)],
+        moves(line_c, "second") + moves(line_d, "near") + [up(1, 1), core_move("out", out_give)],
         chain=(
             "out",
             first_attention,
@@ -1536,34 +1541,33 @@
         ),
     )
     results[0] = found
-    landed((1, 0))
+    landed((1, 1))
     c_pieces = line_c.pieces()
     act, act_t, slope = slot(
-        moves(line_d, "first") + [up(1, 1), down(0, 0)],
+        moves(line_d, "first") + [up(2, 0), down(0, 0)],
         lambda normed, b_in, pieces: hidden(normed, pieces, b_in),
         normed,
         b_in,
         c_pieces,
-        late=[up(2, 0)],
-    )
-    landed((1, 1))
+    )
+    landed((2, 0))
     work, *given = attention(1)
 
     def with_units(given, act_t, own, other):
         found = work(given)
         return found, unit_grads(clock.token[0], act_t, own, other), shift(found[0][4], -1)
 
-    (found, fc_parts, backs[1, 0]), moved[2, 1] = slot(
-        moves(line_d, "second") + [down(0, 1)],
+    found, fc_parts, backs[1, 0] = slot(
+        moves(line_d, "second") + [up(2, 1)],
         with_units,
         *given,
         act_t,
         g_own,
         g_more,
-        chain=((2, 0), lambda value: shift(value, 1), ()),
+        late=[down(0, 1)],
     )
     attended([1], found)
-    landed((2, 0), (2, 1))
+    landed((2, 1))
     d_pieces = line_d.pieces()
     sum_fc = Scatter(fc_parts)
     work2, *given = attention(2)
@@ -1589,9 +1593,17 @@
         more = jnp.concatenate([out_keep, out_more], axis=0)
         return hidden_grad, hidden_sum, row_grads(clock.token, normed_t, hidden_grad, more)
 
-    _, (hidden_grad, hidden_sum, in_parts) = slot(
+    def near_now(last, own, earlier):
+        rows = own.shape[0]
+        total = own.astype(F32) + earlier[:rows].astype(F32) + last.astype(F32)
+        return cross(total.astype(BF), NEAR)
+
+    _, ((hidden_grad, hidden_sum, in_parts), sum_fc.parts["r_b"]) = slot(
         moves(sum_fc, "second") + [core_move("out_grad", out_give)],
-        chain=("out_grad", units_back, (out_keep, normed_t, g_own, g_more, slope, d_pieces)),
+        chain=[
+            ("out_grad", units_back, (out_keep, normed_t, g_own, g_more, slope, d_pieces)),
+            ("r_yb", near_now, (sum_fc.parts["b"], sum_fc.parts["r_xby"])),
+        ],
     )
     sum_in = Scatter(in_parts)
     (out_mine, out_theirs), earlier = slot(
@@ -1613,20 +1625,22 @@
         return projected_grad, total, row_grads(clock.token, normed_t, projected_grad)
 
     projected_grad, qkv_bias_sum, parts = slot(
-        moves(sum_in, "second") + moves(sum_fc, "near") + [core_move("out_side", out_theirs)],
+        moves(sum_in, "second") + moves(sum_fc, "far") + [core_move("out_side", out_theirs)],
         last_grads,
         normed_t,
         tables,
         [(results[group][1], results[group][2], backs[group, 1]) for group in range(3)],
     )
     sum_qkv = Scatter(parts)
-    norm_mine, norm_theirs = slot(
-        moves(sum_qkv, "first") + moves(sum_in, "near") + moves(sum_fc, "far"),
-        lambda projected_grad, earlier, *lines: norm_grad(
-            projected_grad, lines, [(0, 768), (512, 1280)], earlier
+    (norm_mine, norm_theirs), sum_in.parts["r_b"] = slot(
+        moves(sum_qkv, "first"),
+        lambda projected_grad, earlier, terms, *lines: (
+            norm_grad(projected_grad, lines, [(0, 768), (512, 1280)], earlier),
+            near_now(*terms),
         ),
         projected_grad,
         earlier,
+        tuple(sum_in.parts[name] for name in ("r_yb", "b", "r_xby")),
         a_pieces,
         b_pieces,
     )

time: 437 us -> 421 us (0.963)
  waiting for transfers between devices: 79.9 us -> 61.7 us
    ppermute x12, waiting for transfers between devices: 35.3 us -> 20 us  [shift(): lax.ppermute(value, 'seq', [(i, i + by) for i in range(count) if 0 <= i +...]
    ppermute x58, starting transfers between devices: 70.8 us -> 77 us  [swap(): lax.ppermute(value, axis, [(i, i ^ bit) for i in range(lax.axis_size(axis...]
    convert_element_type x3 -> x1, other arithmetic: 6.18 us -> 1.38 us  [jobs(): parts['b'] = self.total(0, rows, 'b', 'r_xby', 'r_yb').astype(BF)]
    convert_element_type x0 -> x2, other arithmetic: none -> 4.7 us  [near_now(): return cross(total.astype(BF), NEAR)]
    unnamed x132 -> x124, local copies, waits for them, and re-layouts: 12.7 us -> 11.5 us
    convert_element_type x5 -> x6, other arithmetic: 8.75 us -> 9.74 us  [jobs(): parts[name] = value.astype(BF)]
  transfers between devices with their start and end apart: 70 -> 70, of which waited for: 24 -> 25; matrix products, arithmetic and copies ran while one was open for 6% -> 7% of each run, Pallas kernels for 41% -> 42%
where the time goes in v1:
time: 421 us; the launch traced here: 419 us
  Pallas kernels  179 us (43%)
  starting transfers between devices  107 us (25%)
  waiting for transfers between devices  61.7 us (15%)
  other arithmetic  46.5 us (11%)
  local copies, waits for them, and re-layouts  23.2 us (6%)
    ppermute x58, starting transfers between devices, swap(): lax.ppermute(value, axis, [(i, i ^ bit) for i in range(lax.axis_size(axis...  77 us
    ppermute x58, waiting for transfers between devices, swap(): lax.ppermute(value, axis, [(i, i ^ bit) for i in range(lax.axis_size(axis...  41.8 us
    pallas_call x3, Pallas kernels, attend(): pl.pallas_call(attend_kernel, grid=(4, pairs), out_shape=(shaped(1024, 12...  34.4 us
    ppermute x12, starting transfers between devices, shift(): lax.ppermute(value, 'seq', [(i, i + by) for i in range(count) if 0 <= i +...  30 us
    ppermute x12, waiting for transfers between devices, shift(): lax.ppermute(value, 'seq', [(i, i + by) for i in range(count) if 0 <= i +...  20 us
    pallas_call x2, Pallas kernels, norm_grad(): pl.pallas_call(partial(norm_grad_kernel, spans), grid=(4,), out_shape=(sh...  19.3 us
    pallas_call x2, Pallas kernels, row_grads(): pl.pallas_call(partial(row_grads_kernel, steps), grid=(columns // step,),...  16.2 us
    pallas_call x1, Pallas kernels, hidden(): pl.pallas_call(hidden_kernel, grid=(width // step,), out_shape=(shaped(ro...  15 us
  transfers between devices with their start and end apart: 70, of which 25 were waited for; matrix products, arithmetic and copies ran while one was open for 7% of the time, Pallas kernels for 42%

profile of v1, /device:TPU:1, one launch (start us, length us, event | category | flops | bytes accessed | tf_op | source)
XLA Modules:
  0.0 418.6 jit_solution(12003976015455764015)
XLA Ops:
  5.9 3.7 collective-permute-start.1
  11.0 4.3 %collective-permute-done.1 = bf16[64,896]{1,0:T(8,128)(2,1)S(1)} collective-permute-done((bf16[64,896]{1,0:T(8,128)(2,1)S(1)}, bf16[64,896]{1,0:T(8,128)(2,1)S(1)}, u32[]{:S(2)}, u32[]{:S(2)}) %collective-permute-start.1) | collective-permute-done | bytes 114720 | tf_op jit(solution)/shard_map/ppermute | solution.py:311
  19.1 3.1 collective-permute-start.5
  24.0 3.6 collective-permute-done.5
  35.7 5.0 %marks.1 = (f32[4,768,256]{2,1,0:T(8,128)}, f32[1024,128]{1,0:T(8,128)}, f32[1024,128]{1,0:T(8,128)}, f32[1024,128]{1,0:T(8,128)}) custom-call(s32[2]{0:T(128)} %pad_add_fusion.where_ref, bf16[128,896]{1,0:T(8,128)(2,1)} %copy-done.15, bf16[128,896]{1,0:T(8,128)(2,1)} %copy-done.16, f32[1,128]{1,0:T(1,128)} %bitcast.41, f32[1,128]{1,0:T(1,128)} %constant.130.clone.forth_ref, ...), custom_call_target="tpu_custom_call" | custom-call | flops 13107200 | bytes 4194304 | tf_op jit(solution)/shard_map/marks/pallas_call | solution.py:586
  46.3 7.1 %prepare.1 = (f32[1024,1024]{1,0:T(8,128)}, f32[1024,1]{1,0:T(8,128)}) custom-call(s32[2]{0:T(128)} %pad_add_fusion.where_ref, bf16[512,1024]{1,0:T(8,128)(2,1)} %bitcast.31, bf16[512,1024]{1,0:T(8,128)(2,1)} %collective-permute-done.2.other_ref), custom_call_target="tpu_custom_call" | custom-call | flops 2147483648 | bytes 8388608 | tf_op jit(solution)/shard_map/prepare/pallas_call | solution.py:644
  53.4 6.2 %collective-permute-done.13 = bf16[64,2048]{1,0:T(8,128)(2,1)S(1)} collective-permute-done((bf16[64,2048]{1,0:T(8,128)(2,1)}, bf16[64,2048]{1,0:T(8,128)(2,1)S(1)}, u32[]{:S(2)}, u32[]{:S(2)}) %collective-permute-start.13) | collective-permute-done | bytes 262176 | tf_op jit(solution)/shard_map/ppermute | solution.py:311
  65.7 7.9 %project_first.1 = (bf16[1024,128]{1,0:T(8,128)(2,1)}, bf16[1024,256]{1,0:T(8,128)(2,1)}, bf16[1024,128]{1,0:T(8,128)(2,1)}, bf16[1024,256]{1,0:T(8,128)(2,1)}, ...) custom-call(s32[2]{0:T(128)} %pad_add_fusion.where_ref, ...), custom_call_target="tpu_custom_call" | custom-call | flops 1610612736 | bytes 12582912 | tf_op jit(solution)/shard_map/project_first/pallas_call | solution.py:728
  73.6 2.6 collective-permute-done.17
  81.6 3.6 collective-permute-start.20
  85.2 8.4 %collective-permute-done.20.refs_1_ = bf16[1024,256]{1,0:T(8,128)(2,1)} collective-permute-done((bf16[1024,256]{1,0:T(8,128)(2,1)}, bf16[1024,256]{1,0:T(8,128)(2,1)}, u32[]{:S(2)}, u32[]{:S(2)}) %collective-permute-start.20) | collective-permute-done | bytes 524320 | tf_op jit(solution)/shard_map/ppermute | solution.py:316
  95.7 4.1 collective-permute-start.23
  107.6 2.3 head_rows.1
  109.9 6.4 %project_more.1 = (bf16[1024,256]{1,0:T(8,128)(2,1)}, bf16[1024,512]{1,0:T(8,128)(2,1)}) custom-call(bf16[1024,1024]{1,0:T(8,128)(2,1)} %get-tuple-element.615.normed_ref, f32[1,768]{1,0:T(1,128)} %get-tuple-element.560.bias_ref, f32[1024,128]{1,0:T(8,128)} %get-tuple-element.780.cos_ref, f32[1024,128]{1,0:T(8,128)} %get-tuple-element.781.forth_ref, ...), custom_call_target="tpu_custom_call" | custom-call | flops 1610612736 | bytes 6291456 | tf_op jit(solution)/shard_map/project_more/pallas_call | solution.py:752
  122.3 5.3 %collective-permute-start.29 = (bf16[256,1024]{1,0:T(8,128)(2,1)S(1)}, bf16[256,1024]{1,0:T(8,128)(2,1)}, u32[]{:S(2)}, u32[]{:S(2)}) collective-permute-start(bf16[256,1024]{1,0:T(8,128)(2,1)S(1)} %copy-done.56), channel_id=1, source_target_pairs={{0,1},{1,0},{2,3},{3,2},{4,5},{5,4},{6,7},{7,6},{8,9},{9,8},{10,11... | collective-permute-start | bytes 1572872 | tf_op jit(solution)/shard_map/ppermute | solution.py:311
  131.8 5.1 %context_grad.1 = (bf16[1024,512]{1,0:T(8,128)(2,1)}, bf16[512,1024]{1,0:T(8,128)(2,1)}) custom-call(s32[2]{0:T(128)} %pad_add_fusion.where_ref, bf16[512,1024]{1,0:T(8,128)(2,1)} %bitcast.24, bf16[512,1024]{1,0:T(8,128)(2,1)} %copy-done.13, bf16[256,1024]{1,0:T(8,128)(2,1)} %get-tuple-element.591.keep_ref, bf16[256,1024]{1,0:T(8,128)(2,1)} %collective-permute-done.29.more_ref), custom_call_target="tpu_custom_call" | custom-call | flops 1073741824 | bytes 6291456 | tf_op jit(solution)/shard_map/context_grad/pallas_call | solution.py:818
  136.9 9.0 %attend.3 = (bf16[1024,128]{1,0:T(8,128)(2,1)}, bf16[1024,128]{1,0:T(8,128)(2,1)}, f32[1024,256]{1,0:T(8,128)}, bf16[1024,256]{1,0:T(8,128)(2,1)}, bf16[1024,256]{1,0:T(8,128)(2,1)}) custom-call(bf16[1024,128]{1,0:T(8,128)(2,1)} %get-tuple-element.594.q_ref, bf16[1024,512]{1,0:T(8,128)(2,1)} %get-tuple-element.674.do_ref, ...), custom_call_target="tpu_custom_call" | custom-call | flops 2415919104 | bytes 9437184 | tf_op jit(solution)/shard_map/attend/pallas_call | solution.py:900
  145.9 6.8 %collective-permute-done.28.refs_2_ = bf16[1024,256]{1,0:T(8,128)(2,1)S(1)} collective-permute-done((bf16[1024,256]{1,0:T(8,128)(2,1)}, bf16[1024,256]{1,0:T(8,128)(2,1)S(1)}, u32[]{:S(2)}, u32[]{:S(2)}) %collective-permute-start.28) | collective-permute-done | bytes 524320 | tf_op jit(solution)/shard_map/ppermute | solution.py:316
  152.7 5.0 %collective-permute-start.32 = (bf16[1024,512]{1,0:T(8,128)(2,1)}, bf16[1024,512]{1,0:T(8,128)(2,1)}, u32[]{:S(2)}, u32[]{:S(2)}) collective-permute-start(bf16[1024,512]{1,0:T(8,128)(2,1)} %get-tuple-element.676.refs_0_), channel_id=1, source_target_pairs={{0,8},{8,16},{16,24},{1,9},{9,17},{17,25},{2,10},{10,18},{18,26},{... | collective-permute-start | bytes 3145736 | tf_op jit(solution)/shard_map/ppermute | solution.py:316
  161.3 15.0 %hidden.1 = (bf16[1024,2048]{1,0:T(8,128)(2,1)}, bf16[2048,1024]{1,0:T(8,128)(2,1)}, f32[1024,2048]{1,0:T(8,128)}) custom-call(bf16[1024,1024]{1,0:T(8,128)(2,1)} %get-tuple-element.615.normed_ref, f32[1,2048]{1,0:T(1,128)} %get-tuple-element.616.bias_ref, bf16[256,2048]{1,0:T(8,128)(2,1)} %copy-done.12, bf16[256,2048]{1,0:T(8,128)(2,1)} %copy-done.45, ...), custom_call_target="tpu_custom_call" | custom-call | flops 4399824896 | bytes 18874368 | tf_op jit(solution)/shard_map/hidden/pallas_call | solution.py:1000
  176.4 2.4 collective-permute-done.32.refs_1_
  182.0 5.0 %collective-permute-start.36 = (bf16[1024,512]{1,0:T(8,128)(2,1)}, bf16[1024,512]{1,0:T(8,128)(2,1)}, u32[]{:S(2)}, u32[]{:S(2)}) collective-permute-start(bf16[1024,512]{1,0:T(8,128)(2,1)} %collective-permute-done.32.refs_1_), channel_id=1, source_target_pairs={{0,8},{8,16},{16,24},{1,9},{9,17},{17,25},{2,10},{10,18},{18,26},{... | collective-permute-start | bytes 3145736 | tf_op jit(solution)/shard_map/ppermute | solution.py:316
  187.0 9.0 %attend.4 = (bf16[1024,128]{1,0:T(8,128)(2,1)}, bf16[1024,128]{1,0:T(8,128)(2,1)}, f32[1024,256]{1,0:T(8,128)}, bf16[1024,256]{1,0:T(8,128)(2,1)}, bf16[1024,256]{1,0:T(8,128)(2,1)}) custom-call(bf16[1024,128]{1,0:T(8,128)(2,1)} %get-tuple-element.638.q_ref, bf16[1024,512]{1,0:T(8,128)(2,1)} %get-tuple-element.674.do_ref, ...), custom_call_target="tpu_custom_call" | custom-call | flops 2415919104 | bytes 9437184 | tf_op jit(solution)/shard_map/attend/pallas_call | solution.py:900
  197.9 11.6 %unit_grads.1 = (bf16[256,1024]{1,0:T(8,128)(2,1)}, bf16[256,1024]{1,0:T(8,128)(2,1)}, bf16[256,1024]{1,0:T(8,128)(2,1)}, bf16[256,1024]{1,0:T(8,128)(2,1)}, bf1...) custom-call(s32[16]{0:T(128)} %broadcast_xor_fusion.order_ref, ...), custom_call_target="tpu_custom_call" | custom-call | flops 4294967296 | bytes 8388608 | tf_op jit(solution)/shard_map/unit_grads/pallas_call | solution.py:1192
  215.0 16.3 %attend.5 = (bf16[1024,256]{1,0:T(8,128)(2,1)}, bf16[1024,256]{1,0:T(8,128)(2,1)}, f32[1024,512]{1,0:T(8,128)}, bf16[1024,512]{1,0:T(8,128)(2,1)}, bf16[1024,512]{1,0:T(8,128)(2,1)}) custom-call(bf16[1024,256]{1,0:T(8,128)(2,1)} %get-tuple-element.673.q_ref, bf16[1024,512]{1,0:T(8,128)(2,1)} %get-tuple-element.674.do_ref, ...), custom_call_target="tpu_custom_call" | custom-call | flops 4831838208 | bytes 18874368 | tf_op jit(solution)/shard_map/attend/pallas_call | solution.py:900
  231.3 5.0 %out_grad.1 = (bf16[256,1024]{1,0:T(8,128)(2,1)}, bf16[256,1024]{1,0:T(8,128)(2,1)}) custom-call(s32[2]{0:T(128)} %pad_add_fusion.where_ref, bf16[512,1024]{1,0:T(8,128)(2,1)} %bitcast.26, bf16[512,1024]{1,0:T(8,128)(2,1)} %copy-done.13, bf16[1024,128]{1,0:T(8,128)(2,1)} %get-tuple-element.743.refs_0_, bf16[1024,128]{1,0:T(8,128)(2,1)} %get-tuple-element.744.refs_1_, ...), custom_call_target="tpu_custom_call" | custom-call | flops 1073741824 | bytes 6291456 | tf_op jit(solution)/shard_map/out_grad/pallas_call | solution.py:1234
  236.7 2.4 add_convert_fusion.7
  243.8 4.6 %collective-permute-start.44 = (bf16[256,1024]{1,0:T(8,128)(2,1)}, bf16[256,1024]{1,0:T(8,128)(2,1)}, u32[]{:S(2)}, u32[]{:S(2)}) collective-permute-start(bf16[256,1024]{1,0:T(8,128)(2,1)} %get-tuple-element.704), channel_id=1, source_target_pairs={{0,1},{1,0},{2,3},{3,2},{4,5},{5,4},{6,7},{7,6},{8,9},{9,8},{10,11... | collective-permute-start | bytes 1572872 | tf_op jit(solution)/shard_map/ppermute | solution.py:311
  248.4 11.6 %unit_back.1 = (bf16[1024,2048]{1,0:T(8,128)(2,1)}, f32[1,2048]{1,0:T(1,128)}) custom-call(s32[2]{0:T(128)} %pad_add_fusion.where_ref, bf16[512,1024]{1,0:T(8,128)(2,1)} %bitcast.27, bf16[512,1024]{1,0:T(8,128)(2,1)} %copy-done.13, f32[1024,2048]{1,0:T(8,128)} %get-tuple-element.708.slope_ref, bf16[512,1024]{1,0:T(8,128)(2,1)} %get-tuple-element.746.refs_0_.refs_3_, ...), custom_call_target="tpu_custom_call" | custom-call | flops 4294967296 | bytes 16777216 | tf_op jit(solution)/shard_map/unit_back/pallas_call | solution.py:1056
  260.0 2.3 add_convert_fusion.5
  262.3 3.0 collective-permute-start.46
  267.4 9.2 %row_grads.2 = (bf16[128,2560]{1,0:T(8,128)(2,1)}, bf16[128,2560]{1,0:T(8,128)(2,1)}, bf16[128,2560]{1,0:T(8,128)(2,1)}, bf16[128,2560]{1,0:T(8,128)(2,1)}, bf16...) custom-call(s32[2]{0:T(128)} %pad_add_fusion.where_ref, bf16[1024,1024]{1,0:T(8,128)(2,1)} %get-tuple-element.795.left_ref, ...), custom_call_target="tpu_custom_call" | custom-call | flops 5368709120 | bytes 7340032 | tf_op jit(solution)/shard_map/row_grads/pallas_call | solution.py:1145
  285.3 9.6 %norm_grad.2 = (f32[512,1024]{1,0:T(8,128)}, f32[512,1024]{1,0:T(8,128)}) custom-call(bf16[1024,2048]{1,0:T(8,128)(2,1)} %get-tuple-element.752.right_ref.left_ref, bf16[256,2048]{1,0:T(8,128)(2,1)} %copy-done.12, bf16[256,2048]{1,0:T(8,128)(2,1)} %copy-done.45, bf16[256,2048]{1,0:T(8,128)(2,1)} %collective-permute-done.25.refs_2_, ...), custom_call_target="tpu_custom_call" | custom-call | flops 4294967296 | bytes 12582912 | tf_op jit(solution)/shard_map/norm_grad/pallas_call | solution.py:1283
  294.9 11.9 %unit_out.1 = (f32[512,1024]{1,0:T(8,128)}, f32[512,1024]{1,0:T(8,128)}) custom-call(s32[2]{0:T(128)} %pad_add_fusion.where_ref, bf16[1024,2048]{1,0:T(8,128)(2,1)} %get-tuple-element.741.act_ref, bf16[512,1024]{1,0:T(8,128)(2,1)} %get-tuple-element.742.heads_ref, bf16[1024,128]{1,0:T(8,128)(2,1)} %get-tuple-element.743.refs_0_, ...), custom_call_target="tpu_custom_call" | custom-call | flops 6442450944 | bytes 12582912 | tf_op jit(solution)/shard_map/unit_out/pallas_call | solution.py:1092
  309.7 5.0 %collective-permute-start.53 = (f32[512,1024]{1,0:T(8,128)}, f32[512,1024]{1,0:T(8,128)S(1)}, u32[]{:S(2)}, u32[]{:S(2)}) collective-permute-start(f32[512,1024]{1,0:T(8,128)} %get-tuple-element.779), channel_id=1, source_target_pairs={{0,1},{1,0},{2,3},{3,2},{4,5},{5,4},{6,7},{7,6},{8,9},{9,8},{10,11... | collective-permute-start | bytes 6291464 | tf_op jit(solution)/shard_map/ppermute | solution.py:311
  315.6 3.2 collective-permute-start.52
  318.8 6.5 %unturn.1 = (bf16[1024,1536]{1,0:T(8,128)(2,1)}, f32[1,1536]{1,0:T(1,128)}) custom-call(f32[1024,128]{1,0:T(8,128)} %get-tuple-element.780.cos_ref, f32[1024,128]{1,0:T(8,128)} %get-tuple-element.781.forth_ref, f32[1024,128]{1,0:T(8,128)} %get-tuple-element.782.back_ref, bf16[1024,128]{1,0:T(8,128)(2,1)} %get-tuple-element.783.refs_0_, ...), custom_call_target="tpu_custom_call" | custom-call | flops 15728640 | bytes 12582912 | tf_op jit(solution)/shard_map/unturn/pallas_call | solution.py:956
  325.3 7.1 %row_grads.3 = (bf16[128,1536]{1,0:T(8,128)(2,1)}, bf16[128,1536]{1,0:T(8,128)(2,1)}, bf16[128,1536]{1,0:T(8,128)(2,1)}, bf16[128,1536]{1,0:T(8,128)(2,1)}, bf16...) custom-call(s32[2]{0:T(128)} %pad_add_fusion.where_ref, bf16[1024,1024]{1,0:T(8,128)(2,1)} %get-tuple-element.795.left_ref, ...), custom_call_target="tpu_custom_call" | custom-call | flops 3221225472 | bytes 5242880 | tf_op jit(solution)/shard_map/row_grads/pallas_call | solution.py:1145
  334.6 2.4 add_convert_fusion.2
  338.8 9.7 %norm_grad.3 = (f32[512,1024]{1,0:T(8,128)}, f32[512,1024]{1,0:T(8,128)}) custom-call(bf16[1024,1536]{1,0:T(8,128)(2,1)} %get-tuple-element.813.right_ref.left_ref, bf16[256,896]{1,0:T(8,128)(2,1)} %copy-done.8, bf16[256,896]{1,0:T(8,128)(2,1)} %copy-done.14, bf16[256,896]{1,0:T(8,128)(2,1)} %copy-done.41, bf16[256,896]{1,0:T(8,128)(2,1)} %collective-permute-done.12.refs_3_, ...), custom_call_target="tpu_custom_call" | custom-call | flops 3221225472 | bytes 12582912 | tf_op jit(solution)/shard_map/norm_grad/pallas_call | solution.py:1283
  348.6 4.2 %collective-permute-done.56 = bf16[128,2560]{1,0:T(8,128)(2,1)S(1)} collective-permute-done((bf16[128,2560]{1,0:T(8,128)(2,1)}, bf16[128,2560]{1,0:T(8,128)(2,1)S(1)}, u32[]{:S(2)}, u32[]{:S(2)}) %collective-permute-start.56) | collective-permute-done | bytes 655392 | tf_op jit(solution)/shard_map/ppermute | solution.py:311
  361.1 2.4 collective-permute-start.59
  365.3 7.3 %norm_back.1 = (bf16[512,1024]{1,0:T(8,128)(2,1)}, f32[8,1024]{1,0:T(8,128)}) custom-call(s32[2]{0:T(128)} %pad_add_fusion.where_ref, f32[512,1024]{1,0:T(8,128)} %get-tuple-element.850.part_ref, f32[512,1024]{1,0:T(8,128)} %copy-done.7, f32[1024,1024]{1,0:T(8,128)} %get-tuple-element.851.xhat_ref, f32[1024,1]{1,0:T(8,128)} %get-tuple-element.852.inv_ref, ...), custom_call_target="tpu_custom_call" | custom-call | flops 2147483648 | bytes 8388608 | tf_op jit(solution)/shard_map/norm_back/pallas_call | solution.py:1324
  374.8 3.3 collective-permute-done.59
  387.8 3.4 add_convert_fusion
  393.4 3.5 collective-permute-start.65
  402.1 3.5 collective-permute-done.65
  409.1 3.3 collective-permute-done.68
  (326 shorter events, 133.6 us)
Async XLA Ops:
  45.1 14.6 %collective-permute-start.11 = (bf16[256,896]{1,0:T(8,128)(2,1)S(1)}, bf16[256,896]{1,0:T(8,128)(2,1)S(1)}, u32[]{:S(2)}, u32[]{:S(2)}) collective-permute-start(bf16[256,896]{1,0:T(8,128)(2,1)S(1)} %pad_maximum_fusion.4.refs_0_), channel_id=1, source_target_pairs={{0,4},{1,5},{2,6},{3,7},{4,0},{5,1},{6,2},{7,3},{8,12},{9,13},{10,... | collective-permute-start | bytes 1376264 | tf_op jit(solution)/shard_map/ppermute | solution.py:311
  45.3 14.3 %collective-permute-start.12 = (bf16[256,896]{1,0:T(8,128)(2,1)S(1)}, bf16[256,896]{1,0:T(8,128)(2,1)}, u32[]{:S(2)}, u32[]{:S(2)}) collective-permute-start(bf16[256,896]{1,0:T(8,128)(2,1)S(1)} %constant_dynamic-update-slice_fusion.refs_1_), channel_id=1, source_target_pairs={{0,2},{1,3},{2,0},{3,1},{4,6},{5,7},{6,4},{7,5},{8,10},{9,11},{10,... | collective-permute-start | bytes 1376264 | tf_op jit(solution)/shard_map/ppermute | solution.py:311
  45.6 14.0 %collective-permute-start.13 = (bf16[64,2048]{1,0:T(8,128)(2,1)}, bf16[64,2048]{1,0:T(8,128)(2,1)S(1)}, u32[]{:S(2)}, u32[]{:S(2)}) collective-permute-start(bf16[64,2048]{1,0:T(8,128)(2,1)} %pad_maximum_fusion.6), channel_id=1, source_target_pairs={{0,16},{8,24},{16,0},{24,8},{1,17},{9,25},{17,1},{25,9},{2,18},{10... | collective-permute-start | bytes 786440 | tf_op jit(solution)/shard_map/ppermute | solution.py:311
  60.4 17.7 %collective-permute-start.16 = (bf16[128,2048]{1,0:T(8,128)(2,1)S(1)}, bf16[128,2048]{1,0:T(8,128)(2,1)S(1)}, u32[]{:S(2)}, u32[]{:S(2)}) collective-permute-start(bf16[128,2048]{1,0:T(8,128)(2,1)S(1)} %pad_maximum_fusion.3), channel_id=1, source_target_pairs={{0,8},{8,0},{16,24},{24,16},{1,9},{9,1},{17,25},{25,17},{2,10},{10... | collective-permute-start | bytes 1572872 | tf_op jit(solution)/shard_map/ppermute | solution.py:311
  60.5 15.8 %collective-permute-start.14 = (bf16[128,1280]{1,0:T(8,128)(2,1)}, bf16[128,1280]{1,0:T(8,128)(2,1)S(1)}, u32[]{:S(2)}, u32[]{:S(2)}) collective-permute-start(bf16[128,1280]{1,0:T(8,128)(2,1)} %pad_maximum_fusion.5), channel_id=1, source_target_pairs={{0,2},{1,3},{2,0},{3,1},{4,6},{5,7},{6,4},{7,5},{8,10},{9,11},{10,... | collective-permute-start | bytes 983048 | tf_op jit(solution)/shard_map/ppermute | solution.py:311
  61.8 14.5 %collective-permute-start.15 = (bf16[128,1280]{1,0:T(8,128)(2,1)}, bf16[128,1280]{1,0:T(8,128)(2,1)S(1)}, u32[]{:S(2)}, u32[]{:S(2)}) collective-permute-start(bf16[128,1280]{1,0:T(8,128)(2,1)} %collective-permute-done.10), channel_id=1, source_target_pairs={{0,4},{1,5},{2,6},{3,7},{4,0},{5,1},{6,2},{7,3},{8,12},{9,13},{10,... | collective-permute-start | bytes 983048 | tf_op jit(solution)/shard_map/ppermute | solution.py:311
  63.0 13.2 %collective-permute-start.17 = (bf16[128,1024]{1,0:T(8,128)(2,1)}, bf16[128,1024]{1,0:T(8,128)(2,1)}, u32[]{:S(2)}, u32[]{:S(2)}) collective-permute-start(bf16[128,1024]{1,0:T(8,128)(2,1)} %param.28), channel_id=1, source_target_pairs={{0,16},{8,24},{16,0},{24,8},{1,17},{9,25},{17,1},{25,9},{2,18},{10... | collective-permute-start | bytes 786440 | tf_op jit(solution)/shard_map/ppermute | solution.py:311
  79.0 14.6 %collective-permute-start.18 = (bf16[256,1280]{1,0:T(8,128)(2,1)S(1)}, bf16[256,1280]{1,0:T(8,128)(2,1)S(1)}, u32[]{:S(2)}, u32[]{:S(2)}) collective-permute-start(bf16[256,1280]{1,0:T(8,128)(2,1)S(1)} %pad_maximum_fusion.2.refs_0_.refs_4_), channel_id=1, source_target_pairs={{0,4},{1,5},{2,6},{3,7},{4,0},{5,1},{6,2},{7,3},{8,12},{9,13},{10,... | collective-permute-start | bytes 1966088 | tf_op jit(solution)/shard_map/ppermute | solution.py:311
  80.3 13.6 %collective-permute-start.19 = (bf16[256,1280]{1,0:T(8,128)(2,1)S(1)}, bf16[256,1280]{1,0:T(8,128)(2,1)S(1)}, u32[]{:S(2)}, u32[]{:S(2)}) collective-permute-start(bf16[256,1280]{1,0:T(8,128)(2,1)S(1)} %constant_dynamic-update-slice_fusion.4.refs_1_.refs_5_), channel_id=1, source_target_pairs={{0,2},{1,3},{2,0},{3,1},{4,6},{5,7},{6,4},{7,5},{8,10},{9,11},{10,... | collective-permute-start | bytes 1966088 | tf_op jit(solution)/shard_map/ppermute | solution.py:311
  93.9 22.5 %collective-permute-start.21 = (bf16[128,2048]{1,0:T(8,128)(2,1)}, bf16[128,2048]{1,0:T(8,128)(2,1)}, u32[]{:S(2)}, u32[]{:S(2)}) collective-permute-start(bf16[128,2048]{1,0:T(8,128)(2,1)} %copy-done.37), channel_id=1, source_target_pairs={{0,2},{1,3},{2,0},{3,1},{4,6},{5,7},{6,4},{7,5},{8,10},{9,11},{10,... | collective-permute-start | bytes 1572872 | tf_op jit(solution)/shard_map/ppermute | solution.py:311
  95.3 21.0 %collective-permute-start.22 = (bf16[128,2048]{1,0:T(8,128)(2,1)}, bf16[128,2048]{1,0:T(8,128)(2,1)}, u32[]{:S(2)}, u32[]{:S(2)}) collective-permute-start(bf16[128,2048]{1,0:T(8,128)(2,1)} %copy-done.38), channel_id=1, source_target_pairs={{0,4},{1,5},{2,6},{3,7},{4,0},{5,1},{6,2},{7,3},{8,12},{9,13},{10,... | collective-permute-start | bytes 1572872 | tf_op jit(solution)/shard_map/ppermute | solution.py:311
  95.7 20.7 %collective-permute-start.23 = (bf16[1024,256]{1,0:T(8,128)(2,1)}, bf16[1024,256]{1,0:T(8,128)(2,1)}, u32[]{:S(2)}, u32[]{:S(2)}) collective-permute-start(bf16[1024,256]{1,0:T(8,128)(2,1)} %collective-permute-done.20.refs_1_), channel_id=1, source_target_pairs={{0,8},{8,16},{16,24},{1,9},{9,17},{17,25},{2,10},{10,18},{18,26},{... | collective-permute-start | bytes 1572872 | tf_op jit(solution)/shard_map/ppermute | solution.py:316
  99.8 18.6 %collective-permute-start.24 = (bf16[1024,256]{1,0:T(8,128)(2,1)}, bf16[1024,256]{1,0:T(8,128)(2,1)}, u32[]{:S(2)}, u32[]{:S(2)}) collective-permute-start(bf16[1024,256]{1,0:T(8,128)(2,1)} %get-tuple-element.641.refs_0_), channel_id=1, source_target_pairs={{0,8},{8,16},{16,24},{1,9},{9,17},{17,25},{2,10},{10,18},{18,26},{... | collective-permute-start | bytes 1572872 | tf_op jit(solution)/shard_map/ppermute | solution.py:316
  121.1 31.6 %collective-permute-start.25 = (bf16[256,2048]{1,0:T(8,128)(2,1)S(1)}, bf16[256,2048]{1,0:T(8,128)(2,1)}, u32[]{:S(2)}, u32[]{:S(2)}) collective-permute-start(bf16[256,2048]{1,0:T(8,128)(2,1)S(1)} %pad_maximum_fusion.refs_0_), channel_id=1, source_target_pairs={{0,4},{1,5},{2,6},{3,7},{4,0},{5,1},{6,2},{7,3},{8,12},{9,13},{10,... | collective-permute-start | bytes 3145736 | tf_op jit(solution)/shard_map/ppermute | solution.py:311
  122.2 30.6 %collective-permute-start.26 = (bf16[256,2048]{1,0:T(8,128)(2,1)S(1)}, bf16[256,2048]{1,0:T(8,128)(2,1)}, u32[]{:S(2)}, u32[]{:S(2)}) collective-permute-start(bf16[256,2048]{1,0:T(8,128)(2,1)S(1)} %constant_dynamic-update-slice_fusion.6.refs_1_), channel_id=1, source_target_pairs={{0,2},{1,3},{2,0},{3,1},{4,6},{5,7},{6,4},{7,5},{8,10},{9,11},{10,... | collective-permute-start | bytes 3145736 | tf_op jit(solution)/shard_map/ppermute | solution.py:311
  127.6 18.3 %collective-permute-start.27 = (bf16[256,1024]{1,0:T(8,128)(2,1)}, bf16[256,1024]{1,0:T(8,128)(2,1)S(1)}, u32[]{:S(2)}, u32[]{:S(2)}) collective-permute-start(bf16[256,1024]{1,0:T(8,128)(2,1)} %get-tuple-element.611), channel_id=1, source_target_pairs={{0,8},{8,0},{16,24},{24,16},{1,9},{9,1},{17,25},{25,17},{2,10},{10... | collective-permute-start | bytes 1572872 | tf_op jit(solution)/shard_map/ppermute | solution.py:311
  129.8 22.9 %collective-permute-start.28 = (bf16[1024,256]{1,0:T(8,128)(2,1)}, bf16[1024,256]{1,0:T(8,128)(2,1)S(1)}, u32[]{:S(2)}, u32[]{:S(2)}) collective-permute-start(bf16[1024,256]{1,0:T(8,128)(2,1)} %collective-permute-done.24.refs_1_), channel_id=1, source_target_pairs={{0,8},{8,16},{16,24},{1,9},{9,17},{17,25},{2,10},{10,18},{18,26},{... | collective-permute-start | bytes 1572872 | tf_op jit(solution)/shard_map/ppermute | solution.py:316
  152.7 26.0 %collective-permute-start.32 = (bf16[1024,512]{1,0:T(8,128)(2,1)}, bf16[1024,512]{1,0:T(8,128)(2,1)}, u32[]{:S(2)}, u32[]{:S(2)}) collective-permute-start(bf16[1024,512]{1,0:T(8,128)(2,1)} %get-tuple-element.676.refs_0_), channel_id=1, source_target_pairs={{0,8},{8,16},{16,24},{1,9},{9,17},{17,25},{2,10},{10,18},{18,26},{... | collective-permute-start | bytes 3145736 | tf_op jit(solution)/shard_map/ppermute | solution.py:316
  157.7 18.6 %collective-permute-start.30 = (bf16[256,1024]{1,0:T(8,128)(2,1)}, bf16[256,1024]{1,0:T(8,128)(2,1)S(1)}, u32[]{:S(2)}, u32[]{:S(2)}) collective-permute-start(bf16[256,1024]{1,0:T(8,128)(2,1)} %get-tuple-element.611), channel_id=1, source_target_pairs={{0,2},{1,3},{2,0},{3,1},{4,6},{5,7},{6,4},{7,5},{8,10},{9,11},{10,... | collective-permute-start | bytes 1572872 | tf_op jit(solution)/shard_map/ppermute | solution.py:311
  158.6 17.7 %collective-permute-start.31 = (bf16[256,1024]{1,0:T(8,128)(2,1)S(1)}, bf16[256,1024]{1,0:T(8,128)(2,1)S(1)}, u32[]{:S(2)}, u32[]{:S(2)}) collective-permute-start(bf16[256,1024]{1,0:T(8,128)(2,1)S(1)} %collective-permute-done.27), channel_id=1, source_target_pairs={{0,4},{1,5},{2,6},{3,7},{4,0},{5,1},{6,2},{7,3},{8,12},{9,13},{10,... | collective-permute-start | bytes 1572872 | tf_op jit(solution)/shard_map/ppermute | solution.py:311
  159.0 17.4 %collective-permute-start.33 = (bf16[1024,256]{1,0:T(8,128)(2,1)}, bf16[1024,256]{1,0:T(8,128)(2,1)S(1)}, u32[]{:S(2)}, u32[]{:S(2)}) collective-permute-start(bf16[1024,256]{1,0:T(8,128)(2,1)} %get-tuple-element.614), channel_id=1, source_target_pairs={{8,0},{16,8},{24,16},{9,1},{17,9},{25,17},{10,2},{18,10},{26,18},{... | collective-permute-start | bytes 1572872 | tf_op jit(solution)/shard_map/ppermute | solution.py:316
  180.7 28.8 %collective-permute-start.34 = (bf16[512,1024]{1,0:T(8,128)(2,1)}, bf16[512,1024]{1,0:T(8,128)(2,1)S(1)}, u32[]{:S(2)}, u32[]{:S(2)}) collective-permute-start(bf16[512,1024]{1,0:T(8,128)(2,1)} %get-tuple-element.746.refs_0_.refs_3_), channel_id=1, source_target_pairs={{0,4},{1,5},{2,6},{3,7},{4,0},{5,1},{6,2},{7,3},{8,12},{9,13},{10,... | collective-permute-start | bytes 3145736 | tf_op jit(solution)/shard_map/ppermute | solution.py:311
  181.0 28.6 %collective-permute-start.35 = (bf16[512,1024]{1,0:T(8,128)(2,1)}, bf16[512,1024]{1,0:T(8,128)(2,1)S(1)}, u32[]{:S(2)}, u32[]{:S(2)}) collective-permute-start(bf16[512,1024]{1,0:T(8,128)(2,1)} %get-tuple-element.747.refs_1_.refs_4_), channel_id=1, source_target_pairs={{0,2},{1,3},{2,0},{3,1},{4,6},{5,7},{6,4},{7,5},{8,10},{9,11},{10,... | collective-permute-start | bytes 3145736 | tf_op jit(solution)/shard_map/ppermute | solution.py:311
  182.0 27.6 %collective-permute-start.36 = (bf16[1024,512]{1,0:T(8,128)(2,1)}, bf16[1024,512]{1,0:T(8,128)(2,1)}, u32[]{:S(2)}, u32[]{:S(2)}) collective-permute-start(bf16[1024,512]{1,0:T(8,128)(2,1)} %collective-permute-done.32.refs_1_), channel_id=1, source_target_pairs={{0,8},{8,16},{16,24},{1,9},{9,17},{17,25},{2,10},{10,18},{18,26},{... | collective-permute-start | bytes 3145736 | tf_op jit(solution)/shard_map/ppermute | solution.py:316
  196.1 13.4 %collective-permute-start.37 = (bf16[1024,256]{1,0:T(8,128)(2,1)}, bf16[1024,256]{1,0:T(8,128)(2,1)S(1)}, u32[]{:S(2)}, u32[]{:S(2)}) collective-permute-start(bf16[1024,256]{1,0:T(8,128)(2,1)} %get-tuple-element.648), channel_id=1, source_target_pairs={{8,0},{16,8},{24,16},{9,1},{17,9},{25,17},{10,2},{18,10},{26,18},{... | collective-permute-start | bytes 1572872 | tf_op jit(solution)/shard_map/ppermute | solution.py:316
  210.7 26.0 %collective-permute-start.38 = (bf16[512,1024]{1,0:T(8,128)(2,1)}, bf16[512,1024]{1,0:T(8,128)(2,1)S(1)}, u32[]{:S(2)}, u32[]{:S(2)}) collective-permute-start(bf16[512,1024]{1,0:T(8,128)(2,1)} %get-tuple-element.669), channel_id=1, source_target_pairs={{0,4},{1,5},{2,6},{3,7},{4,0},{5,1},{6,2},{7,3},{8,12},{9,13},{10,... | collective-permute-start | bytes 3145736 | tf_op jit(solution)/shard_map/ppermute | solution.py:311
  211.8 24.9 %collective-permute-start.39 = (bf16[512,1024]{1,0:T(8,128)(2,1)}, bf16[512,1024]{1,0:T(8,128)(2,1)S(1)}, u32[]{:S(2)}, u32[]{:S(2)}) collective-permute-start(bf16[512,1024]{1,0:T(8,128)(2,1)} %get-tuple-element.670), channel_id=1, source_target_pairs={{0,2},{1,3},{2,0},{3,1},{4,6},{5,7},{6,4},{7,5},{8,10},{9,11},{10,... | collective-permute-start | bytes 3145736 | tf_op jit(solution)/shard_map/ppermute | solution.py:311
  212.4 23.9 %collective-permute-start.41 = (bf16[1024,256]{1,0:T(8,128)(2,1)}, bf16[1024,256]{1,0:T(8,128)(2,1)S(1)}, u32[]{:S(2)}, u32[]{:S(2)}) collective-permute-start(bf16[1024,256]{1,0:T(8,128)(2,1)} %add_convert_fusion.9), channel_id=1, source_target_pairs={{8,0},{16,8},{24,16},{9,1},{17,9},{25,17},{10,2},{18,10},{26,18},{... | collective-permute-start | bytes 1572872 | tf_op jit(solution)/shard_map/ppermute | solution.py:316
  213.7 23.0 %collective-permute-start.40 = (bf16[1024,256]{1,0:T(8,128)(2,1)}, bf16[1024,256]{1,0:T(8,128)(2,1)S(1)}, u32[]{:S(2)}, u32[]{:S(2)}) collective-permute-start(bf16[1024,256]{1,0:T(8,128)(2,1)} %add_convert_fusion.8), channel_id=1, source_target_pairs={{8,0},{16,8},{24,16},{9,1},{17,9},{25,17},{10,2},{18,10},{26,18},{... | collective-permute-start | bytes 1572872 | tf_op jit(solution)/shard_map/ppermute | solution.py:316
  241.2 18.8 %collective-permute-start.43 = (bf16[256,1024]{1,0:T(8,128)(2,1)}, bf16[256,1024]{1,0:T(8,128)(2,1)}, u32[]{:S(2)}, u32[]{:S(2)}) collective-permute-start(bf16[256,1024]{1,0:T(8,128)(2,1)} %add_convert_fusion.6), channel_id=1, source_target_pairs={{0,4},{1,5},{2,6},{3,7},{4,0},{5,1},{6,2},{7,3},{8,12},{9,13},{10,... | collective-permute-start | bytes 1572872 | tf_op jit(solution)/shard_map/ppermute | solution.py:311
  241.6 35.1 %collective-permute-start.45 = (bf16[1024,512]{1,0:T(8,128)(2,1)}, bf16[1024,512]{1,0:T(8,128)(2,1)S(1)}, u32[]{:S(2)}, u32[]{:S(2)}) collective-permute-start(bf16[1024,512]{1,0:T(8,128)(2,1)} %get-tuple-element.683), channel_id=1, source_target_pairs={{8,0},{16,8},{24,16},{9,1},{17,9},{25,17},{10,2},{18,10},{26,18},{... | collective-permute-start | bytes 3145736 | tf_op jit(solution)/shard_map/ppermute | solution.py:316
  242.9 33.8 %collective-permute-start.42 = (bf16[256,1024]{1,0:T(8,128)(2,1)}, bf16[256,1024]{1,0:T(8,128)(2,1)}, u32[]{:S(2)}, u32[]{:S(2)}) collective-permute-start(bf16[256,1024]{1,0:T(8,128)(2,1)} %add_convert_fusion.7), channel_id=1, source_target_pairs={{0,2},{1,3},{2,0},{3,1},{4,6},{5,7},{6,4},{7,5},{8,10},{9,11},{10,... | collective-permute-start | bytes 1572872 | tf_op jit(solution)/shard_map/ppermute | solution.py:311
  243.8 21.6 %collective-permute-start.44 = (bf16[256,1024]{1,0:T(8,128)(2,1)}, bf16[256,1024]{1,0:T(8,128)(2,1)}, u32[]{:S(2)}, u32[]{:S(2)}) collective-permute-start(bf16[256,1024]{1,0:T(8,128)(2,1)} %get-tuple-element.704), channel_id=1, source_target_pairs={{0,1},{1,0},{2,3},{3,2},{4,5},{5,4},{6,7},{7,6},{8,9},{9,8},{10,11... | collective-permute-start | bytes 1572872 | tf_op jit(solution)/shard_map/ppermute | solution.py:311
  262.3 15.8 %collective-permute-start.46 = (bf16[256,1024]{1,0:T(8,128)(2,1)}, bf16[256,1024]{1,0:T(8,128)(2,1)S(1)}, u32[]{:S(2)}, u32[]{:S(2)}) collective-permute-start(bf16[256,1024]{1,0:T(8,128)(2,1)} %add_convert_fusion.5), channel_id=1, source_target_pairs={{0,8},{8,0},{16,24},{24,16},{1,9},{9,1},{17,25},{25,17},{2,10},{10... | collective-permute-start | bytes 1572872 | tf_op jit(solution)/shard_map/ppermute | solution.py:311
  280.2 26.7 %collective-permute-start.47 = (bf16[256,2560]{1,0:T(8,128)(2,1)}, bf16[256,2560]{1,0:T(8,128)(2,1)S(1)}, u32[]{:S(2)}, u32[]{:S(2)}) collective-permute-start(bf16[256,2560]{1,0:T(8,128)(2,1)} %get-tuple-element.737), channel_id=1, source_target_pairs={{0,4},{1,5},{2,6},{3,7},{4,0},{5,1},{6,2},{7,3},{8,12},{9,13},{10,... | collective-permute-start | bytes 3932168 | tf_op jit(solution)/shard_map/ppermute | solution.py:311
  281.3 26.4 %collective-permute-start.48 = (bf16[256,2560]{1,0:T(8,128)(2,1)}, bf16[256,2560]{1,0:T(8,128)(2,1)S(1)}, u32[]{:S(2)}, u32[]{:S(2)}) collective-permute-start(bf16[256,2560]{1,0:T(8,128)(2,1)} %get-tuple-element.738), channel_id=1, source_target_pairs={{0,2},{1,3},{2,0},{3,1},{4,6},{5,7},{6,4},{7,5},{8,10},{9,11},{10,... | collective-permute-start | bytes 3932168 | tf_op jit(solution)/shard_map/ppermute | solution.py:311
  281.8 25.0 %collective-permute-start.49 = (bf16[1024,512]{1,0:T(8,128)(2,1)}, bf16[1024,512]{1,0:T(8,128)(2,1)}, u32[]{:S(2)}, u32[]{:S(2)}) collective-permute-start(bf16[1024,512]{1,0:T(8,128)(2,1)} %add_convert_fusion.1), channel_id=1, source_target_pairs={{8,0},{16,8},{24,16},{9,1},{17,9},{25,17},{10,2},{18,10},{26,18},{... | collective-permute-start | bytes 3145736 | tf_op jit(solution)/shard_map/ppermute | solution.py:316
  309.7 22.7 %collective-permute-start.53 = (f32[512,1024]{1,0:T(8,128)}, f32[512,1024]{1,0:T(8,128)S(1)}, u32[]{:S(2)}, u32[]{:S(2)}) collective-permute-start(f32[512,1024]{1,0:T(8,128)} %get-tuple-element.779), channel_id=1, source_target_pairs={{0,1},{1,0},{2,3},{3,2},{4,5},{5,4},{6,7},{7,6},{8,9},{9,8},{10,11... | collective-permute-start | bytes 6291464 | tf_op jit(solution)/shard_map/ppermute | solution.py:311
  314.7 17.7 %collective-permute-start.50 = (bf16[128,2560]{1,0:T(8,128)(2,1)}, bf16[128,2560]{1,0:T(8,128)(2,1)}, u32[]{:S(2)}, u32[]{:S(2)}) collective-permute-start(bf16[128,2560]{1,0:T(8,128)(2,1)} %add_convert_fusion.4), channel_id=1, source_target_pairs={{0,2},{1,3},{2,0},{3,1},{4,6},{5,7},{6,4},{7,5},{8,10},{9,11},{10,... | collective-permute-start | bytes 1966088 | tf_op jit(solution)/shard_map/ppermute | solution.py:311
  315.2 17.2 %collective-permute-start.51 = (bf16[128,2560]{1,0:T(8,128)(2,1)}, bf16[128,2560]{1,0:T(8,128)(2,1)}, u32[]{:S(2)}, u32[]{:S(2)}) collective-permute-start(bf16[128,2560]{1,0:T(8,128)(2,1)} %add_convert_fusion.3), channel_id=1, source_target_pairs={{0,4},{1,5},{2,6},{3,7},{4,0},{5,1},{6,2},{7,3},{8,12},{9,13},{10,... | collective-permute-start | bytes 1966088 | tf_op jit(solution)/shard_map/ppermute | solution.py:311
  315.6 16.8 %collective-permute-start.52 = (bf16[128,1024]{1,0:T(8,128)(2,1)}, bf16[128,1024]{1,0:T(8,128)(2,1)}, u32[]{:S(2)}, u32[]{:S(2)}) collective-permute-start(bf16[128,1024]{1,0:T(8,128)(2,1)} %add_convert_fusion.14), channel_id=1, source_target_pairs={{0,16},{8,24},{16,0},{24,8},{1,17},{9,25},{17,1},{25,9},{2,18},{10... | collective-permute-start | bytes 786440 | tf_op jit(solution)/shard_map/ppermute | solution.py:311
  332.4 20.4 %collective-permute-start.54 = (bf16[256,1536]{1,0:T(8,128)(2,1)}, bf16[256,1536]{1,0:T(8,128)(2,1)}, u32[]{:S(2)}, u32[]{:S(2)}) collective-permute-start(bf16[256,1536]{1,0:T(8,128)(2,1)} %get-tuple-element.811), channel_id=1, source_target_pairs={{0,4},{1,5},{2,6},{3,7},{4,0},{5,1},{6,2},{7,3},{8,12},{9,13},{10,... | collective-permute-start | bytes 2359304 | tf_op jit(solution)/shard_map/ppermute | solution.py:311
  333.6 19.1 %collective-permute-start.55 = (bf16[256,1536]{1,0:T(8,128)(2,1)}, bf16[256,1536]{1,0:T(8,128)(2,1)}, u32[]{:S(2)}, u32[]{:S(2)}) collective-permute-start(bf16[256,1536]{1,0:T(8,128)(2,1)} %get-tuple-element.812), channel_id=1, source_target_pairs={{0,2},{1,3},{2,0},{3,1},{4,6},{5,7},{6,4},{7,5},{8,10},{9,11},{10,... | collective-permute-start | bytes 2359304 | tf_op jit(solution)/shard_map/ppermute | solution.py:311
  336.9 15.8 %collective-permute-start.56 = (bf16[128,2560]{1,0:T(8,128)(2,1)}, bf16[128,2560]{1,0:T(8,128)(2,1)S(1)}, u32[]{:S(2)}, u32[]{:S(2)}) collective-permute-start(bf16[128,2560]{1,0:T(8,128)(2,1)} %add_convert_fusion.2), channel_id=1, source_target_pairs={{0,8},{8,0},{16,24},{24,16},{1,9},{9,1},{17,25},{25,17},{2,10},{10... | collective-permute-start | bytes 1966088 | tf_op jit(solution)/shard_map/ppermute | solution.py:311
  360.2 17.9 %collective-permute-start.57 = (bf16[128,1536]{1,0:T(8,128)(2,1)}, bf16[128,1536]{1,0:T(8,128)(2,1)}, u32[]{:S(2)}, u32[]{:S(2)}) collective-permute-start(bf16[128,1536]{1,0:T(8,128)(2,1)} %add_convert_fusion.12), channel_id=1, source_target_pairs={{0,2},{1,3},{2,0},{3,1},{4,6},{5,7},{6,4},{7,5},{8,10},{9,11},{10,... | collective-permute-start | bytes 1179656 | tf_op jit(solution)/shard_map/ppermute | solution.py:311
  360.8 17.3 %collective-permute-start.58 = (bf16[128,1536]{1,0:T(8,128)(2,1)S(1)}, bf16[128,1536]{1,0:T(8,128)(2,1)}, u32[]{:S(2)}, u32[]{:S(2)}) collective-permute-start(bf16[128,1536]{1,0:T(8,128)(2,1)S(1)} %add_convert_fusion.11), channel_id=1, source_target_pairs={{0,4},{1,5},{2,6},{3,7},{4,0},{5,1},{6,2},{7,3},{8,12},{9,13},{10,... | collective-permute-start | bytes 1179656 | tf_op jit(solution)/shard_map/ppermute | solution.py:311
  361.1 17.0 %collective-permute-start.59 = (bf16[64,2560]{1,0:T(8,128)(2,1)}, bf16[64,2560]{1,0:T(8,128)(2,1)}, u32[]{:S(2)}, u32[]{:S(2)}) collective-permute-start(bf16[64,2560]{1,0:T(8,128)(2,1)} %add_convert_fusion.13), channel_id=1, source_target_pairs={{0,16},{8,24},{16,0},{24,8},{1,17},{9,25},{17,1},{25,9},{2,18},{10... | collective-permute-start | bytes 983048 | tf_op jit(solution)/shard_map/ppermute | solution.py:311
  393.4 12.2 %collective-permute-start.65 = (bf16[64,1536]{1,0:T(8,128)(2,1)S(1)}, bf16[64,1536]{1,0:T(8,128)(2,1)S(1)}, u32[]{:S(2)}, u32[]{:S(2)}) collective-permute-start(bf16[64,1536]{1,0:T(8,128)(2,1)S(1)} %add_convert_fusion.15), channel_id=1, source_target_pairs={{0,16},{8,24},{16,0},{24,8},{1,17},{9,25},{17,1},{25,9},{2,18},{10... | collective-permute-start | bytes 589832 | tf_op jit(solution)/shard_map/ppermute | solution.py:311
  (81 other events, 835.4 us)

commit v2 on v1

--- a/solution.py
+++ b/solution.py
@@ -1394,7 +1394,7 @@
     clock = Clock(jnp.stack([me, core]).astype(jnp.int32))
     box = {}
 
-    waiting = []
+    waiting, deferred = [], []
 
     def slot(jobs, work=None, *inputs, chain=None, late=(), then=None):
         nonlocal waiting
@@ -1410,6 +1410,10 @@
             for job, value in list(zip(jobs, values)) + waiting:
                 if job[1] == name:
                     after.append(follow(value, *inputs))
+        for job, value in deferred:
+            late.append(job)
+            values.append(value)
+        deferred.clear()
         if then is not None:
             started = then(made)
             late = late + started
@@ -1456,22 +1460,20 @@
     line_d = Gather(fc_out_weight)
     slot(moves(line_a, "near") + moves(line_b, "far") + [core_move("in", in_give), core_move("g", g_own)])
     g_more = box["g"]
-    bias, *tables = slot(
-        moves(line_a, "first") + moves(line_b, "near"),
-        lambda a, b: marks(clock.token, a, b),
-        line_a.parts["a"],
-        line_a.parts["b"],
-    )
+    slot(moves(line_a, "first") + moves(line_b, "near"))
     line_c = Gather(joined(in_keep, box["in"]))
-    (xhat, inv_std), grad_sum = slot(
+    (xhat, inv_std), grad_sum, (bias, *tables) = slot(
         moves(line_a, "second") + moves(line_c, "far"),
-        lambda own, other, g: (
+        lambda own, other, g, a, b: (
             prepare(clock.token, own, other),
             jnp.sum(g.astype(F32), axis=0),
+            marks(clock.token, a, b),
         ),
         x_own,
         box["x"],
         g_own,
+        line_a.parts["a"],
+        line_a.parts["b"],
     )
     a_pieces = line_a.pieces()
     made = slot(
@@ -1624,25 +1626,35 @@
         projected_grad, total = unturn(tables, triples)
         return projected_grad, total, row_grads(clock.token, normed_t, projected_grad)
 
-    projected_grad, qkv_bias_sum, parts = slot(
+    def near_soon(*terms):
+        deferred.append(((sum_in.parts, "r_b"), near_now(*terms)))
+        return ()
+
+    def far_soon(last, *terms):
+        rows = last.shape[0]
+        total = sum(term[rows // 2 : rows].astype(F32) for term in terms + (last,))
+        deferred.append(((sum_in.parts, "r_far"), cross(total.astype(BF), FAR)))
+        return ()
+
+    (projected_grad, qkv_bias_sum, parts), _ = slot(
         moves(sum_in, "second") + moves(sum_fc, "far") + [core_move("out_side", out_theirs)],
         last_grads,
         normed_t,
         tables,
         [(results[group][1], results[group][2], backs[group, 1]) for group in range(3)],
+        chain=[("r_yb", near_soon, (sum_in.parts["b"], sum_in.parts["r_xby"]))],
     )
     sum_qkv = Scatter(parts)
-    (norm_mine, norm_theirs), sum_in.parts["r_b"] = slot(
+    (norm_mine, norm_theirs), _ = slot(
         moves(sum_qkv, "first"),
-        lambda projected_grad, earlier, terms, *lines: (
-            norm_grad(projected_grad, lines, [(0, 768), (512, 1280)], earlier),
-            near_now(*terms),
+        lambda projected_grad, earlier, *lines: norm_grad(
+            projected_grad, lines, [(0, 768), (512, 1280)], earlier
         ),
         projected_grad,
         earlier,
-        tuple(sum_in.parts[name] for name in ("r_yb", "b", "r_xby")),
         a_pieces,
         b_pieces,
+        chain=[("r_b", far_soon, [sum_in.parts[name] for name in ("a", "r_yax", "r_xa")])],
     )
 
     def finish_output(x_own, out_mine, out_more, b_rows):
@@ -1669,7 +1681,8 @@
             ],
             axis=1,
         ).reshape(CHIPS, -1)
-        return packed[jnp.asarray(np.array(ORDER, np.int32)) ^ me]
+        order = [NEAR * (i % 2) + FAR * (i // 2 % 2) + i // 4 % 2 + Y * (i // 8) for i in range(CHIPS)]
+        return packed[jnp.asarray(np.array(order, np.int32)) ^ me]
 
     def back_work(norm_more, norm_mine, xhat, inv_std, gain, g_own, *sums):
         input_grad, norm_sums = norm_back(
@@ -1678,7 +1691,7 @@
         return input_grad, small_rows(norm_sums, *sums)
 
     _, (input_grad, packed) = slot(
-        moves(sum_qkv, "second") + moves(sum_in, "far") + [core_move("norm", norm_theirs)],
+        moves(sum_qkv, "second") + [core_move("norm", norm_theirs)],
         chain=(
             "norm",
             back_work,
@@ -1710,14 +1723,14 @@
         chain=("fold", two_folds, (packed,)),
     )
     fc_in_weight_grad = slot(
-        moves(sum_qkv, "far") + [fold(NEAR)],
+        moves(sum_qkv, "far") + [fold(FAR)],
         lambda mine, other: paste(paste_in_kernel, clock.token, mine, other),
         in_keep,
         box["in_rows"],
     )
     packed = half_sum()
     qkv_keep, qkv_give = pick(sum_qkv.result().reshape(2, d_rows, -1))
-    slot([core_move("qkv_rows", qkv_give), fold(FAR)])
+    slot([core_move("qkv_rows", qkv_give), fold(NEAR)])
     sums_keep, sums_give = pick(half_sum().reshape(2, -1))
     sums = sums_keep + other_core(sums_give)
     parts = []

time: 421 us -> 415 us (0.986)
    ppermute x58, waiting for transfers between devices: 41.8 us -> 47.6 us  [swap(): lax.ppermute(value, axis, [(i, i ^ bit) for i in range(lax.axis_size(axis...]
    unnamed x124 -> x104, local copies, waits for them, and re-layouts: 11.5 us -> 9.21 us
  transfers between devices with their start and end apart: 70 -> 70, of which waited for: 25 -> 27; matrix products, arithmetic and copies ran while one was open for 7% -> 8% of each run, Pallas kernels for 42% -> 43%
where the time goes in v2:
time: 415 us; the launch traced here: 412 us
  Pallas kernels  178 us (43%)
  starting transfers between devices  103 us (25%)
  waiting for transfers between devices  63.6 us (15%)
  other arithmetic  44.9 us (11%)
  local copies, waits for them, and re-layouts  20.9 us (5%)
    ppermute x58, starting transfers between devices, swap(): lax.ppermute(value, axis, [(i, i ^ bit) for i in range(lax.axis_size(axis...  77.1 us
    ppermute x58, waiting for transfers between devices, swap(): lax.ppermute(value, axis, [(i, i ^ bit) for i in range(lax.axis_size(axis...  47.6 us
    pallas_call x3, Pallas kernels, attend(): pl.pallas_call(attend_kernel, grid=(4, pairs), out_shape=(shaped(1024, 12...  34.4 us
    ppermute x12, starting transfers between devices, shift(): lax.ppermute(value, 'seq', [(i, i + by) for i in range(count) if 0 <= i +...  26.1 us
    pallas_call x2, Pallas kernels, norm_grad(): pl.pallas_call(partial(norm_grad_kernel, spans), grid=(4,), out_shape=(sh...  19.2 us
    pallas_call x2, Pallas kernels, row_grads(): pl.pallas_call(partial(row_grads_kernel, steps), grid=(columns // step,),...  16.2 us
    ppermute x12, waiting for transfers between devices, shift(): lax.ppermute(value, 'seq', [(i, i + by) for i in range(count) if 0 <= i +...  16 us
    pallas_call x1, Pallas kernels, hidden(): pl.pallas_call(hidden_kernel, grid=(width // step,), out_shape=(shaped(ro...  15 us
  transfers between devices with their start and end apart: 70, of which 27 were waited for; matrix products, arithmetic and copies ran while one was open for 8% of the time, Pallas kernels for 43%

profile of v2, /device:TPU:1, one launch (start us, length us, event | category | flops | bytes accessed | tf_op | source)
XLA Modules:
  0.0 412.4 jit_solution(5189818577020586655)
XLA Ops:
  5.9 3.7 collective-permute-start.1
  11.0 4.3 %collective-permute-done.1 = bf16[64,896]{1,0:T(8,128)(2,1)S(1)} collective-permute-done((bf16[64,896]{1,0:T(8,128)(2,1)S(1)}, bf16[64,896]{1,0:T(8,128)(2,1)S(1)}, u32[]{:S(2)}, u32[]{:S(2)}) %collective-permute-start.1) | collective-permute-done | bytes 114720 | tf_op jit(solution)/shard_map/ppermute | solution.py:311
  18.4 3.1 collective-permute-start.5
  23.3 3.6 collective-permute-done.5
  32.1 2.2 collective-permute-start.10
  36.8 4.4 %collective-permute-done.10 = bf16[128,1280]{1,0:T(8,128)(2,1)} collective-permute-done((bf16[128,1280]{1,0:T(8,128)(2,1)S(1)}, bf16[128,1280]{1,0:T(8,128)(2,1)}, u32[]{:S(2)}, u32[]{:S(2)}) %collective-permute-start.10) | collective-permute-done | bytes 327712 | tf_op jit(solution)/shard_map/ppermute | solution.py:311
  43.0 5.0 %marks.1 = (f32[4,768,256]{2,1,0:T(8,128)}, f32[1024,128]{1,0:T(8,128)}, f32[1024,128]{1,0:T(8,128)}, f32[1024,128]{1,0:T(8,128)}) custom-call(s32[2]{0:T(128)} %pad_add_fusion.where_ref, bf16[128,896]{1,0:T(8,128)(2,1)} %copy-done.14, bf16[128,896]{1,0:T(8,128)(2,1)} %copy-done.15, f32[1,128]{1,0:T(1,128)} %bitcast.41, f32[1,128]{1,0:T(1,128)} %constant.130.clone.forth_ref, ...), custom_call_target="tpu_custom_call" | custom-call | flops 13107200 | bytes 4194304 | tf_op jit(solution)/shard_map/marks/pallas_call | solution.py:586
  48.0 7.2 %prepare.1 = (f32[1024,1024]{1,0:T(8,128)}, f32[1024,1]{1,0:T(8,128)}) custom-call(s32[2]{0:T(128)} %pad_add_fusion.where_ref, bf16[512,1024]{1,0:T(8,128)(2,1)} %bitcast.31, bf16[512,1024]{1,0:T(8,128)(2,1)} %collective-permute-done.2.other_ref), custom_call_target="tpu_custom_call" | custom-call | flops 2147483648 | bytes 8388608 | tf_op jit(solution)/shard_map/prepare/pallas_call | solution.py:644
  62.1 7.9 %project_first.1 = (bf16[1024,128]{1,0:T(8,128)(2,1)}, bf16[1024,256]{1,0:T(8,128)(2,1)}, bf16[1024,128]{1,0:T(8,128)(2,1)}, bf16[1024,256]{1,0:T(8,128)(2,1)}, ...) custom-call(s32[2]{0:T(128)} %pad_add_fusion.where_ref, ...), custom_call_target="tpu_custom_call" | custom-call | flops 1610612736 | bytes 12582912 | tf_op jit(solution)/shard_map/project_first/pallas_call | solution.py:728
  70.2 3.5 collective-permute-done.16
  78.9 2.1 collective-permute-start.20
  81.0 6.4 %collective-permute-done.20.refs_1_ = bf16[1024,256]{1,0:T(8,128)(2,1)} collective-permute-done((bf16[1024,256]{1,0:T(8,128)(2,1)}, bf16[1024,256]{1,0:T(8,128)(2,1)}, u32[]{:S(2)}, u32[]{:S(2)}) %collective-permute-start.20) | collective-permute-done | bytes 524320 | tf_op jit(solution)/shard_map/ppermute | solution.py:316
  102.6 2.3 head_rows.1
  105.0 6.4 %project_more.1 = (bf16[1024,256]{1,0:T(8,128)(2,1)}, bf16[1024,512]{1,0:T(8,128)(2,1)}) custom-call(bf16[1024,1024]{1,0:T(8,128)(2,1)} %get-tuple-element.615.normed_ref, f32[1,768]{1,0:T(1,128)} %get-tuple-element.560.bias_ref, f32[1024,128]{1,0:T(8,128)} %get-tuple-element.781.cos_ref, f32[1024,128]{1,0:T(8,128)} %get-tuple-element.782.forth_ref, ...), custom_call_target="tpu_custom_call" | custom-call | flops 1610612736 | bytes 6291456 | tf_op jit(solution)/shard_map/project_more/pallas_call | solution.py:752
  116.1 6.2 %collective-permute-start.29 = (bf16[256,1024]{1,0:T(8,128)(2,1)S(1)}, bf16[256,1024]{1,0:T(8,128)(2,1)}, u32[]{:S(2)}, u32[]{:S(2)}) collective-permute-start(bf16[256,1024]{1,0:T(8,128)(2,1)S(1)} %copy-done.46), channel_id=1, source_target_pairs={{0,1},{1,0},{2,3},{3,2},{4,5},{5,4},{6,7},{7,6},{8,9},{9,8},{10,11... | collective-permute-start | bytes 1572872 | tf_op jit(solution)/shard_map/ppermute | solution.py:311
  122.3 2.2 collective-permute-start.27
  126.5 5.1 %context_grad.1 = (bf16[1024,512]{1,0:T(8,128)(2,1)}, bf16[512,1024]{1,0:T(8,128)(2,1)}) custom-call(s32[2]{0:T(128)} %pad_add_fusion.where_ref, bf16[512,1024]{1,0:T(8,128)(2,1)} %bitcast.24, bf16[512,1024]{1,0:T(8,128)(2,1)} %collective-permute-done.7.other_ref.refs_5_, bf16[256,1024]{1,0:T(8,128)(2,1)} %get-tuple-element.591.keep_ref, ...), custom_call_target="tpu_custom_call" | custom-call | flops 1073741824 | bytes 6291456 | tf_op jit(solution)/shard_map/context_grad/pallas_call | solution.py:818
  131.6 9.1 %attend.3 = (bf16[1024,128]{1,0:T(8,128)(2,1)}, bf16[1024,128]{1,0:T(8,128)(2,1)}, f32[1024,256]{1,0:T(8,128)}, bf16[1024,256]{1,0:T(8,128)(2,1)}, bf16[1024,256]{1,0:T(8,128)(2,1)}) custom-call(bf16[1024,128]{1,0:T(8,128)(2,1)} %get-tuple-element.594.q_ref, bf16[1024,512]{1,0:T(8,128)(2,1)} %get-tuple-element.674.do_ref, ...), custom_call_target="tpu_custom_call" | custom-call | flops 2415919104 | bytes 9437184 | tf_op jit(solution)/shard_map/attend/pallas_call | solution.py:900
  140.7 6.8 %collective-permute-done.28.refs_2_ = bf16[1024,256]{1,0:T(8,128)(2,1)S(1)} collective-permute-done((bf16[1024,256]{1,0:T(8,128)(2,1)}, bf16[1024,256]{1,0:T(8,128)(2,1)S(1)}, u32[]{:S(2)}, u32[]{:S(2)}) %collective-permute-start.28) | collective-permute-done | bytes 524320 | tf_op jit(solution)/shard_map/ppermute | solution.py:316
  147.4 5.0 %collective-permute-start.32 = (bf16[1024,512]{1,0:T(8,128)(2,1)}, bf16[1024,512]{1,0:T(8,128)(2,1)}, u32[]{:S(2)}, u32[]{:S(2)}) collective-permute-start(bf16[1024,512]{1,0:T(8,128)(2,1)} %get-tuple-element.676.refs_0_), channel_id=1, source_target_pairs={{0,8},{8,16},{16,24},{1,9},{9,17},{17,25},{2,10},{10,18},{18,26},{... | collective-permute-start | bytes 3145736 | tf_op jit(solution)/shard_map/ppermute | solution.py:316
  156.4 15.0 %hidden.1 = (bf16[1024,2048]{1,0:T(8,128)(2,1)}, bf16[2048,1024]{1,0:T(8,128)(2,1)}, f32[1024,2048]{1,0:T(8,128)}) custom-call(bf16[1024,1024]{1,0:T(8,128)(2,1)} %get-tuple-element.615.normed_ref, f32[1,2048]{1,0:T(1,128)} %get-tuple-element.616.bias_ref, bf16[256,2048]{1,0:T(8,128)(2,1)} %copy-done.12, bf16[256,2048]{1,0:T(8,128)(2,1)} %copy-done.35, ...), custom_call_target="tpu_custom_call" | custom-call | flops 4399824896 | bytes 18874368 | tf_op jit(solution)/shard_map/hidden/pallas_call | solution.py:1000
  177.3 5.1 %collective-permute-start.36 = (bf16[1024,512]{1,0:T(8,128)(2,1)}, bf16[1024,512]{1,0:T(8,128)(2,1)}, u32[]{:S(2)}, u32[]{:S(2)}) collective-permute-start(bf16[1024,512]{1,0:T(8,128)(2,1)} %collective-permute-done.32.refs_1_), channel_id=1, source_target_pairs={{0,8},{8,16},{16,24},{1,9},{9,17},{17,25},{2,10},{10,18},{18,26},{... | collective-permute-start | bytes 3145736 | tf_op jit(solution)/shard_map/ppermute | solution.py:316
  182.3 9.0 %attend.4 = (bf16[1024,128]{1,0:T(8,128)(2,1)}, bf16[1024,128]{1,0:T(8,128)(2,1)}, f32[1024,256]{1,0:T(8,128)}, bf16[1024,256]{1,0:T(8,128)(2,1)}, bf16[1024,256]{1,0:T(8,128)(2,1)}) custom-call(bf16[1024,128]{1,0:T(8,128)(2,1)} %get-tuple-element.638.q_ref, bf16[1024,512]{1,0:T(8,128)(2,1)} %get-tuple-element.674.do_ref, ...), custom_call_target="tpu_custom_call" | custom-call | flops 2415919104 | bytes 9437184 | tf_op jit(solution)/shard_map/attend/pallas_call | solution.py:900
  193.2 11.5 %unit_grads.1 = (bf16[256,1024]{1,0:T(8,128)(2,1)}, bf16[256,1024]{1,0:T(8,128)(2,1)}, bf16[256,1024]{1,0:T(8,128)(2,1)}, bf16[256,1024]{1,0:T(8,128)(2,1)}, bf1...) custom-call(s32[16]{0:T(128)} %broadcast_xor_fusion.order_ref, ...), custom_call_target="tpu_custom_call" | custom-call | flops 4294967296 | bytes 8388608 | tf_op jit(solution)/shard_map/unit_grads/pallas_call | solution.py:1192
  209.7 16.3 %attend.5 = (bf16[1024,256]{1,0:T(8,128)(2,1)}, bf16[1024,256]{1,0:T(8,128)(2,1)}, f32[1024,512]{1,0:T(8,128)}, bf16[1024,512]{1,0:T(8,128)(2,1)}, bf16[1024,512]{1,0:T(8,128)(2,1)}) custom-call(bf16[1024,256]{1,0:T(8,128)(2,1)} %get-tuple-element.673.q_ref, bf16[1024,512]{1,0:T(8,128)(2,1)} %get-tuple-element.674.do_ref, ...), custom_call_target="tpu_custom_call" | custom-call | flops 4831838208 | bytes 18874368 | tf_op jit(solution)/shard_map/attend/pallas_call | solution.py:900
  226.0 5.1 %out_grad.1 = (bf16[256,1024]{1,0:T(8,128)(2,1)}, bf16[256,1024]{1,0:T(8,128)(2,1)}) custom-call(s32[2]{0:T(128)} %pad_add_fusion.where_ref, bf16[512,1024]{1,0:T(8,128)(2,1)} %bitcast.26, bf16[512,1024]{1,0:T(8,128)(2,1)} %collective-permute-done.7.other_ref.refs_5_, bf16[1024,128]{1,0:T(8,128)(2,1)} %get-tuple-element.743.refs_0_, ...), custom_call_target="tpu_custom_call" | custom-call | flops 1073741824 | bytes 6291456 | tf_op jit(solution)/shard_map/out_grad/pallas_call | solution.py:1234
  231.4 2.4 add_convert_fusion.7
  239.0 4.6 %collective-permute-start.44 = (bf16[256,1024]{1,0:T(8,128)(2,1)}, bf16[256,1024]{1,0:T(8,128)(2,1)}, u32[]{:S(2)}, u32[]{:S(2)}) collective-permute-start(bf16[256,1024]{1,0:T(8,128)(2,1)} %get-tuple-element.704), channel_id=1, source_target_pairs={{0,1},{1,0},{2,3},{3,2},{4,5},{5,4},{6,7},{7,6},{8,9},{9,8},{10,11... | collective-permute-start | bytes 1572872 | tf_op jit(solution)/shard_map/ppermute | solution.py:311
  243.6 11.6 %unit_back.1 = (bf16[1024,2048]{1,0:T(8,128)(2,1)}, f32[1,2048]{1,0:T(1,128)}) custom-call(s32[2]{0:T(128)} %pad_add_fusion.where_ref, bf16[512,1024]{1,0:T(8,128)(2,1)} %bitcast.27, bf16[512,1024]{1,0:T(8,128)(2,1)} %collective-permute-done.7.other_ref.refs_5_, f32[1024,2048]{1,0:T(8,128)} %get-tuple-element.708.slope_ref, ...), custom_call_target="tpu_custom_call" | custom-call | flops 4294967296 | bytes 16777216 | tf_op jit(solution)/shard_map/unit_back/pallas_call | solution.py:1056
  255.3 2.3 add_convert_fusion.5
  257.6 3.0 collective-permute-start.46
  262.7 9.2 %row_grads.2 = (bf16[128,2560]{1,0:T(8,128)(2,1)}, bf16[128,2560]{1,0:T(8,128)(2,1)}, bf16[128,2560]{1,0:T(8,128)(2,1)}, bf16[128,2560]{1,0:T(8,128)(2,1)}, bf16...) custom-call(s32[2]{0:T(128)} %pad_add_fusion.where_ref, bf16[1024,1024]{1,0:T(8,128)(2,1)} %get-tuple-element.796.left_ref, ...), custom_call_target="tpu_custom_call" | custom-call | flops 5368709120 | bytes 7340032 | tf_op jit(solution)/shard_map/row_grads/pallas_call | solution.py:1145
  280.6 9.5 %norm_grad.2 = (f32[512,1024]{1,0:T(8,128)}, f32[512,1024]{1,0:T(8,128)}) custom-call(bf16[1024,2048]{1,0:T(8,128)(2,1)} %get-tuple-element.752.right_ref.left_ref, bf16[256,2048]{1,0:T(8,128)(2,1)} %copy-done.12, bf16[256,2048]{1,0:T(8,128)(2,1)} %copy-done.35, bf16[256,2048]{1,0:T(8,128)(2,1)} %collective-permute-done.25.refs_2_, ...), custom_call_target="tpu_custom_call" | custom-call | flops 4294967296 | bytes 12582912 | tf_op jit(solution)/shard_map/norm_grad/pallas_call | solution.py:1283
  290.1 11.9 %unit_out.1 = (f32[512,1024]{1,0:T(8,128)}, f32[512,1024]{1,0:T(8,128)}) custom-call(s32[2]{0:T(128)} %pad_add_fusion.where_ref, bf16[1024,2048]{1,0:T(8,128)(2,1)} %get-tuple-element.741.act_ref, bf16[512,1024]{1,0:T(8,128)(2,1)} %get-tuple-element.742.heads_ref, bf16[1024,128]{1,0:T(8,128)(2,1)} %get-tuple-element.743.refs_0_, ...), custom_call_target="tpu_custom_call" | custom-call | flops 6442450944 | bytes 12582912 | tf_op jit(solution)/shard_map/unit_out/pallas_call | solution.py:1092
  305.5 4.4 %collective-permute-start.53 = (f32[512,1024]{1,0:T(8,128)}, f32[512,1024]{1,0:T(8,128)S(1)}, u32[]{:S(2)}, u32[]{:S(2)}) collective-permute-start(f32[512,1024]{1,0:T(8,128)} %get-tuple-element.780), channel_id=1, source_target_pairs={{0,1},{1,0},{2,3},{3,2},{4,5},{5,4},{6,7},{7,6},{8,9},{9,8},{10,11... | collective-permute-start | bytes 6291464 | tf_op jit(solution)/shard_map/ppermute | solution.py:311
  310.8 2.8 collective-permute-start.52
  313.6 6.5 %unturn.1 = (bf16[1024,1536]{1,0:T(8,128)(2,1)}, f32[1,1536]{1,0:T(1,128)}) custom-call(f32[1024,128]{1,0:T(8,128)} %get-tuple-element.781.cos_ref, f32[1024,128]{1,0:T(8,128)} %get-tuple-element.782.forth_ref, f32[1024,128]{1,0:T(8,128)} %get-tuple-element.783.back_ref, bf16[1024,128]{1,0:T(8,128)(2,1)} %get-tuple-element.784.refs_0_, ...), custom_call_target="tpu_custom_call" | custom-call | flops 15728640 | bytes 12582912 | tf_op jit(solution)/shard_map/unturn/pallas_call | solution.py:956
  320.1 7.1 %row_grads.3 = (bf16[128,1536]{1,0:T(8,128)(2,1)}, bf16[128,1536]{1,0:T(8,128)(2,1)}, bf16[128,1536]{1,0:T(8,128)(2,1)}, bf16[128,1536]{1,0:T(8,128)(2,1)}, bf16...) custom-call(s32[2]{0:T(128)} %pad_add_fusion.where_ref, bf16[1024,1024]{1,0:T(8,128)(2,1)} %get-tuple-element.796.left_ref, ...), custom_call_target="tpu_custom_call" | custom-call | flops 3221225472 | bytes 5242880 | tf_op jit(solution)/shard_map/row_grads/pallas_call | solution.py:1145
  329.8 2.4 add_convert_fusion.2
  334.0 9.7 %norm_grad.3 = (f32[512,1024]{1,0:T(8,128)}, f32[512,1024]{1,0:T(8,128)}) custom-call(bf16[1024,1536]{1,0:T(8,128)(2,1)} %get-tuple-element.816.right_ref.left_ref, bf16[256,896]{1,0:T(8,128)(2,1)} %copy-done.8, bf16[256,896]{1,0:T(8,128)(2,1)} %copy-done.13, bf16[256,896]{1,0:T(8,128)(2,1)} %collective-permute-done.11.refs_2_, ...), custom_call_target="tpu_custom_call" | custom-call | flops 3221225472 | bytes 12582912 | tf_op jit(solution)/shard_map/norm_grad/pallas_call | solution.py:1283
  343.6 4.3 %collective-permute-done.56 = bf16[128,2560]{1,0:T(8,128)(2,1)S(1)} collective-permute-done((bf16[128,2560]{1,0:T(8,128)(2,1)}, bf16[128,2560]{1,0:T(8,128)(2,1)S(1)}, u32[]{:S(2)}, u32[]{:S(2)}) %collective-permute-start.56) | collective-permute-done | bytes 655392 | tf_op jit(solution)/shard_map/ppermute | solution.py:311
  347.9 2.2 add_convert_fusion.12
  360.3 7.1 %norm_back.1 = (bf16[512,1024]{1,0:T(8,128)(2,1)}, f32[8,1024]{1,0:T(8,128)}) custom-call(s32[2]{0:T(128)} %pad_add_fusion.where_ref, f32[512,1024]{1,0:T(8,128)} %get-tuple-element.849.part_ref, f32[512,1024]{1,0:T(8,128)} %copy-done.7, f32[1024,1024]{1,0:T(8,128)} %get-tuple-element.850.xhat_ref, f32[1024,1]{1,0:T(8,128)} %get-tuple-element.851.inv_ref, ...), custom_call_target="tpu_custom_call" | custom-call | flops 2147483648 | bytes 8388608 | tf_op jit(solution)/shard_map/norm_back/pallas_call | solution.py:1324
  369.7 3.3 collective-permute-done.60
  381.5 3.4 add_convert_fusion
  388.2 3.2 collective-permute-start.65
  391.5 2.1 convert_add_fusion.1
  395.5 4.8 %collective-permute-done.66 = f32[2,640]{1,0:T(2,128)S(1)} collective-permute-done((f32[2,640]{1,0:T(2,128)S(1)}, f32[2,640]{1,0:T(2,128)S(1)}, u32[]{:S(2)}, u32[]{:S(2)}) %collective-permute-start.66) | collective-permute-done | bytes 5152 | tf_op jit(solution)/shard_map/ppermute | solution.py:311
  (306 shorter events, 134.7 us)
Async XLA Ops:
  17.2 11.5 %collective-permute-start.7 = (bf16[512,1024]{1,0:T(8,128)(2,1)}, bf16[512,1024]{1,0:T(8,128)(2,1)}, u32[]{:S(2)}, u32[]{:S(2)}) collective-permute-start(bf16[512,1024]{1,0:T(8,128)(2,1)} %bitcast.23), channel_id=1, source_target_pairs={{0,1},{1,0},{2,3},{3,2},{4,5},{5,4},{6,7},{7,6},{8,9},{9,8},{10,11... | collective-permute-start | bytes 3145736 | tf_op jit(solution)/shard_map/ppermute | solution.py:311
  41.4 15.2 %collective-permute-start.11 = (bf16[256,896]{1,0:T(8,128)(2,1)S(1)}, bf16[256,896]{1,0:T(8,128)(2,1)}, u32[]{:S(2)}, u32[]{:S(2)}) collective-permute-start(bf16[256,896]{1,0:T(8,128)(2,1)S(1)} %pad_maximum_fusion.4.refs_0_), channel_id=1, source_target_pairs={{0,4},{1,5},{2,6},{3,7},{4,0},{5,1},{6,2},{7,3},{8,12},{9,13},{10,... | collective-permute-start | bytes 1376264 | tf_op jit(solution)/shard_map/ppermute | solution.py:311
  41.6 14.9 %collective-permute-start.12 = (bf16[256,896]{1,0:T(8,128)(2,1)S(1)}, bf16[256,896]{1,0:T(8,128)(2,1)}, u32[]{:S(2)}, u32[]{:S(2)}) collective-permute-start(bf16[256,896]{1,0:T(8,128)(2,1)S(1)} %constant_dynamic-update-slice_fusion.refs_1_), channel_id=1, source_target_pairs={{0,2},{1,3},{2,0},{3,1},{4,6},{5,7},{6,4},{7,5},{8,10},{9,11},{10,... | collective-permute-start | bytes 1376264 | tf_op jit(solution)/shard_map/ppermute | solution.py:311
  42.5 14.0 %collective-permute-start.13 = (bf16[64,2048]{1,0:T(8,128)(2,1)}, bf16[64,2048]{1,0:T(8,128)(2,1)S(1)}, u32[]{:S(2)}, u32[]{:S(2)}) collective-permute-start(bf16[64,2048]{1,0:T(8,128)(2,1)} %pad_maximum_fusion.6), channel_id=1, source_target_pairs={{0,16},{8,24},{16,0},{24,8},{1,17},{9,25},{17,1},{25,9},{2,18},{10... | collective-permute-start | bytes 786440 | tf_op jit(solution)/shard_map/ppermute | solution.py:311
  56.6 17.1 %collective-permute-start.16 = (bf16[128,2048]{1,0:T(8,128)(2,1)S(1)}, bf16[128,2048]{1,0:T(8,128)(2,1)S(1)}, u32[]{:S(2)}, u32[]{:S(2)}) collective-permute-start(bf16[128,2048]{1,0:T(8,128)(2,1)S(1)} %pad_maximum_fusion.3), channel_id=1, source_target_pairs={{0,8},{8,0},{16,24},{24,16},{1,9},{9,1},{17,25},{25,17},{2,10},{10... | collective-permute-start | bytes 1572872 | tf_op jit(solution)/shard_map/ppermute | solution.py:311
  56.7 13.5 %collective-permute-start.14 = (bf16[128,1280]{1,0:T(8,128)(2,1)S(1)}, bf16[128,1280]{1,0:T(8,128)(2,1)S(1)}, u32[]{:S(2)}, u32[]{:S(2)}) collective-permute-start(bf16[128,1280]{1,0:T(8,128)(2,1)S(1)} %pad_maximum_fusion.5), channel_id=1, source_target_pairs={{0,2},{1,3},{2,0},{3,1},{4,6},{5,7},{6,4},{7,5},{8,10},{9,11},{10,... | collective-permute-start | bytes 983048 | tf_op jit(solution)/shard_map/ppermute | solution.py:311
  57.9 12.2 %collective-permute-start.15 = (bf16[128,1280]{1,0:T(8,128)(2,1)}, bf16[128,1280]{1,0:T(8,128)(2,1)}, u32[]{:S(2)}, u32[]{:S(2)}) collective-permute-start(bf16[128,1280]{1,0:T(8,128)(2,1)} %collective-permute-done.10), channel_id=1, source_target_pairs={{0,4},{1,5},{2,6},{3,7},{4,0},{5,1},{6,2},{7,3},{8,12},{9,13},{10,... | collective-permute-start | bytes 983048 | tf_op jit(solution)/shard_map/ppermute | solution.py:311
  75.8 13.4 %collective-permute-start.18 = (bf16[256,1280]{1,0:T(8,128)(2,1)S(1)}, bf16[256,1280]{1,0:T(8,128)(2,1)S(1)}, u32[]{:S(2)}, u32[]{:S(2)}) collective-permute-start(bf16[256,1280]{1,0:T(8,128)(2,1)S(1)} %pad_maximum_fusion.2.refs_0_.refs_4_), channel_id=1, source_target_pairs={{0,4},{1,5},{2,6},{3,7},{4,0},{5,1},{6,2},{7,3},{8,12},{9,13},{10,... | collective-permute-start | bytes 1966088 | tf_op jit(solution)/shard_map/ppermute | solution.py:311
  77.1 13.9 %collective-permute-start.19 = (bf16[256,1280]{1,0:T(8,128)(2,1)S(1)}, bf16[256,1280]{1,0:T(8,128)(2,1)S(1)}, u32[]{:S(2)}, u32[]{:S(2)}) collective-permute-start(bf16[256,1280]{1,0:T(8,128)(2,1)S(1)} %constant_dynamic-update-slice_fusion.4.refs_1_.refs_5_), channel_id=1, source_target_pairs={{0,2},{1,3},{2,0},{3,1},{4,6},{5,7},{6,4},{7,5},{8,10},{9,11},{10,... | collective-permute-start | bytes 1966088 | tf_op jit(solution)/shard_map/ppermute | solution.py:311
  90.9 20.5 %collective-permute-start.21 = (bf16[128,2048]{1,0:T(8,128)(2,1)}, bf16[128,2048]{1,0:T(8,128)(2,1)}, u32[]{:S(2)}, u32[]{:S(2)}) collective-permute-start(bf16[128,2048]{1,0:T(8,128)(2,1)} %copy-done.29), channel_id=1, source_target_pairs={{0,2},{1,3},{2,0},{3,1},{4,6},{5,7},{6,4},{7,5},{8,10},{9,11},{10,... | collective-permute-start | bytes 1572872 | tf_op jit(solution)/shard_map/ppermute | solution.py:311
  92.6 18.8 %collective-permute-start.22 = (bf16[128,2048]{1,0:T(8,128)(2,1)}, bf16[128,2048]{1,0:T(8,128)(2,1)}, u32[]{:S(2)}, u32[]{:S(2)}) collective-permute-start(bf16[128,2048]{1,0:T(8,128)(2,1)} %copy-done.30), channel_id=1, source_target_pairs={{0,4},{1,5},{2,6},{3,7},{4,0},{5,1},{6,2},{7,3},{8,12},{9,13},{10,... | collective-permute-start | bytes 1572872 | tf_op jit(solution)/shard_map/ppermute | solution.py:311
  93.0 18.4 %collective-permute-start.23 = (bf16[1024,256]{1,0:T(8,128)(2,1)}, bf16[1024,256]{1,0:T(8,128)(2,1)}, u32[]{:S(2)}, u32[]{:S(2)}) collective-permute-start(bf16[1024,256]{1,0:T(8,128)(2,1)} %collective-permute-done.20.refs_1_), channel_id=1, source_target_pairs={{0,8},{8,16},{16,24},{1,9},{9,17},{17,25},{2,10},{10,18},{18,26},{... | collective-permute-start | bytes 1572872 | tf_op jit(solution)/shard_map/ppermute | solution.py:316
  95.0 16.9 %collective-permute-start.24 = (bf16[1024,256]{1,0:T(8,128)(2,1)}, bf16[1024,256]{1,0:T(8,128)(2,1)}, u32[]{:S(2)}, u32[]{:S(2)}) collective-permute-start(bf16[1024,256]{1,0:T(8,128)(2,1)} %get-tuple-element.641.refs_0_), channel_id=1, source_target_pairs={{0,8},{8,16},{16,24},{1,9},{9,17},{17,25},{2,10},{10,18},{18,26},{... | collective-permute-start | bytes 1572872 | tf_op jit(solution)/shard_map/ppermute | solution.py:316
  114.5 32.9 %collective-permute-start.25 = (bf16[256,2048]{1,0:T(8,128)(2,1)S(1)}, bf16[256,2048]{1,0:T(8,128)(2,1)}, u32[]{:S(2)}, u32[]{:S(2)}) collective-permute-start(bf16[256,2048]{1,0:T(8,128)(2,1)S(1)} %pad_maximum_fusion.refs_0_), channel_id=1, source_target_pairs={{0,4},{1,5},{2,6},{3,7},{4,0},{5,1},{6,2},{7,3},{8,12},{9,13},{10,... | collective-permute-start | bytes 3145736 | tf_op jit(solution)/shard_map/ppermute | solution.py:311
  115.5 32.0 %collective-permute-start.26 = (bf16[256,2048]{1,0:T(8,128)(2,1)S(1)}, bf16[256,2048]{1,0:T(8,128)(2,1)}, u32[]{:S(2)}, u32[]{:S(2)}) collective-permute-start(bf16[256,2048]{1,0:T(8,128)(2,1)S(1)} %constant_dynamic-update-slice_fusion.6.refs_1_), channel_id=1, source_target_pairs={{0,2},{1,3},{2,0},{3,1},{4,6},{5,7},{6,4},{7,5},{8,10},{9,11},{10,... | collective-permute-start | bytes 3145736 | tf_op jit(solution)/shard_map/ppermute | solution.py:311
  122.3 18.3 %collective-permute-start.27 = (bf16[256,1024]{1,0:T(8,128)(2,1)}, bf16[256,1024]{1,0:T(8,128)(2,1)S(1)}, u32[]{:S(2)}, u32[]{:S(2)}) collective-permute-start(bf16[256,1024]{1,0:T(8,128)(2,1)} %get-tuple-element.611), channel_id=1, source_target_pairs={{0,8},{8,0},{16,24},{24,16},{1,9},{9,1},{17,25},{25,17},{2,10},{10... | collective-permute-start | bytes 1572872 | tf_op jit(solution)/shard_map/ppermute | solution.py:311
  124.5 22.9 %collective-permute-start.28 = (bf16[1024,256]{1,0:T(8,128)(2,1)}, bf16[1024,256]{1,0:T(8,128)(2,1)S(1)}, u32[]{:S(2)}, u32[]{:S(2)}) collective-permute-start(bf16[1024,256]{1,0:T(8,128)(2,1)} %collective-permute-done.24.refs_1_), channel_id=1, source_target_pairs={{0,8},{8,16},{16,24},{1,9},{9,17},{17,25},{2,10},{10,18},{18,26},{... | collective-permute-start | bytes 1572872 | tf_op jit(solution)/shard_map/ppermute | solution.py:316
  147.4 26.0 %collective-permute-start.32 = (bf16[1024,512]{1,0:T(8,128)(2,1)}, bf16[1024,512]{1,0:T(8,128)(2,1)}, u32[]{:S(2)}, u32[]{:S(2)}) collective-permute-start(bf16[1024,512]{1,0:T(8,128)(2,1)} %get-tuple-element.676.refs_0_), channel_id=1, source_target_pairs={{0,8},{8,16},{16,24},{1,9},{9,17},{17,25},{2,10},{10,18},{18,26},{... | collective-permute-start | bytes 3145736 | tf_op jit(solution)/shard_map/ppermute | solution.py:316
  152.5 19.0 %collective-permute-start.30 = (bf16[256,1024]{1,0:T(8,128)(2,1)}, bf16[256,1024]{1,0:T(8,128)(2,1)S(1)}, u32[]{:S(2)}, u32[]{:S(2)}) collective-permute-start(bf16[256,1024]{1,0:T(8,128)(2,1)} %get-tuple-element.611), channel_id=1, source_target_pairs={{0,2},{1,3},{2,0},{3,1},{4,6},{5,7},{6,4},{7,5},{8,10},{9,11},{10,... | collective-permute-start | bytes 1572872 | tf_op jit(solution)/shard_map/ppermute | solution.py:311
  153.9 17.5 %collective-permute-start.31 = (bf16[256,1024]{1,0:T(8,128)(2,1)S(1)}, bf16[256,1024]{1,0:T(8,128)(2,1)S(1)}, u32[]{:S(2)}, u32[]{:S(2)}) collective-permute-start(bf16[256,1024]{1,0:T(8,128)(2,1)S(1)} %collective-permute-done.27), channel_id=1, source_target_pairs={{0,4},{1,5},{2,6},{3,7},{4,0},{5,1},{6,2},{7,3},{8,12},{9,13},{10,... | collective-permute-start | bytes 1572872 | tf_op jit(solution)/shard_map/ppermute | solution.py:311
  154.3 17.2 %collective-permute-start.33 = (bf16[1024,256]{1,0:T(8,128)(2,1)}, bf16[1024,256]{1,0:T(8,128)(2,1)S(1)}, u32[]{:S(2)}, u32[]{:S(2)}) collective-permute-start(bf16[1024,256]{1,0:T(8,128)(2,1)} %get-tuple-element.614), channel_id=1, source_target_pairs={{8,0},{16,8},{24,16},{9,1},{17,9},{25,17},{10,2},{18,10},{26,18},{... | collective-permute-start | bytes 1572872 | tf_op jit(solution)/shard_map/ppermute | solution.py:316
  175.4 29.3 %collective-permute-start.34 = (bf16[512,1024]{1,0:T(8,128)(2,1)}, bf16[512,1024]{1,0:T(8,128)(2,1)S(1)}, u32[]{:S(2)}, u32[]{:S(2)}) collective-permute-start(bf16[512,1024]{1,0:T(8,128)(2,1)} %get-tuple-element.746.refs_0_.refs_3_), channel_id=1, source_target_pairs={{0,4},{1,5},{2,6},{3,7},{4,0},{5,1},{6,2},{7,3},{8,12},{9,13},{10,... | collective-permute-start | bytes 3145736 | tf_op jit(solution)/shard_map/ppermute | solution.py:311
  175.9 28.9 %collective-permute-start.35 = (bf16[512,1024]{1,0:T(8,128)(2,1)}, bf16[512,1024]{1,0:T(8,128)(2,1)S(1)}, u32[]{:S(2)}, u32[]{:S(2)}) collective-permute-start(bf16[512,1024]{1,0:T(8,128)(2,1)} %get-tuple-element.747.refs_1_.refs_4_), channel_id=1, source_target_pairs={{0,2},{1,3},{2,0},{3,1},{4,6},{5,7},{6,4},{7,5},{8,10},{9,11},{10,... | collective-permute-start | bytes 3145736 | tf_op jit(solution)/shard_map/ppermute | solution.py:311
  177.3 27.5 %collective-permute-start.36 = (bf16[1024,512]{1,0:T(8,128)(2,1)}, bf16[1024,512]{1,0:T(8,128)(2,1)}, u32[]{:S(2)}, u32[]{:S(2)}) collective-permute-start(bf16[1024,512]{1,0:T(8,128)(2,1)} %collective-permute-done.32.refs_1_), channel_id=1, source_target_pairs={{0,8},{8,16},{16,24},{1,9},{9,17},{17,25},{2,10},{10,18},{18,26},{... | collective-permute-start | bytes 3145736 | tf_op jit(solution)/shard_map/ppermute | solution.py:316
  191.4 13.4 %collective-permute-start.37 = (bf16[1024,256]{1,0:T(8,128)(2,1)}, bf16[1024,256]{1,0:T(8,128)(2,1)S(1)}, u32[]{:S(2)}, u32[]{:S(2)}) collective-permute-start(bf16[1024,256]{1,0:T(8,128)(2,1)} %get-tuple-element.648), channel_id=1, source_target_pairs={{8,0},{16,8},{24,16},{9,1},{17,9},{25,17},{10,2},{18,10},{26,18},{... | collective-permute-start | bytes 1572872 | tf_op jit(solution)/shard_map/ppermute | solution.py:316
  206.0 25.4 %collective-permute-start.38 = (bf16[512,1024]{1,0:T(8,128)(2,1)}, bf16[512,1024]{1,0:T(8,128)(2,1)S(1)}, u32[]{:S(2)}, u32[]{:S(2)}) collective-permute-start(bf16[512,1024]{1,0:T(8,128)(2,1)} %get-tuple-element.669), channel_id=1, source_target_pairs={{0,4},{1,5},{2,6},{3,7},{4,0},{5,1},{6,2},{7,3},{8,12},{9,13},{10,... | collective-permute-start | bytes 3145736 | tf_op jit(solution)/shard_map/ppermute | solution.py:311
  207.1 24.3 %collective-permute-start.39 = (bf16[512,1024]{1,0:T(8,128)(2,1)}, bf16[512,1024]{1,0:T(8,128)(2,1)S(1)}, u32[]{:S(2)}, u32[]{:S(2)}) collective-permute-start(bf16[512,1024]{1,0:T(8,128)(2,1)} %get-tuple-element.670), channel_id=1, source_target_pairs={{0,2},{1,3},{2,0},{3,1},{4,6},{5,7},{6,4},{7,5},{8,10},{9,11},{10,... | collective-permute-start | bytes 3145736 | tf_op jit(solution)/shard_map/ppermute | solution.py:311
  207.1 23.9 %collective-permute-start.41 = (bf16[1024,256]{1,0:T(8,128)(2,1)}, bf16[1024,256]{1,0:T(8,128)(2,1)S(1)}, u32[]{:S(2)}, u32[]{:S(2)}) collective-permute-start(bf16[1024,256]{1,0:T(8,128)(2,1)} %add_convert_fusion.9), channel_id=1, source_target_pairs={{8,0},{16,8},{24,16},{9,1},{17,9},{25,17},{10,2},{18,10},{26,18},{... | collective-permute-start | bytes 1572872 | tf_op jit(solution)/shard_map/ppermute | solution.py:316
  208.4 23.0 %collective-permute-start.40 = (bf16[1024,256]{1,0:T(8,128)(2,1)}, bf16[1024,256]{1,0:T(8,128)(2,1)S(1)}, u32[]{:S(2)}, u32[]{:S(2)}) collective-permute-start(bf16[1024,256]{1,0:T(8,128)(2,1)} %add_convert_fusion.8), channel_id=1, source_target_pairs={{8,0},{16,8},{24,16},{9,1},{17,9},{25,17},{10,2},{18,10},{26,18},{... | collective-permute-start | bytes 1572872 | tf_op jit(solution)/shard_map/ppermute | solution.py:316
  235.9 19.4 %collective-permute-start.43 = (bf16[256,1024]{1,0:T(8,128)(2,1)}, bf16[256,1024]{1,0:T(8,128)(2,1)}, u32[]{:S(2)}, u32[]{:S(2)}) collective-permute-start(bf16[256,1024]{1,0:T(8,128)(2,1)} %add_convert_fusion.6), channel_id=1, source_target_pairs={{0,4},{1,5},{2,6},{3,7},{4,0},{5,1},{6,2},{7,3},{8,12},{9,13},{10,... | collective-permute-start | bytes 1572872 | tf_op jit(solution)/shard_map/ppermute | solution.py:311
  236.3 35.6 %collective-permute-start.45 = (bf16[1024,512]{1,0:T(8,128)(2,1)}, bf16[1024,512]{1,0:T(8,128)(2,1)S(1)}, u32[]{:S(2)}, u32[]{:S(2)}) collective-permute-start(bf16[1024,512]{1,0:T(8,128)(2,1)} %get-tuple-element.683), channel_id=1, source_target_pairs={{8,0},{16,8},{24,16},{9,1},{17,9},{25,17},{10,2},{18,10},{26,18},{... | collective-permute-start | bytes 3145736 | tf_op jit(solution)/shard_map/ppermute | solution.py:316
  237.6 34.3 %collective-permute-start.42 = (bf16[256,1024]{1,0:T(8,128)(2,1)}, bf16[256,1024]{1,0:T(8,128)(2,1)}, u32[]{:S(2)}, u32[]{:S(2)}) collective-permute-start(bf16[256,1024]{1,0:T(8,128)(2,1)} %add_convert_fusion.7), channel_id=1, source_target_pairs={{0,2},{1,3},{2,0},{3,1},{4,6},{5,7},{6,4},{7,5},{8,10},{9,11},{10,... | collective-permute-start | bytes 1572872 | tf_op jit(solution)/shard_map/ppermute | solution.py:311
  239.0 21.6 %collective-permute-start.44 = (bf16[256,1024]{1,0:T(8,128)(2,1)}, bf16[256,1024]{1,0:T(8,128)(2,1)}, u32[]{:S(2)}, u32[]{:S(2)}) collective-permute-start(bf16[256,1024]{1,0:T(8,128)(2,1)} %get-tuple-element.704), channel_id=1, source_target_pairs={{0,1},{1,0},{2,3},{3,2},{4,5},{5,4},{6,7},{7,6},{8,9},{9,8},{10,11... | collective-permute-start | bytes 1572872 | tf_op jit(solution)/shard_map/ppermute | solution.py:311
  257.6 15.8 %collective-permute-start.46 = (bf16[256,1024]{1,0:T(8,128)(2,1)}, bf16[256,1024]{1,0:T(8,128)(2,1)S(1)}, u32[]{:S(2)}, u32[]{:S(2)}) collective-permute-start(bf16[256,1024]{1,0:T(8,128)(2,1)} %add_convert_fusion.5), channel_id=1, source_target_pairs={{0,8},{8,0},{16,24},{24,16},{1,9},{9,1},{17,25},{25,17},{2,10},{10... | collective-permute-start | bytes 1572872 | tf_op jit(solution)/shard_map/ppermute | solution.py:311
  275.4 27.2 %collective-permute-start.47 = (bf16[256,2560]{1,0:T(8,128)(2,1)}, bf16[256,2560]{1,0:T(8,128)(2,1)S(1)}, u32[]{:S(2)}, u32[]{:S(2)}) collective-permute-start(bf16[256,2560]{1,0:T(8,128)(2,1)} %get-tuple-element.737), channel_id=1, source_target_pairs={{0,4},{1,5},{2,6},{3,7},{4,0},{5,1},{6,2},{7,3},{8,12},{9,13},{10,... | collective-permute-start | bytes 3932168 | tf_op jit(solution)/shard_map/ppermute | solution.py:311
  276.6 27.0 %collective-permute-start.48 = (bf16[256,2560]{1,0:T(8,128)(2,1)}, bf16[256,2560]{1,0:T(8,128)(2,1)S(1)}, u32[]{:S(2)}, u32[]{:S(2)}) collective-permute-start(bf16[256,2560]{1,0:T(8,128)(2,1)} %get-tuple-element.738), channel_id=1, source_target_pairs={{0,2},{1,3},{2,0},{3,1},{4,6},{5,7},{6,4},{7,5},{8,10},{9,11},{10,... | collective-permute-start | bytes 3932168 | tf_op jit(solution)/shard_map/ppermute | solution.py:311
  277.1 24.9 %collective-permute-start.49 = (bf16[1024,512]{1,0:T(8,128)(2,1)}, bf16[1024,512]{1,0:T(8,128)(2,1)}, u32[]{:S(2)}, u32[]{:S(2)}) collective-permute-start(bf16[1024,512]{1,0:T(8,128)(2,1)} %add_convert_fusion.1), channel_id=1, source_target_pairs={{8,0},{16,8},{24,16},{9,1},{17,9},{25,17},{10,2},{18,10},{26,18},{... | collective-permute-start | bytes 3145736 | tf_op jit(solution)/shard_map/ppermute | solution.py:316
  305.5 21.7 %collective-permute-start.53 = (f32[512,1024]{1,0:T(8,128)}, f32[512,1024]{1,0:T(8,128)S(1)}, u32[]{:S(2)}, u32[]{:S(2)}) collective-permute-start(f32[512,1024]{1,0:T(8,128)} %get-tuple-element.780), channel_id=1, source_target_pairs={{0,1},{1,0},{2,3},{3,2},{4,5},{5,4},{6,7},{7,6},{8,9},{9,8},{10,11... | collective-permute-start | bytes 6291464 | tf_op jit(solution)/shard_map/ppermute | solution.py:311
  310.0 17.2 %collective-permute-start.50 = (bf16[128,2560]{1,0:T(8,128)(2,1)}, bf16[128,2560]{1,0:T(8,128)(2,1)}, u32[]{:S(2)}, u32[]{:S(2)}) collective-permute-start(bf16[128,2560]{1,0:T(8,128)(2,1)} %add_convert_fusion.4), channel_id=1, source_target_pairs={{0,2},{1,3},{2,0},{3,1},{4,6},{5,7},{6,4},{7,5},{8,10},{9,11},{10,... | collective-permute-start | bytes 1966088 | tf_op jit(solution)/shard_map/ppermute | solution.py:311
  310.5 16.7 %collective-permute-start.51 = (bf16[128,2560]{1,0:T(8,128)(2,1)}, bf16[128,2560]{1,0:T(8,128)(2,1)}, u32[]{:S(2)}, u32[]{:S(2)}) collective-permute-start(bf16[128,2560]{1,0:T(8,128)(2,1)} %add_convert_fusion.3), channel_id=1, source_target_pairs={{0,4},{1,5},{2,6},{3,7},{4,0},{5,1},{6,2},{7,3},{8,12},{9,13},{10,... | collective-permute-start | bytes 1966088 | tf_op jit(solution)/shard_map/ppermute | solution.py:311
  310.8 16.4 %collective-permute-start.52 = (bf16[128,1024]{1,0:T(8,128)(2,1)}, bf16[128,1024]{1,0:T(8,128)(2,1)}, u32[]{:S(2)}, u32[]{:S(2)}) collective-permute-start(bf16[128,1024]{1,0:T(8,128)(2,1)} %add_convert_fusion.14), channel_id=1, source_target_pairs={{0,16},{8,24},{16,0},{24,8},{1,17},{9,25},{17,1},{25,9},{2,18},{10... | collective-permute-start | bytes 786440 | tf_op jit(solution)/shard_map/ppermute | solution.py:311
  327.2 20.7 %collective-permute-start.54 = (bf16[256,1536]{1,0:T(8,128)(2,1)}, bf16[256,1536]{1,0:T(8,128)(2,1)}, u32[]{:S(2)}, u32[]{:S(2)}) collective-permute-start(bf16[256,1536]{1,0:T(8,128)(2,1)} %get-tuple-element.812), channel_id=1, source_target_pairs={{0,4},{1,5},{2,6},{3,7},{4,0},{5,1},{6,2},{7,3},{8,12},{9,13},{10,... | collective-permute-start | bytes 2359304 | tf_op jit(solution)/shard_map/ppermute | solution.py:311
  328.3 19.6 %collective-permute-start.55 = (bf16[256,1536]{1,0:T(8,128)(2,1)}, bf16[256,1536]{1,0:T(8,128)(2,1)}, u32[]{:S(2)}, u32[]{:S(2)}) collective-permute-start(bf16[256,1536]{1,0:T(8,128)(2,1)} %get-tuple-element.813), channel_id=1, source_target_pairs={{0,2},{1,3},{2,0},{3,1},{4,6},{5,7},{6,4},{7,5},{8,10},{9,11},{10,... | collective-permute-start | bytes 2359304 | tf_op jit(solution)/shard_map/ppermute | solution.py:311
  332.2 15.7 %collective-permute-start.56 = (bf16[128,2560]{1,0:T(8,128)(2,1)}, bf16[128,2560]{1,0:T(8,128)(2,1)S(1)}, u32[]{:S(2)}, u32[]{:S(2)}) collective-permute-start(bf16[128,2560]{1,0:T(8,128)(2,1)} %add_convert_fusion.2), channel_id=1, source_target_pairs={{0,8},{8,0},{16,24},{24,16},{1,9},{9,1},{17,25},{25,17},{2,10},{10... | collective-permute-start | bytes 1966088 | tf_op jit(solution)/shard_map/ppermute | solution.py:311
  355.5 17.6 %collective-permute-start.60 = (bf16[64,2560]{1,0:T(8,128)(2,1)}, bf16[64,2560]{1,0:T(8,128)(2,1)}, u32[]{:S(2)}, u32[]{:S(2)}) collective-permute-start(bf16[64,2560]{1,0:T(8,128)(2,1)} %add_convert_fusion.13), channel_id=1, source_target_pairs={{0,16},{8,24},{16,0},{24,8},{1,17},{9,25},{17,1},{25,9},{2,18},{10... | collective-permute-start | bytes 983048 | tf_op jit(solution)/shard_map/ppermute | solution.py:311
  357.1 16.0 %collective-permute-start.57 = (bf16[128,1536]{1,0:T(8,128)(2,1)}, bf16[128,1536]{1,0:T(8,128)(2,1)}, u32[]{:S(2)}, u32[]{:S(2)}) collective-permute-start(bf16[128,1536]{1,0:T(8,128)(2,1)} %add_convert_fusion.12), channel_id=1, source_target_pairs={{0,2},{1,3},{2,0},{3,1},{4,6},{5,7},{6,4},{7,5},{8,10},{9,11},{10,... | collective-permute-start | bytes 1179656 | tf_op jit(solution)/shard_map/ppermute | solution.py:311
  357.5 15.6 %collective-permute-start.58 = (bf16[128,1536]{1,0:T(8,128)(2,1)S(1)}, bf16[128,1536]{1,0:T(8,128)(2,1)}, u32[]{:S(2)}, u32[]{:S(2)}) collective-permute-start(bf16[128,1536]{1,0:T(8,128)(2,1)S(1)} %add_convert_fusion.11), channel_id=1, source_target_pairs={{0,4},{1,5},{2,6},{3,7},{4,0},{5,1},{6,2},{7,3},{8,12},{9,13},{10,... | collective-permute-start | bytes 1179656 | tf_op jit(solution)/shard_map/ppermute | solution.py:311
  388.2 12.1 %collective-permute-start.65 = (bf16[64,1536]{1,0:T(8,128)(2,1)S(1)}, bf16[64,1536]{1,0:T(8,128)(2,1)S(1)}, u32[]{:S(2)}, u32[]{:S(2)}) collective-permute-start(bf16[64,1536]{1,0:T(8,128)(2,1)S(1)} %add_convert_fusion.15), channel_id=1, source_target_pairs={{0,16},{8,24},{16,0},{24,8},{1,17},{9,25},{17,1},{25,9},{2,18},{10... | collective-permute-start | bytes 589832 | tf_op jit(solution)/shard_map/ppermute | solution.py:311
  (71 other events, 705.8 us)

commit v3 on v2

--- a/solution.py
+++ b/solution.py
@@ -351,7 +351,7 @@
 
     def jobs(self, stage):
         parts = self.parts
-        if stage == "near":
+        if stage == "near" and "a" not in parts:
             parts["a"] = jnp.concatenate([parts["s"], parts["f"]], axis=0)
         if stage == "second":
             parts["ax"] = jnp.concatenate([parts["a"], parts["xa"]], axis=0)
@@ -990,12 +990,12 @@
         slope_ref[here, :] = slope
         return carry
 
-    lax.fori_loop(0, normed_ref.shape[0] // rows, some, 0)
+    lax.fori_loop(0, normed_ref.shape[0] // rows, some, 0, unroll=True)
 
 
 def hidden(normed, pieces, bias):
     rows, width = normed.shape[0], bias.shape[1]
-    step = 512
+    step = 256
     column = pl.BlockSpec((rows, step), lambda j: (0, j))
     return pl.pallas_call(
         hidden_kernel,
@@ -1111,7 +1111,7 @@
 
 
 def row_grads_kernel(steps, where_ref, left_ref, right_ref, *refs):
-    out_refs = refs[-6:]
+    out_refs = refs[:6] if len(refs) == 6 else refs[2:8]
     spots = [[place_of(chip) for chip in chips] for chips in BLOCKS.values()]
 
     @pl.when(pl.program_id(0) < steps)
@@ -1121,12 +1121,14 @@
             for at, place in enumerate(places):
                 ref[at * 64 : at * 64 + 64, :] = value[place * 64 : place * 64 + 64]
 
-    if len(refs) == 7:
-        held_ref = refs[0]
+    if len(refs) > 6:
+        keep_ref, more_ref, held_ref = refs[0], refs[1], refs[-1]
         me, core = where_ref[0], where_ref[1]
 
         @pl.when(pl.program_id(0) >= steps)
         def _():
+            held_ref[:256, :] = keep_ref[...]
+            held_ref[256:, :] = more_ref[...]
             for chips, ref in zip(BLOCKS.values(), out_refs):
                 for at, chip in enumerate(chips):
                     found = chip ^ me
@@ -1136,11 +1138,11 @@
                     ref[at * 64 + 32 : at * 64 + 64, :] = rows[:, D // 2 :]
 
 
-def row_grads(where, left, right, more=None):
+def row_grads(where, left, right, more=()):
     rows, tokens = left.shape
     step = 512
     steps = right.shape[1] // step
-    columns = right.shape[1] + (0 if more is None else D // 2)
+    columns = right.shape[1] + (D // 2 if more else 0)
     heights = [64 * len(chips) for chips in BLOCKS.values()]
     return pl.pallas_call(
         partial(row_grads_kernel, steps),
@@ -1151,11 +1153,12 @@
             whole(left),
             pl.BlockSpec((tokens, step), lambda j: (0, jnp.minimum(j, steps - 1))),
         ]
-        + ([] if more is None else [whole(more)]),
+        + [whole(rows) for rows in more],
         out_specs=tuple(pl.BlockSpec((height, step), lambda j: (0, j)) for height in heights),
+        scratch_shapes=[pltpu.VMEM((512, D), BF)] if more else [],
         cost_estimate=cost(2 * rows * tokens * columns, 2 * (rows * tokens + rows * columns)),
         name="row_grads",
-    )(where, left, right, *([] if more is None else [more]))
+    )(where, left, right, *more)
 
 
 def unit_grads_kernel(order_ref, *refs):
@@ -1163,23 +1166,15 @@
     left = stack(lefts)
     tokens = own_ref.shape[0]
     a, xa, b, yb, yax, xby = out_refs
-    columns = 512
-
-    def some(i, carry):
-        here = pl.ds(pl.multiple_of(i * columns, columns), columns)
-        value = dot(left[:, :tokens], own_ref[:, here]) + dot(left[:, tokens:], other_ref[:, here])
-        value = value.astype(BF)
-        for piece, outs in enumerate(((a, xa), (b, yb), (yax,), (xby,))):
-
-            @pl.when(pl.program_id(0) == piece)
-            def _(outs=outs):
-                rows = 512 // len(outs)
-                for at, ref in enumerate(outs):
-                    ref[:, here] = value[at * rows : at * rows + rows]
-
-        return carry
-
-    lax.fori_loop(0, D // columns, some, 0)
+    value = dot(left[:, :tokens], own_ref[...]) + dot(left[:, tokens:], other_ref[...])
+    value = value.astype(BF)
+    for piece, outs in enumerate(((a, xa), (b, yb), (yax,), (xby,))):
+
+        @pl.when(pl.program_id(0) == piece)
+        def _(outs=outs):
+            rows = 512 // len(outs)
+            for at, ref in enumerate(outs):
+                ref[...] = value[at * rows : at * rows + rows]
 
 
 def unit_grads(me, left, own, other):
@@ -1310,9 +1305,7 @@
         - jnp.mean(scaled, axis=-1, keepdims=True)
         - xhat * jnp.mean(scaled * xhat, axis=-1, keepdims=True)
     ) * inv_ref[...]
-    high = value.astype(BF)
-    low = (value - high.astype(F32)).astype(BF)
-    value = times_transposed(high, chosen_ref[...]) + times_transposed(low, chosen_ref[...])
+    value = times_transposed(value.astype(BF), chosen_ref[...])
     out_ref[...] = (g_ref[...].astype(F32) + value).astype(BF)
     sum_ref[0:1, :] += jnp.sum(grad * xhat, axis=0, keepdims=True)
     sum_ref[1:2, :] += jnp.sum(grad, axis=0, keepdims=True)
@@ -1512,11 +1505,17 @@
         for group, result in zip(groups, found):
             results[group] = result
 
-    slot(moves(line_b, "second") + [up(0, 0)])
+    line_d.parts["a"] = slot(
+        moves(line_b, "second") + [up(0, 0)],
+        lambda own, other: jnp.concatenate([own, other], axis=0),
+        line_d.parts["s"],
+        line_d.parts["f"],
+        late=[up(1, 0)],
+    )
     landed((0, 0))
     b_pieces = line_b.pieces()
     made, (out_keep, out_give) = slot(
-        moves(line_c, "first") + [up(0, 1), up(1, 0)],
+        moves(line_c, "first") + [up(0, 1)],
         lambda normed, bias, tables, pieces: (
             project_more(normed, bias, tables, pieces),
             head_rows(clock.token, pieces),
@@ -1592,19 +1591,24 @@
 
     def units_back(out_more, out_keep, normed_t, own, other, slope, pieces):
         hidden_grad, hidden_sum = unit_back(clock.token, own, other, slope, pieces)
-        more = jnp.concatenate([out_keep, out_more], axis=0)
-        return hidden_grad, hidden_sum, row_grads(clock.token, normed_t, hidden_grad, more)
+        parts = row_grads(clock.token, normed_t, hidden_grad, (out_keep, out_more))
+        box["unit_sum"] = hidden_sum
+        return hidden_grad, parts
 
     def near_now(last, own, earlier):
         rows = own.shape[0]
         total = own.astype(F32) + earlier[:rows].astype(F32) + last.astype(F32)
         return cross(total.astype(BF), NEAR)
 
-    _, ((hidden_grad, hidden_sum, in_parts), sum_fc.parts["r_b"]) = slot(
+    def near_after(last, own, earlier):
+        last, total = lax.optimization_barrier((last, box["unit_sum"]))
+        return near_now(last, own, earlier), total
+
+    _, ((hidden_grad, in_parts), (sum_fc.parts["r_b"], hidden_sum)) = slot(
         moves(sum_fc, "second") + [core_move("out_grad", out_give)],
         chain=[
             ("out_grad", units_back, (out_keep, normed_t, g_own, g_more, slope, d_pieces)),
-            ("r_yb", near_now, (sum_fc.parts["b"], sum_fc.parts["r_xby"])),
+            ("r_yb", near_after, (sum_fc.parts["b"], sum_fc.parts["r_xby"])),
         ],
     )
     sum_in = Scatter(in_parts)

time: 415 us -> 410 us (0.988)
    ppermute x58, waiting for transfers between devices: 47.6 us -> 52.9 us  [swap(): lax.ppermute(value, axis, [(i, i ^ bit) for i in range(lax.axis_size(axis...]
    unnamed x104 -> x108, local copies, waits for them, and re-layouts: 9.21 us -> 8.46 us
  transfers between devices with their start and end apart: 70 -> 70, of which waited for: 27 -> 26; matrix products, arithmetic and copies ran while one was open for 8% -> 6% of each run, Pallas kernels for 43% -> 42%
where the time goes in v3:
time: 410 us; the launch traced here: 408 us
  Pallas kernels  175 us (43%)
  starting transfers between devices  104 us (25%)
  waiting for transfers between devices  67.2 us (16%)
  other arithmetic  42.8 us (10%)
  local copies, waits for them, and re-layouts  17.2 us (4%)
    ppermute x58, starting transfers between devices, swap(): lax.ppermute(value, axis, [(i, i ^ bit) for i in range(lax.axis_size(axis...  75.6 us
    ppermute x58, waiting for transfers between devices, swap(): lax.ppermute(value, axis, [(i, i ^ bit) for i in range(lax.axis_size(axis...  52.9 us
    pallas_call x3, Pallas kernels, attend(): pl.pallas_call(attend_kernel, grid=(4, pairs), out_shape=(shaped(1024, 12...  34.3 us
    ppermute x12, starting transfers between devices, shift(): lax.ppermute(value, 'seq', [(i, i + by) for i in range(count) if 0 <= i +...  28.3 us
    pallas_call x2, Pallas kernels, norm_grad(): pl.pallas_call(partial(norm_grad_kernel, spans), grid=(4,), out_shape=(sh...  19.4 us
    pallas_call x2, Pallas kernels, row_grads(): pl.pallas_call(partial(row_grads_kernel, steps), grid=(columns // step,),...  16.2 us
    ppermute x12, waiting for transfers between devices, shift(): lax.ppermute(value, 'seq', [(i, i + by) for i in range(count) if 0 <= i +...  14.4 us
    pallas_call x1, Pallas kernels, hidden(): pl.pallas_call(hidden_kernel, grid=(width // step,), out_shape=(shaped(ro...  14.2 us
  transfers between devices with their start and end apart: 70, of which 26 were waited for; matrix products, arithmetic and copies ran while one was open for 6% of the time, Pallas kernels for 42%

profile of v3, /device:TPU:1, one launch (start us, length us, event | category | flops | bytes accessed | tf_op | source)
XLA Modules:
  0.0 408.0 jit_solution(14898472218471263050)
XLA Ops:
  5.9 3.7 collective-permute-start.1
  11.0 4.3 %collective-permute-done.1 = bf16[64,896]{1,0:T(8,128)(2,1)S(1)} collective-permute-done((bf16[64,896]{1,0:T(8,128)(2,1)S(1)}, bf16[64,896]{1,0:T(8,128)(2,1)S(1)}, u32[]{:S(2)}, u32[]{:S(2)}) %collective-permute-start.1) | collective-permute-done | bytes 114720 | tf_op jit(solution)/shard_map/ppermute | solution.py:311
  18.4 3.1 collective-permute-start.5
  23.3 3.6 collective-permute-done.5
  36.8 4.4 %collective-permute-done.10 = bf16[128,1280]{1,0:T(8,128)(2,1)} collective-permute-done((bf16[128,1280]{1,0:T(8,128)(2,1)S(1)}, bf16[128,1280]{1,0:T(8,128)(2,1)}, u32[]{:S(2)}, u32[]{:S(2)}) %collective-permute-start.10) | collective-permute-done | bytes 327712 | tf_op jit(solution)/shard_map/ppermute | solution.py:311
  43.0 5.0 %marks.1 = (f32[4,768,256]{2,1,0:T(8,128)}, f32[1024,128]{1,0:T(8,128)}, f32[1024,128]{1,0:T(8,128)}, f32[1024,128]{1,0:T(8,128)}) custom-call(s32[2]{0:T(128)} %pad_add_fusion.where_ref, bf16[128,896]{1,0:T(8,128)(2,1)} %copy-done.16, bf16[128,896]{1,0:T(8,128)(2,1)} %copy-done.17, f32[1,128]{1,0:T(1,128)} %bitcast.41, f32[1,128]{1,0:T(1,128)} %constant.130.clone.forth_ref, ...), custom_call_target="tpu_custom_call" | custom-call | flops 13107200 | bytes 4194304 | tf_op jit(solution)/shard_map/marks/pallas_call | solution.py:586
  48.0 7.2 %prepare.1 = (f32[1024,1024]{1,0:T(8,128)}, f32[1024,1]{1,0:T(8,128)}) custom-call(s32[2]{0:T(128)} %pad_add_fusion.where_ref, bf16[512,1024]{1,0:T(8,128)(2,1)} %bitcast.31, bf16[512,1024]{1,0:T(8,128)(2,1)} %collective-permute-done.2.other_ref), custom_call_target="tpu_custom_call" | custom-call | flops 2147483648 | bytes 8388608 | tf_op jit(solution)/shard_map/prepare/pallas_call | solution.py:644
  62.8 7.8 %project_first.1 = (bf16[1024,128]{1,0:T(8,128)(2,1)}, bf16[1024,256]{1,0:T(8,128)(2,1)}, bf16[1024,128]{1,0:T(8,128)(2,1)}, bf16[1024,256]{1,0:T(8,128)(2,1)}, ...) custom-call(s32[2]{0:T(128)} %pad_add_fusion.where_ref, ...), custom_call_target="tpu_custom_call" | custom-call | flops 1610612736 | bytes 12582912 | tf_op jit(solution)/shard_map/project_first/pallas_call | solution.py:728
  71.0 3.8 collective-permute-done.16
  80.7 2.3 collective-permute-start.24
  83.0 4.0 collective-permute-done.20.refs_1_
  88.2 2.8 collective-permute-done.19.refs_3_.refs_7_
  97.1 2.3 head_rows.1
  99.5 6.4 %project_more.1 = (bf16[1024,256]{1,0:T(8,128)(2,1)}, bf16[1024,512]{1,0:T(8,128)(2,1)}) custom-call(bf16[1024,1024]{1,0:T(8,128)(2,1)} %get-tuple-element.623.normed_ref, f32[1,768]{1,0:T(1,128)} %get-tuple-element.568.bias_ref, f32[1024,128]{1,0:T(8,128)} %get-tuple-element.791.cos_ref, f32[1024,128]{1,0:T(8,128)} %get-tuple-element.792.forth_ref, ...), custom_call_target="tpu_custom_call" | custom-call | flops 1610612736 | bytes 6291456 | tf_op jit(solution)/shard_map/project_more/pallas_call | solution.py:752
  106.0 3.6 collective-permute-done.23.refs_2_
  112.4 7.7 %collective-permute-start.29 = (bf16[256,1024]{1,0:T(8,128)(2,1)S(1)}, bf16[256,1024]{1,0:T(8,128)(2,1)}, u32[]{:S(2)}, u32[]{:S(2)}) collective-permute-start(bf16[256,1024]{1,0:T(8,128)(2,1)S(1)} %copy-done.48), channel_id=1, source_target_pairs={{0,1},{1,0},{2,3},{3,2},{4,5},{5,4},{6,7},{7,6},{8,9},{9,8},{10,11... | collective-permute-start | bytes 1572872 | tf_op jit(solution)/shard_map/ppermute | solution.py:311
  120.5 3.7 collective-permute-start.28
  124.2 5.1 %context_grad.1 = (bf16[1024,512]{1,0:T(8,128)(2,1)}, bf16[512,1024]{1,0:T(8,128)(2,1)}) custom-call(s32[2]{0:T(128)} %pad_add_fusion.where_ref, bf16[512,1024]{1,0:T(8,128)(2,1)} %bitcast.24, bf16[512,1024]{1,0:T(8,128)(2,1)} %collective-permute-done.7.other_ref.refs_5_, bf16[256,1024]{1,0:T(8,128)(2,1)} %get-tuple-element.599.keep_ref, ...), custom_call_target="tpu_custom_call" | custom-call | flops 1073741824 | bytes 6291456 | tf_op jit(solution)/shard_map/context_grad/pallas_call | solution.py:818
  129.3 9.0 %attend.3 = (bf16[1024,128]{1,0:T(8,128)(2,1)}, bf16[1024,128]{1,0:T(8,128)(2,1)}, f32[1024,256]{1,0:T(8,128)}, bf16[1024,256]{1,0:T(8,128)(2,1)}, bf16[1024,256]{1,0:T(8,128)(2,1)}) custom-call(bf16[1024,128]{1,0:T(8,128)(2,1)} %get-tuple-element.602.q_ref, bf16[1024,512]{1,0:T(8,128)(2,1)} %get-tuple-element.682.do_ref, ...), custom_call_target="tpu_custom_call" | custom-call | flops 2415919104 | bytes 9437184 | tf_op jit(solution)/shard_map/attend/pallas_call | solution.py:900
  138.4 4.9 %collective-permute-done.28.refs_2_ = bf16[1024,256]{1,0:T(8,128)(2,1)} collective-permute-done((bf16[1024,256]{1,0:T(8,128)(2,1)}, bf16[1024,256]{1,0:T(8,128)(2,1)}, u32[]{:S(2)}, u32[]{:S(2)}) %collective-permute-start.28) | collective-permute-done | bytes 524320 | tf_op jit(solution)/shard_map/ppermute | solution.py:316
  143.2 5.1 %collective-permute-start.32 = (bf16[1024,512]{1,0:T(8,128)(2,1)}, bf16[1024,512]{1,0:T(8,128)(2,1)}, u32[]{:S(2)}, u32[]{:S(2)}) collective-permute-start(bf16[1024,512]{1,0:T(8,128)(2,1)} %get-tuple-element.684.refs_0_), channel_id=1, source_target_pairs={{0,8},{8,16},{16,24},{1,9},{9,17},{17,25},{2,10},{10,18},{18,26},{... | collective-permute-start | bytes 3145736 | tf_op jit(solution)/shard_map/ppermute | solution.py:316
  153.9 14.2 %hidden.1 = (bf16[1024,2048]{1,0:T(8,128)(2,1)}, bf16[2048,1024]{1,0:T(8,128)(2,1)}, f32[1024,2048]{1,0:T(8,128)}) custom-call(bf16[1024,1024]{1,0:T(8,128)(2,1)} %get-tuple-element.623.normed_ref, f32[1,2048]{1,0:T(1,128)} %get-tuple-element.624.bias_ref, bf16[256,2048]{1,0:T(8,128)(2,1)} %copy-done.12, bf16[256,2048]{1,0:T(8,128)(2,1)} %copy-done.34, ...), custom_call_target="tpu_custom_call" | custom-call | flops 4399824896 | bytes 18874368 | tf_op jit(solution)/shard_map/hidden/pallas_call | solution.py:1000
  174.0 5.1 %collective-permute-start.36 = (bf16[1024,512]{1,0:T(8,128)(2,1)}, bf16[1024,512]{1,0:T(8,128)(2,1)}, u32[]{:S(2)}, u32[]{:S(2)}) collective-permute-start(bf16[1024,512]{1,0:T(8,128)(2,1)} %collective-permute-done.32.refs_1_), channel_id=1, source_target_pairs={{0,8},{8,16},{16,24},{1,9},{9,17},{17,25},{2,10},{10,18},{18,26},{... | collective-permute-start | bytes 3145736 | tf_op jit(solution)/shard_map/ppermute | solution.py:316
  179.0 9.0 %attend.4 = (bf16[1024,128]{1,0:T(8,128)(2,1)}, bf16[1024,128]{1,0:T(8,128)(2,1)}, f32[1024,256]{1,0:T(8,128)}, bf16[1024,256]{1,0:T(8,128)(2,1)}, bf16[1024,256]{1,0:T(8,128)(2,1)}) custom-call(bf16[1024,128]{1,0:T(8,128)(2,1)} %get-tuple-element.646.q_ref, bf16[1024,512]{1,0:T(8,128)(2,1)} %get-tuple-element.682.do_ref, ...), custom_call_target="tpu_custom_call" | custom-call | flops 2415919104 | bytes 9437184 | tf_op jit(solution)/shard_map/attend/pallas_call | solution.py:900
  189.9 10.4 %unit_grads.1 = (bf16[256,1024]{1,0:T(8,128)(2,1)}, bf16[256,1024]{1,0:T(8,128)(2,1)}, bf16[256,1024]{1,0:T(8,128)(2,1)}, bf16[256,1024]{1,0:T(8,128)(2,1)}, bf1...) custom-call(s32[16]{0:T(128)} %broadcast_xor_fusion.order_ref, ...), custom_call_target="tpu_custom_call" | custom-call | flops 4294967296 | bytes 8388608 | tf_op jit(solution)/shard_map/unit_grads/pallas_call | solution.py:1187
  205.9 16.3 %attend.5 = (bf16[1024,256]{1,0:T(8,128)(2,1)}, bf16[1024,256]{1,0:T(8,128)(2,1)}, f32[1024,512]{1,0:T(8,128)}, bf16[1024,512]{1,0:T(8,128)(2,1)}, bf16[1024,512]{1,0:T(8,128)(2,1)}) custom-call(bf16[1024,256]{1,0:T(8,128)(2,1)} %get-tuple-element.681.q_ref, bf16[1024,512]{1,0:T(8,128)(2,1)} %get-tuple-element.682.do_ref, ...), custom_call_target="tpu_custom_call" | custom-call | flops 4831838208 | bytes 18874368 | tf_op jit(solution)/shard_map/attend/pallas_call | solution.py:900
  222.1 5.0 %out_grad.1 = (bf16[256,1024]{1,0:T(8,128)(2,1)}, bf16[256,1024]{1,0:T(8,128)(2,1)}) custom-call(s32[2]{0:T(128)} %pad_add_fusion.where_ref, bf16[512,1024]{1,0:T(8,128)(2,1)} %bitcast.26, bf16[512,1024]{1,0:T(8,128)(2,1)} %collective-permute-done.7.other_ref.refs_5_, bf16[1024,128]{1,0:T(8,128)(2,1)} %get-tuple-element.753.refs_0_, ...), custom_call_target="tpu_custom_call" | custom-call | flops 1073741824 | bytes 6291456 | tf_op jit(solution)/shard_map/out_grad/pallas_call | solution.py:1229
  227.3 2.4 add_convert_fusion.7
  235.7 4.6 %collective-permute-start.44 = (bf16[256,1024]{1,0:T(8,128)(2,1)}, bf16[256,1024]{1,0:T(8,128)(2,1)}, u32[]{:S(2)}, u32[]{:S(2)}) collective-permute-start(bf16[256,1024]{1,0:T(8,128)(2,1)} %get-tuple-element.712), channel_id=1, source_target_pairs={{0,1},{1,0},{2,3},{3,2},{4,5},{5,4},{6,7},{7,6},{8,9},{9,8},{10,11... | collective-permute-start | bytes 1572872 | tf_op jit(solution)/shard_map/ppermute | solution.py:311
  240.3 11.6 %unit_back.1 = (bf16[1024,2048]{1,0:T(8,128)(2,1)}, f32[1,2048]{1,0:T(1,128)}) custom-call(s32[2]{0:T(128)} %pad_add_fusion.where_ref, bf16[512,1024]{1,0:T(8,128)(2,1)} %bitcast.27, bf16[512,1024]{1,0:T(8,128)(2,1)} %collective-permute-done.7.other_ref.refs_5_, f32[1024,2048]{1,0:T(8,128)} %get-tuple-element.716.slope_ref, ...), custom_call_target="tpu_custom_call" | custom-call | flops 4294967296 | bytes 16777216 | tf_op jit(solution)/shard_map/unit_back/pallas_call | solution.py:1056
  253.4 3.7 collective-permute-start.46
  257.1 9.1 %row_grads.2 = (bf16[128,2560]{1,0:T(8,128)(2,1)}, bf16[128,2560]{1,0:T(8,128)(2,1)}, bf16[128,2560]{1,0:T(8,128)(2,1)}, bf16[128,2560]{1,0:T(8,128)(2,1)}, bf16...) custom-call(s32[2]{0:T(128)} %pad_add_fusion.where_ref, bf16[1024,1024]{1,0:T(8,128)(2,1)} %get-tuple-element.806.left_ref, ...), custom_call_target="tpu_custom_call" | custom-call | flops 5368709120 | bytes 7340032 | tf_op jit(solution)/shard_map/row_grads/pallas_call | solution.py:1147
  266.3 3.4 collective-permute-done.46
  275.5 9.5 %norm_grad.2 = (f32[512,1024]{1,0:T(8,128)}, f32[512,1024]{1,0:T(8,128)}) custom-call(bf16[1024,2048]{1,0:T(8,128)(2,1)} %get-tuple-element.762.right_ref.left_ref, bf16[256,2048]{1,0:T(8,128)(2,1)} %copy-done.12, bf16[256,2048]{1,0:T(8,128)(2,1)} %copy-done.34, bf16[256,2048]{1,0:T(8,128)(2,1)} %collective-permute-done.25.refs_2_, ...), custom_call_target="tpu_custom_call" | custom-call | flops 4294967296 | bytes 12582912 | tf_op jit(solution)/shard_map/norm_grad/pallas_call | solution.py:1278
  285.0 11.9 %unit_out.1 = (f32[512,1024]{1,0:T(8,128)}, f32[512,1024]{1,0:T(8,128)}) custom-call(s32[2]{0:T(128)} %pad_add_fusion.where_ref, bf16[1024,2048]{1,0:T(8,128)(2,1)} %get-tuple-element.751.act_ref, bf16[512,1024]{1,0:T(8,128)(2,1)} %get-tuple-element.752.heads_ref, bf16[1024,128]{1,0:T(8,128)(2,1)} %get-tuple-element.753.refs_0_, ...), custom_call_target="tpu_custom_call" | custom-call | flops 6442450944 | bytes 12582912 | tf_op jit(solution)/shard_map/unit_out/pallas_call | solution.py:1092
  301.1 4.3 %collective-permute-start.53 = (f32[512,1024]{1,0:T(8,128)}, f32[512,1024]{1,0:T(8,128)S(1)}, u32[]{:S(2)}, u32[]{:S(2)}) collective-permute-start(f32[512,1024]{1,0:T(8,128)} %get-tuple-element.790), channel_id=1, source_target_pairs={{0,1},{1,0},{2,3},{3,2},{4,5},{5,4},{6,7},{7,6},{8,9},{9,8},{10,11... | collective-permute-start | bytes 6291464 | tf_op jit(solution)/shard_map/ppermute | solution.py:311
  306.7 3.2 collective-permute-start.52
  309.9 6.5 %unturn.1 = (bf16[1024,1536]{1,0:T(8,128)(2,1)}, f32[1,1536]{1,0:T(1,128)}) custom-call(f32[1024,128]{1,0:T(8,128)} %get-tuple-element.791.cos_ref, f32[1024,128]{1,0:T(8,128)} %get-tuple-element.792.forth_ref, f32[1024,128]{1,0:T(8,128)} %get-tuple-element.793.back_ref, bf16[1024,128]{1,0:T(8,128)(2,1)} %get-tuple-element.794.refs_0_, ...), custom_call_target="tpu_custom_call" | custom-call | flops 15728640 | bytes 12582912 | tf_op jit(solution)/shard_map/unturn/pallas_call | solution.py:956
  316.4 7.1 %row_grads.3 = (bf16[128,1536]{1,0:T(8,128)(2,1)}, bf16[128,1536]{1,0:T(8,128)(2,1)}, bf16[128,1536]{1,0:T(8,128)(2,1)}, bf16[128,1536]{1,0:T(8,128)(2,1)}, bf16...) custom-call(s32[2]{0:T(128)} %pad_add_fusion.where_ref, bf16[1024,1024]{1,0:T(8,128)(2,1)} %get-tuple-element.806.left_ref, ...), custom_call_target="tpu_custom_call" | custom-call | flops 3221225472 | bytes 5242880 | tf_op jit(solution)/shard_map/row_grads/pallas_call | solution.py:1147
  325.3 2.4 add_convert_fusion.2
  329.3 9.9 %norm_grad.3 = (f32[512,1024]{1,0:T(8,128)}, f32[512,1024]{1,0:T(8,128)}) custom-call(bf16[1024,1536]{1,0:T(8,128)(2,1)} %get-tuple-element.826.right_ref.left_ref, bf16[256,896]{1,0:T(8,128)(2,1)} %copy-done.8, bf16[256,896]{1,0:T(8,128)(2,1)} %copy-done.15, bf16[256,896]{1,0:T(8,128)(2,1)} %collective-permute-done.11.refs_2_, ...), custom_call_target="tpu_custom_call" | custom-call | flops 3221225472 | bytes 12582912 | tf_op jit(solution)/shard_map/norm_grad/pallas_call | solution.py:1278
  339.2 4.0 collective-permute-done.56
  350.8 2.6 collective-permute-start.60
  355.9 6.0 %norm_back.1 = (bf16[512,1024]{1,0:T(8,128)(2,1)}, f32[8,1024]{1,0:T(8,128)}) custom-call(s32[2]{0:T(128)} %pad_add_fusion.where_ref, f32[512,1024]{1,0:T(8,128)} %get-tuple-element.859.part_ref, f32[512,1024]{1,0:T(8,128)} %copy-done.7, f32[1024,1024]{1,0:T(8,128)} %get-tuple-element.860.xhat_ref, f32[1024,1]{1,0:T(8,128)} %get-tuple-element.861.inv_ref, ...), custom_call_target="tpu_custom_call" | custom-call | flops 2147483648 | bytes 8388608 | tf_op jit(solution)/shard_map/norm_back/pallas_call | solution.py:1317
  364.1 4.7 %collective-permute-done.60 = bf16[64,2560]{1,0:T(8,128)(2,1)} collective-permute-done((bf16[64,2560]{1,0:T(8,128)(2,1)}, bf16[64,2560]{1,0:T(8,128)(2,1)}, u32[]{:S(2)}, u32[]{:S(2)}) %collective-permute-start.60) | collective-permute-done | bytes 327712 | tf_op jit(solution)/shard_map/ppermute | solution.py:311
  377.1 3.5 add_convert_fusion
  380.6 2.8 collective-permute-done.61
  391.0 5.1 %collective-permute-done.66 = f32[2,640]{1,0:T(2,128)S(1)} collective-permute-done((f32[2,640]{1,0:T(2,128)S(1)}, f32[2,640]{1,0:T(2,128)S(1)}, u32[]{:S(2)}, u32[]{:S(2)}) %collective-permute-start.66) | collective-permute-done | bytes 5152 | tf_op jit(solution)/shard_map/ppermute | solution.py:311
  (309 shorter events, 128.5 us)
Async XLA Ops:
  41.4 15.2 %collective-permute-start.11 = (bf16[256,896]{1,0:T(8,128)(2,1)S(1)}, bf16[256,896]{1,0:T(8,128)(2,1)}, u32[]{:S(2)}, u32[]{:S(2)}) collective-permute-start(bf16[256,896]{1,0:T(8,128)(2,1)S(1)} %pad_maximum_fusion.4.refs_0_), channel_id=1, source_target_pairs={{0,4},{1,5},{2,6},{3,7},{4,0},{5,1},{6,2},{7,3},{8,12},{9,13},{10,... | collective-permute-start | bytes 1376264 | tf_op jit(solution)/shard_map/ppermute | solution.py:311
  41.6 14.9 %collective-permute-start.12 = (bf16[256,896]{1,0:T(8,128)(2,1)S(1)}, bf16[256,896]{1,0:T(8,128)(2,1)}, u32[]{:S(2)}, u32[]{:S(2)}) collective-permute-start(bf16[256,896]{1,0:T(8,128)(2,1)S(1)} %constant_dynamic-update-slice_fusion.refs_1_), channel_id=1, source_target_pairs={{0,2},{1,3},{2,0},{3,1},{4,6},{5,7},{6,4},{7,5},{8,10},{9,11},{10,... | collective-permute-start | bytes 1376264 | tf_op jit(solution)/shard_map/ppermute | solution.py:311
  42.5 14.0 %collective-permute-start.13 = (bf16[64,2048]{1,0:T(8,128)(2,1)}, bf16[64,2048]{1,0:T(8,128)(2,1)S(1)}, u32[]{:S(2)}, u32[]{:S(2)}) collective-permute-start(bf16[64,2048]{1,0:T(8,128)(2,1)} %pad_maximum_fusion.6), channel_id=1, source_target_pairs={{0,16},{8,24},{16,0},{24,8},{1,17},{9,25},{17,1},{25,9},{2,18},{10... | collective-permute-start | bytes 786440 | tf_op jit(solution)/shard_map/ppermute | solution.py:311
  57.4 17.3 %collective-permute-start.16 = (bf16[128,2048]{1,0:T(8,128)(2,1)}, bf16[128,2048]{1,0:T(8,128)(2,1)}, u32[]{:S(2)}, u32[]{:S(2)}) collective-permute-start(bf16[128,2048]{1,0:T(8,128)(2,1)} %pad_maximum_fusion.2), channel_id=1, source_target_pairs={{0,8},{8,0},{16,24},{24,16},{1,9},{9,1},{17,25},{25,17},{2,10},{10... | collective-permute-start | bytes 1572872 | tf_op jit(solution)/shard_map/ppermute | solution.py:311
  57.4 13.6 %collective-permute-start.14 = (bf16[128,1280]{1,0:T(8,128)(2,1)S(1)}, bf16[128,1280]{1,0:T(8,128)(2,1)S(1)}, u32[]{:S(2)}, u32[]{:S(2)}) collective-permute-start(bf16[128,1280]{1,0:T(8,128)(2,1)S(1)} %pad_maximum_fusion.5), channel_id=1, source_target_pairs={{0,2},{1,3},{2,0},{3,1},{4,6},{5,7},{6,4},{7,5},{8,10},{9,11},{10,... | collective-permute-start | bytes 983048 | tf_op jit(solution)/shard_map/ppermute | solution.py:311
  58.6 12.4 %collective-permute-start.15 = (bf16[128,1280]{1,0:T(8,128)(2,1)}, bf16[128,1280]{1,0:T(8,128)(2,1)S(1)}, u32[]{:S(2)}, u32[]{:S(2)}) collective-permute-start(bf16[128,1280]{1,0:T(8,128)(2,1)} %collective-permute-done.10), channel_id=1, source_target_pairs={{0,4},{1,5},{2,6},{3,7},{4,0},{5,1},{6,2},{7,3},{8,12},{9,13},{10,... | collective-permute-start | bytes 983048 | tf_op jit(solution)/shard_map/ppermute | solution.py:311
  74.9 13.4 %collective-permute-start.18 = (bf16[256,1280]{1,0:T(8,128)(2,1)S(1)}, bf16[256,1280]{1,0:T(8,128)(2,1)S(1)}, u32[]{:S(2)}, u32[]{:S(2)}) collective-permute-start(bf16[256,1280]{1,0:T(8,128)(2,1)S(1)} %pad_maximum_fusion.1.refs_0_.refs_4_), channel_id=1, source_target_pairs={{0,4},{1,5},{2,6},{3,7},{4,0},{5,1},{6,2},{7,3},{8,12},{9,13},{10,... | collective-permute-start | bytes 1966088 | tf_op jit(solution)/shard_map/ppermute | solution.py:311
  76.4 14.7 %collective-permute-start.19 = (bf16[256,1280]{1,0:T(8,128)(2,1)S(1)}, bf16[256,1280]{1,0:T(8,128)(2,1)S(1)}, u32[]{:S(2)}, u32[]{:S(2)}) collective-permute-start(bf16[256,1280]{1,0:T(8,128)(2,1)S(1)} %constant_dynamic-update-slice_fusion.2.refs_1_.refs_5_), channel_id=1, source_target_pairs={{0,2},{1,3},{2,0},{3,1},{4,6},{5,7},{6,4},{7,5},{8,10},{9,11},{10,... | collective-permute-start | bytes 1966088 | tf_op jit(solution)/shard_map/ppermute | solution.py:311
  80.7 25.3 %collective-permute-start.24 = (bf16[1024,256]{1,0:T(8,128)(2,1)}, bf16[1024,256]{1,0:T(8,128)(2,1)}, u32[]{:S(2)}, u32[]{:S(2)}) collective-permute-start(bf16[1024,256]{1,0:T(8,128)(2,1)} %get-tuple-element.649.refs_0_), channel_id=1, source_target_pairs={{0,8},{8,16},{16,24},{1,9},{9,17},{17,25},{2,10},{10,18},{18,26},{... | collective-permute-start | bytes 1572872 | tf_op jit(solution)/shard_map/ppermute | solution.py:316
  91.1 14.9 %collective-permute-start.21 = (bf16[128,2048]{1,0:T(8,128)(2,1)}, bf16[128,2048]{1,0:T(8,128)(2,1)}, u32[]{:S(2)}, u32[]{:S(2)}) collective-permute-start(bf16[128,2048]{1,0:T(8,128)(2,1)} %pad_maximum_fusion.2), channel_id=1, source_target_pairs={{0,2},{1,3},{2,0},{3,1},{4,6},{5,7},{6,4},{7,5},{8,10},{9,11},{10,... | collective-permute-start | bytes 1572872 | tf_op jit(solution)/shard_map/ppermute | solution.py:311
  92.8 13.2 %collective-permute-start.22 = (bf16[128,2048]{1,0:T(8,128)(2,1)}, bf16[128,2048]{1,0:T(8,128)(2,1)}, u32[]{:S(2)}, u32[]{:S(2)}) collective-permute-start(bf16[128,2048]{1,0:T(8,128)(2,1)} %collective-permute-done.16), channel_id=1, source_target_pairs={{0,4},{1,5},{2,6},{3,7},{4,0},{5,1},{6,2},{7,3},{8,12},{9,13},{10,... | collective-permute-start | bytes 1572872 | tf_op jit(solution)/shard_map/ppermute | solution.py:311
  93.1 16.4 %collective-permute-start.23 = (bf16[1024,256]{1,0:T(8,128)(2,1)}, bf16[1024,256]{1,0:T(8,128)(2,1)}, u32[]{:S(2)}, u32[]{:S(2)}) collective-permute-start(bf16[1024,256]{1,0:T(8,128)(2,1)} %collective-permute-done.20.refs_1_), channel_id=1, source_target_pairs={{0,8},{8,16},{16,24},{1,9},{9,17},{17,25},{2,10},{10,18},{18,26},{... | collective-permute-start | bytes 1572872 | tf_op jit(solution)/shard_map/ppermute | solution.py:316
  112.1 31.1 %collective-permute-start.25 = (bf16[256,2048]{1,0:T(8,128)(2,1)S(1)}, bf16[256,2048]{1,0:T(8,128)(2,1)}, u32[]{:S(2)}, u32[]{:S(2)}) collective-permute-start(bf16[256,2048]{1,0:T(8,128)(2,1)S(1)} %pad_maximum_fusion.refs_0_), channel_id=1, source_target_pairs={{0,4},{1,5},{2,6},{3,7},{4,0},{5,1},{6,2},{7,3},{8,12},{9,13},{10,... | collective-permute-start | bytes 3145736 | tf_op jit(solution)/shard_map/ppermute | solution.py:311
  112.2 31.0 %collective-permute-start.26 = (bf16[256,2048]{1,0:T(8,128)(2,1)S(1)}, bf16[256,2048]{1,0:T(8,128)(2,1)}, u32[]{:S(2)}, u32[]{:S(2)}) collective-permute-start(bf16[256,2048]{1,0:T(8,128)(2,1)S(1)} %constant_dynamic-update-slice_fusion.4.refs_1_), channel_id=1, source_target_pairs={{0,2},{1,3},{2,0},{3,1},{4,6},{5,7},{6,4},{7,5},{8,10},{9,11},{10,... | collective-permute-start | bytes 3145736 | tf_op jit(solution)/shard_map/ppermute | solution.py:311
  112.4 11.8 %collective-permute-start.29 = (bf16[256,1024]{1,0:T(8,128)(2,1)S(1)}, bf16[256,1024]{1,0:T(8,128)(2,1)}, u32[]{:S(2)}, u32[]{:S(2)}) collective-permute-start(bf16[256,1024]{1,0:T(8,128)(2,1)S(1)} %copy-done.48), channel_id=1, source_target_pairs={{0,1},{1,0},{2,3},{3,2},{4,5},{5,4},{6,7},{7,6},{8,9},{9,8},{10,11... | collective-permute-start | bytes 1572872 | tf_op jit(solution)/shard_map/ppermute | solution.py:311
  120.0 18.3 %collective-permute-start.27 = (bf16[256,1024]{1,0:T(8,128)(2,1)S(1)}, bf16[256,1024]{1,0:T(8,128)(2,1)S(1)}, u32[]{:S(2)}, u32[]{:S(2)}) collective-permute-start(bf16[256,1024]{1,0:T(8,128)(2,1)S(1)} %pad_maximum_fusion.3), channel_id=1, source_target_pairs={{0,8},{8,0},{16,24},{24,16},{1,9},{9,1},{17,25},{25,17},{2,10},{10... | collective-permute-start | bytes 1572872 | tf_op jit(solution)/shard_map/ppermute | solution.py:311
  120.5 22.7 %collective-permute-start.28 = (bf16[1024,256]{1,0:T(8,128)(2,1)}, bf16[1024,256]{1,0:T(8,128)(2,1)}, u32[]{:S(2)}, u32[]{:S(2)}) collective-permute-start(bf16[1024,256]{1,0:T(8,128)(2,1)} %collective-permute-done.24.refs_1_), channel_id=1, source_target_pairs={{0,8},{8,16},{16,24},{1,9},{9,17},{17,25},{2,10},{10,18},{18,26},{... | collective-permute-start | bytes 1572872 | tf_op jit(solution)/shard_map/ppermute | solution.py:316
  143.2 26.1 %collective-permute-start.32 = (bf16[1024,512]{1,0:T(8,128)(2,1)}, bf16[1024,512]{1,0:T(8,128)(2,1)}, u32[]{:S(2)}, u32[]{:S(2)}) collective-permute-start(bf16[1024,512]{1,0:T(8,128)(2,1)} %get-tuple-element.684.refs_0_), channel_id=1, source_target_pairs={{0,8},{8,16},{16,24},{1,9},{9,17},{17,25},{2,10},{10,18},{18,26},{... | collective-permute-start | bytes 3145736 | tf_op jit(solution)/shard_map/ppermute | solution.py:316
  149.2 18.9 %collective-permute-start.30 = (bf16[256,1024]{1,0:T(8,128)(2,1)S(1)}, bf16[256,1024]{1,0:T(8,128)(2,1)S(1)}, u32[]{:S(2)}, u32[]{:S(2)}) collective-permute-start(bf16[256,1024]{1,0:T(8,128)(2,1)S(1)} %pad_maximum_fusion.3), channel_id=1, source_target_pairs={{0,2},{1,3},{2,0},{3,1},{4,6},{5,7},{6,4},{7,5},{8,10},{9,11},{10,... | collective-permute-start | bytes 1572872 | tf_op jit(solution)/shard_map/ppermute | solution.py:311
  150.4 17.7 %collective-permute-start.31 = (bf16[256,1024]{1,0:T(8,128)(2,1)S(1)}, bf16[256,1024]{1,0:T(8,128)(2,1)S(1)}, u32[]{:S(2)}, u32[]{:S(2)}) collective-permute-start(bf16[256,1024]{1,0:T(8,128)(2,1)S(1)} %collective-permute-done.27), channel_id=1, source_target_pairs={{0,4},{1,5},{2,6},{3,7},{4,0},{5,1},{6,2},{7,3},{8,12},{9,13},{10,... | collective-permute-start | bytes 1572872 | tf_op jit(solution)/shard_map/ppermute | solution.py:311
  151.8 16.4 %collective-permute-start.33 = (bf16[1024,256]{1,0:T(8,128)(2,1)}, bf16[1024,256]{1,0:T(8,128)(2,1)S(1)}, u32[]{:S(2)}, u32[]{:S(2)}) collective-permute-start(bf16[1024,256]{1,0:T(8,128)(2,1)} %get-tuple-element.622), channel_id=1, source_target_pairs={{8,0},{16,8},{24,16},{9,1},{17,9},{25,17},{10,2},{18,10},{26,18},{... | collective-permute-start | bytes 1572872 | tf_op jit(solution)/shard_map/ppermute | solution.py:316
  171.3 29.7 %collective-permute-start.34 = (bf16[512,1024]{1,0:T(8,128)(2,1)}, bf16[512,1024]{1,0:T(8,128)(2,1)S(1)}, u32[]{:S(2)}, u32[]{:S(2)}) collective-permute-start(bf16[512,1024]{1,0:T(8,128)(2,1)} %get-tuple-element.756.refs_0_.refs_3_), channel_id=1, source_target_pairs={{0,4},{1,5},{2,6},{3,7},{4,0},{5,1},{6,2},{7,3},{8,12},{9,13},{10,... | collective-permute-start | bytes 3145736 | tf_op jit(solution)/shard_map/ppermute | solution.py:311
  172.6 28.5 %collective-permute-start.35 = (bf16[512,1024]{1,0:T(8,128)(2,1)}, bf16[512,1024]{1,0:T(8,128)(2,1)S(1)}, u32[]{:S(2)}, u32[]{:S(2)}) collective-permute-start(bf16[512,1024]{1,0:T(8,128)(2,1)} %get-tuple-element.757.refs_1_.refs_4_), channel_id=1, source_target_pairs={{0,2},{1,3},{2,0},{3,1},{4,6},{5,7},{6,4},{7,5},{8,10},{9,11},{10,... | collective-permute-start | bytes 3145736 | tf_op jit(solution)/shard_map/ppermute | solution.py:311
  174.0 27.1 %collective-permute-start.36 = (bf16[1024,512]{1,0:T(8,128)(2,1)}, bf16[1024,512]{1,0:T(8,128)(2,1)}, u32[]{:S(2)}, u32[]{:S(2)}) collective-permute-start(bf16[1024,512]{1,0:T(8,128)(2,1)} %collective-permute-done.32.refs_1_), channel_id=1, source_target_pairs={{0,8},{8,16},{16,24},{1,9},{9,17},{17,25},{2,10},{10,18},{18,26},{... | collective-permute-start | bytes 3145736 | tf_op jit(solution)/shard_map/ppermute | solution.py:316
  188.1 13.0 %collective-permute-start.37 = (bf16[1024,256]{1,0:T(8,128)(2,1)}, bf16[1024,256]{1,0:T(8,128)(2,1)S(1)}, u32[]{:S(2)}, u32[]{:S(2)}) collective-permute-start(bf16[1024,256]{1,0:T(8,128)(2,1)} %get-tuple-element.656), channel_id=1, source_target_pairs={{8,0},{16,8},{24,16},{9,1},{17,9},{25,17},{10,2},{18,10},{26,18},{... | collective-permute-start | bytes 1572872 | tf_op jit(solution)/shard_map/ppermute | solution.py:316
  203.0 24.3 %collective-permute-start.38 = (bf16[512,1024]{1,0:T(8,128)(2,1)}, bf16[512,1024]{1,0:T(8,128)(2,1)S(1)}, u32[]{:S(2)}, u32[]{:S(2)}) collective-permute-start(bf16[512,1024]{1,0:T(8,128)(2,1)} %get-tuple-element.677), channel_id=1, source_target_pairs={{0,4},{1,5},{2,6},{3,7},{4,0},{5,1},{6,2},{7,3},{8,12},{9,13},{10,... | collective-permute-start | bytes 3145736 | tf_op jit(solution)/shard_map/ppermute | solution.py:311
  203.0 24.2 %collective-permute-start.39 = (bf16[512,1024]{1,0:T(8,128)(2,1)}, bf16[512,1024]{1,0:T(8,128)(2,1)S(1)}, u32[]{:S(2)}, u32[]{:S(2)}) collective-permute-start(bf16[512,1024]{1,0:T(8,128)(2,1)} %get-tuple-element.678), channel_id=1, source_target_pairs={{0,2},{1,3},{2,0},{3,1},{4,6},{5,7},{6,4},{7,5},{8,10},{9,11},{10,... | collective-permute-start | bytes 3145736 | tf_op jit(solution)/shard_map/ppermute | solution.py:311
  203.3 23.9 %collective-permute-start.41 = (bf16[1024,256]{1,0:T(8,128)(2,1)}, bf16[1024,256]{1,0:T(8,128)(2,1)S(1)}, u32[]{:S(2)}, u32[]{:S(2)}) collective-permute-start(bf16[1024,256]{1,0:T(8,128)(2,1)} %add_convert_fusion.9), channel_id=1, source_target_pairs={{8,0},{16,8},{24,16},{9,1},{17,9},{25,17},{10,2},{18,10},{26,18},{... | collective-permute-start | bytes 1572872 | tf_op jit(solution)/shard_map/ppermute | solution.py:316
  204.6 22.6 %collective-permute-start.40 = (bf16[1024,256]{1,0:T(8,128)(2,1)}, bf16[1024,256]{1,0:T(8,128)(2,1)S(1)}, u32[]{:S(2)}, u32[]{:S(2)}) collective-permute-start(bf16[1024,256]{1,0:T(8,128)(2,1)} %add_convert_fusion.8), channel_id=1, source_target_pairs={{8,0},{16,8},{24,16},{9,1},{17,9},{25,17},{10,2},{18,10},{26,18},{... | collective-permute-start | bytes 1572872 | tf_op jit(solution)/shard_map/ppermute | solution.py:316
  231.7 20.2 %collective-permute-start.43 = (bf16[256,1024]{1,0:T(8,128)(2,1)}, bf16[256,1024]{1,0:T(8,128)(2,1)}, u32[]{:S(2)}, u32[]{:S(2)}) collective-permute-start(bf16[256,1024]{1,0:T(8,128)(2,1)} %add_convert_fusion.6), channel_id=1, source_target_pairs={{0,4},{1,5},{2,6},{3,7},{4,0},{5,1},{6,2},{7,3},{8,12},{9,13},{10,... | collective-permute-start | bytes 1572872 | tf_op jit(solution)/shard_map/ppermute | solution.py:311
  233.0 33.3 %collective-permute-start.45 = (bf16[1024,512]{1,0:T(8,128)(2,1)}, bf16[1024,512]{1,0:T(8,128)(2,1)S(1)}, u32[]{:S(2)}, u32[]{:S(2)}) collective-permute-start(bf16[1024,512]{1,0:T(8,128)(2,1)} %get-tuple-element.691), channel_id=1, source_target_pairs={{8,0},{16,8},{24,16},{9,1},{17,9},{25,17},{10,2},{18,10},{26,18},{... | collective-permute-start | bytes 3145736 | tf_op jit(solution)/shard_map/ppermute | solution.py:316
  234.3 32.0 %collective-permute-start.42 = (bf16[256,1024]{1,0:T(8,128)(2,1)}, bf16[256,1024]{1,0:T(8,128)(2,1)}, u32[]{:S(2)}, u32[]{:S(2)}) collective-permute-start(bf16[256,1024]{1,0:T(8,128)(2,1)} %add_convert_fusion.7), channel_id=1, source_target_pairs={{0,2},{1,3},{2,0},{3,1},{4,6},{5,7},{6,4},{7,5},{8,10},{9,11},{10,... | collective-permute-start | bytes 1572872 | tf_op jit(solution)/shard_map/ppermute | solution.py:311
  235.7 21.4 %collective-permute-start.44 = (bf16[256,1024]{1,0:T(8,128)(2,1)}, bf16[256,1024]{1,0:T(8,128)(2,1)}, u32[]{:S(2)}, u32[]{:S(2)}) collective-permute-start(bf16[256,1024]{1,0:T(8,128)(2,1)} %get-tuple-element.712), channel_id=1, source_target_pairs={{0,1},{1,0},{2,3},{3,2},{4,5},{5,4},{6,7},{7,6},{8,9},{9,8},{10,11... | collective-permute-start | bytes 1572872 | tf_op jit(solution)/shard_map/ppermute | solution.py:311
  253.4 16.2 %collective-permute-start.46 = (bf16[256,1024]{1,0:T(8,128)(2,1)S(1)}, bf16[256,1024]{1,0:T(8,128)(2,1)S(1)}, u32[]{:S(2)}, u32[]{:S(2)}) collective-permute-start(bf16[256,1024]{1,0:T(8,128)(2,1)S(1)} %add_convert_fusion.5), channel_id=1, source_target_pairs={{0,8},{8,0},{16,24},{24,16},{1,9},{9,1},{17,25},{25,17},{2,10},{10... | collective-permute-start | bytes 1572872 | tf_op jit(solution)/shard_map/ppermute | solution.py:311
  271.7 27.1 %collective-permute-start.47 = (bf16[256,2560]{1,0:T(8,128)(2,1)}, bf16[256,2560]{1,0:T(8,128)(2,1)S(1)}, u32[]{:S(2)}, u32[]{:S(2)}) collective-permute-start(bf16[256,2560]{1,0:T(8,128)(2,1)} %get-tuple-element.747), channel_id=1, source_target_pairs={{0,4},{1,5},{2,6},{3,7},{4,0},{5,1},{6,2},{7,3},{8,12},{9,13},{10,... | collective-permute-start | bytes 3932168 | tf_op jit(solution)/shard_map/ppermute | solution.py:311
  271.8 27.0 %collective-permute-start.48 = (bf16[256,2560]{1,0:T(8,128)(2,1)}, bf16[256,2560]{1,0:T(8,128)(2,1)S(1)}, u32[]{:S(2)}, u32[]{:S(2)}) collective-permute-start(bf16[256,2560]{1,0:T(8,128)(2,1)} %get-tuple-element.748), channel_id=1, source_target_pairs={{0,2},{1,3},{2,0},{3,1},{4,6},{5,7},{6,4},{7,5},{8,10},{9,11},{10,... | collective-permute-start | bytes 3932168 | tf_op jit(solution)/shard_map/ppermute | solution.py:311
  272.0 24.9 %collective-permute-start.49 = (bf16[1024,512]{1,0:T(8,128)(2,1)}, bf16[1024,512]{1,0:T(8,128)(2,1)}, u32[]{:S(2)}, u32[]{:S(2)}) collective-permute-start(bf16[1024,512]{1,0:T(8,128)(2,1)} %add_convert_fusion.1), channel_id=1, source_target_pairs={{8,0},{16,8},{24,16},{9,1},{17,9},{25,17},{10,2},{18,10},{26,18},{... | collective-permute-start | bytes 3145736 | tf_op jit(solution)/shard_map/ppermute | solution.py:316
  301.1 22.4 %collective-permute-start.53 = (f32[512,1024]{1,0:T(8,128)}, f32[512,1024]{1,0:T(8,128)S(1)}, u32[]{:S(2)}, u32[]{:S(2)}) collective-permute-start(f32[512,1024]{1,0:T(8,128)} %get-tuple-element.790), channel_id=1, source_target_pairs={{0,1},{1,0},{2,3},{3,2},{4,5},{5,4},{6,7},{7,6},{8,9},{9,8},{10,11... | collective-permute-start | bytes 6291464 | tf_op jit(solution)/shard_map/ppermute | solution.py:311
  305.4 18.1 %collective-permute-start.50 = (bf16[128,2560]{1,0:T(8,128)(2,1)}, bf16[128,2560]{1,0:T(8,128)(2,1)}, u32[]{:S(2)}, u32[]{:S(2)}) collective-permute-start(bf16[128,2560]{1,0:T(8,128)(2,1)} %add_convert_fusion.4), channel_id=1, source_target_pairs={{0,2},{1,3},{2,0},{3,1},{4,6},{5,7},{6,4},{7,5},{8,10},{9,11},{10,... | collective-permute-start | bytes 1966088 | tf_op jit(solution)/shard_map/ppermute | solution.py:311
  305.5 18.0 %collective-permute-start.51 = (bf16[128,2560]{1,0:T(8,128)(2,1)}, bf16[128,2560]{1,0:T(8,128)(2,1)}, u32[]{:S(2)}, u32[]{:S(2)}) collective-permute-start(bf16[128,2560]{1,0:T(8,128)(2,1)} %add_convert_fusion.3), channel_id=1, source_target_pairs={{0,4},{1,5},{2,6},{3,7},{4,0},{5,1},{6,2},{7,3},{8,12},{9,13},{10,... | collective-permute-start | bytes 1966088 | tf_op jit(solution)/shard_map/ppermute | solution.py:311
  306.7 16.8 %collective-permute-start.52 = (bf16[128,1024]{1,0:T(8,128)(2,1)}, bf16[128,1024]{1,0:T(8,128)(2,1)}, u32[]{:S(2)}, u32[]{:S(2)}) collective-permute-start(bf16[128,1024]{1,0:T(8,128)(2,1)} %add_convert_fusion.14), channel_id=1, source_target_pairs={{0,16},{8,24},{16,0},{24,8},{1,17},{9,25},{17,1},{25,9},{2,18},{10... | collective-permute-start | bytes 786440 | tf_op jit(solution)/shard_map/ppermute | solution.py:311
  323.5 19.6 %collective-permute-start.54 = (bf16[256,1536]{1,0:T(8,128)(2,1)}, bf16[256,1536]{1,0:T(8,128)(2,1)}, u32[]{:S(2)}, u32[]{:S(2)}) collective-permute-start(bf16[256,1536]{1,0:T(8,128)(2,1)} %get-tuple-element.822), channel_id=1, source_target_pairs={{0,4},{1,5},{2,6},{3,7},{4,0},{5,1},{6,2},{7,3},{8,12},{9,13},{10,... | collective-permute-start | bytes 2359304 | tf_op jit(solution)/shard_map/ppermute | solution.py:311
  323.9 19.3 %collective-permute-start.55 = (bf16[256,1536]{1,0:T(8,128)(2,1)}, bf16[256,1536]{1,0:T(8,128)(2,1)}, u32[]{:S(2)}, u32[]{:S(2)}) collective-permute-start(bf16[256,1536]{1,0:T(8,128)(2,1)} %get-tuple-element.823), channel_id=1, source_target_pairs={{0,2},{1,3},{2,0},{3,1},{4,6},{5,7},{6,4},{7,5},{8,10},{9,11},{10,... | collective-permute-start | bytes 2359304 | tf_op jit(solution)/shard_map/ppermute | solution.py:311
  327.6 15.5 %collective-permute-start.56 = (bf16[128,2560]{1,0:T(8,128)(2,1)}, bf16[128,2560]{1,0:T(8,128)(2,1)S(1)}, u32[]{:S(2)}, u32[]{:S(2)}) collective-permute-start(bf16[128,2560]{1,0:T(8,128)(2,1)} %add_convert_fusion.2), channel_id=1, source_target_pairs={{0,8},{8,0},{16,24},{24,16},{1,9},{9,1},{17,25},{25,17},{2,10},{10... | collective-permute-start | bytes 1966088 | tf_op jit(solution)/shard_map/ppermute | solution.py:311
  350.8 17.9 %collective-permute-start.60 = (bf16[64,2560]{1,0:T(8,128)(2,1)}, bf16[64,2560]{1,0:T(8,128)(2,1)}, u32[]{:S(2)}, u32[]{:S(2)}) collective-permute-start(bf16[64,2560]{1,0:T(8,128)(2,1)} %add_convert_fusion.13), channel_id=1, source_target_pairs={{0,16},{8,24},{16,0},{24,8},{1,17},{9,25},{17,1},{25,9},{2,18},{10... | collective-permute-start | bytes 983048 | tf_op jit(solution)/shard_map/ppermute | solution.py:311
  353.4 15.4 %collective-permute-start.57 = (bf16[128,1536]{1,0:T(8,128)(2,1)}, bf16[128,1536]{1,0:T(8,128)(2,1)}, u32[]{:S(2)}, u32[]{:S(2)}) collective-permute-start(bf16[128,1536]{1,0:T(8,128)(2,1)} %add_convert_fusion.12), channel_id=1, source_target_pairs={{0,2},{1,3},{2,0},{3,1},{4,6},{5,7},{6,4},{7,5},{8,10},{9,11},{10,... | collective-permute-start | bytes 1179656 | tf_op jit(solution)/shard_map/ppermute | solution.py:311
  353.8 15.0 %collective-permute-start.58 = (bf16[128,1536]{1,0:T(8,128)(2,1)S(1)}, bf16[128,1536]{1,0:T(8,128)(2,1)}, u32[]{:S(2)}, u32[]{:S(2)}) collective-permute-start(bf16[128,1536]{1,0:T(8,128)(2,1)S(1)} %add_convert_fusion.11), channel_id=1, source_target_pairs={{0,4},{1,5},{2,6},{3,7},{4,0},{5,1},{6,2},{7,3},{8,12},{9,13},{10,... | collective-permute-start | bytes 1179656 | tf_op jit(solution)/shard_map/ppermute | solution.py:311
  384.6 11.5 %collective-permute-start.65 = (bf16[64,1536]{1,0:T(8,128)(2,1)S(1)}, bf16[64,1536]{1,0:T(8,128)(2,1)S(1)}, u32[]{:S(2)}, u32[]{:S(2)}) collective-permute-start(bf16[64,1536]{1,0:T(8,128)(2,1)S(1)} %add_convert_fusion.15), channel_id=1, source_target_pairs={{0,16},{8,24},{16,0},{24,8},{1,17},{9,25},{17,1},{25,9},{2,18},{10... | collective-permute-start | bytes 589832 | tf_op jit(solution)/shard_map/ppermute | solution.py:311
  (73 other events, 727.8 us)
